TPU v7x, 32 devices: a whole 2x2x4 slice. The times are simulated.
32 devices in a mesh: dp: 8 (over z, y), tensor: 4 (over x, core).
Axes of the slice: x: 2, y: 2, z: 4, core: 2. Of those that a mesh axis runs over, the one named last changes fastest.
Arguments:
- tokens: bfloat16 [9456, 768], P('dp'), as said below
- gain_attn: bfloat16 [768], replicated, may hold values from 0.5 to 1.5
- w_query: bfloat16 [768, 768], P(None, 'tensor'), may hold values from -0.3125 to 0.3125
- w_key: bfloat16 [768, 768], P(None, 'tensor'), may hold values from -0.3125 to 0.3125
- w_value: bfloat16 [768, 768], P(None, 'tensor'), may hold values from -0.21875 to 0.21875
- w_output: bfloat16 [768, 768], P('tensor'), may hold values from -0.625 to 0.625
- gain_moe: bfloat16 [768], replicated, may hold values from 0.5 to 1.5
- w_router: bfloat16 [768, 8], replicated, may hold values from -0.21875 to 0.21875
- expert_in: bfloat16 [8, 768, 3072], P('dp', None, 'tensor'), may hold values from -0.21875 to 0.21875
- expert_out: bfloat16 [8, 3072, 768], P('dp', 'tensor'), may hold values from -0.21875 to 0.21875
- routes: int32 [9456, 2], P('dp'), may hold values from 0 to 7, as said below
- slot_ids: int32 [9456, 2], P('dp'), may hold values from 0 to 340, as said below
- capacity: int32 [8], replicated, may hold values from 255 to 340, as said below
- threshold: float32 [12], P('tensor'), may hold values from 5 to 16
- cotangent: bfloat16 [9456, 768], P('dp'), may hold values from -6 to 6
Outputs:
- block_out: bfloat16 [9456, 768], P('dp')
- grad_tokens: bfloat16 [9456, 768], P('dp')
- grad_gain_attn: float32 [768], P('dp')
- grad_gain_moe: float32 [768], P('dp')
- grad_w_query: float32 [768, 768], P('dp', 'tensor')
- grad_w_key: float32 [768, 768], P('dp', 'tensor')
- grad_w_value: float32 [768, 768], P('dp', 'tensor')
- grad_w_output: float32 [768, 768], P('tensor', 'dp')
- grad_router: float32 [768, 8], P('dp')
- grad_expert_in: float32 [8, 768, 3072], P('dp', None, 'tensor')
- grad_expert_out: float32 [8, 3072, 768], P('dp', 'tensor')
- clipped_query: float32 [768, 768], P(None, 'tensor')
- clipped_key: float32 [768, 768], P(None, 'tensor')
- head_max: float32 [12], P('tensor')
Inputs may be any that keep to these rules, and one draw needn't show every extreme that they name: `routes`: a token's two experts differ; one expert takes the first choices of the first 341 tokens of every block of 1182 tokens. `slot_ids`: among the pairs of the same block of 1182 tokens and the same expert, first choices take slots 0, 1, ... in token order and second choices follow in token order; a pair whose position would be 340 or more gets slot 340, which happens in every block. `capacity`: one expert accepts 340 pairs, and all its slots are filled from every block. The tokens of an image may share a common part that grows from image to image.
All inputs are finite; a program needn't handle non-finite values.
Results may differ from a plain program's by a relative error of at most 0.015.
The roundings to bfloat16 on the way count: a program that leaves them out, or rounds other values in their place, can miss the bound.
Values may be sent and summed in bfloat16 or wider, within the bound.
A program may use at most 192 MiB of HBM per device.

v0:
```python
import math

import jax
import jax.numpy as jnp
from jax import lax
from jax.sharding import PartitionSpec as P

HD = 64
SEQ = 197
TOK_DEV = 1182


epsilon = 1e-06
contract = (((0,), (0,)), ((), ()))
contract_last = (((1,), (1,)), ((), ()))


def split_up(array, dim, peers):
    before, after = (array.shape[:dim], array.shape[dim + 1 :])
    return jnp.moveaxis(array.reshape(*before, peers, -1, *after), dim, 0)


def sent_and_summed(array, axis, dim):
    blocks = split_up(array, dim, lax.axis_size(axis))
    arrived = lax.all_to_all(blocks, axis, split_axis=0, concat_axis=0, tiled=True)
    return arrived.astype(jnp.float32).sum(axis=0)


def in_one_piece(arrays, axis, dim, along):
    ends, at = ([], 0)
    for a in arrays[:-1]:
        at += a.shape[along]
        ends.append(at)
    both = jnp.concatenate(arrays, axis=along)
    return tuple(jnp.split(sent_and_summed(both, axis, dim), ends, axis=along))


def in_one_piece_2(arrays, axis, dim, along):
    widths = [math.prod(a.shape[along:]) for a in arrays]
    both = jnp.concatenate(
        [a.reshape(*a.shape[:along], w) for a, w in zip(arrays, widths)], axis=along
    )
    whole = sent_and_summed(both, axis, dim)
    blocks = jnp.split(whole, [sum(widths[:k]) for k in range(1, len(widths))], axis=along)
    return tuple(
        (b.reshape(*whole.shape[:along], *a.shape[along:]) for a, b in zip(arrays, blocks))
    )


def norm_rows(rows, gain):
    centered = rows - jnp.mean(rows, axis=-1, keepdims=True)
    factor = lax.rsqrt(jnp.mean(centered * centered, axis=-1, keepdims=True) + epsilon)
    return centered * factor * gain


def exact_gelu(values_in):
    return jax.nn.gelu(values_in, approximate=False)


def tensor_total(partial_value):
    return lax.psum(partial_value, "tensor")


def send_rows(buffer):
    complete = lax.all_to_all(buffer, "dp", split_axis=0, concat_axis=1, tiled=True)
    return complete


def return_rows(partial_value):
    row_width = partial_value.shape[2]
    summed = lax.psum(partial_value, "tensor").astype(jnp.bfloat16)
    complete = lax.all_to_all(summed, "dp", split_axis=1, concat_axis=0, tiled=True)
    return complete.reshape(-1, row_width)


def body(
    tokens,
    gain_attn,
    w_query,
    w_key,
    w_value,
    w_output,
    gain_moe,
    w_router,
    expert_in,
    expert_out,
    routes,
    slot_ids,
    capacity,
    threshold,
    cotangent,
):
    dp_count = lax.axis_size("dp")
    row_count = tokens.shape[0]
    images = row_count // SEQ
    heads_here = w_query.shape[1] // HD
    experts = expert_in.shape[0] * dp_count
    blocks_here = row_count // TOK_DEV
    slot_count = 23 * TOK_DEV // (10 * experts) + 1
    block_slots = blocks_here * slot_count
    score_scale = HD ** (-0.5)

    def heads_view(rows):
        return rows.reshape(images, SEQ, heads_here, HD)

    def as_rows(heads):
        return heads.reshape(row_count, heads_here * HD)

    inputs = tokens.astype(jnp.float32)
    norm_one, norm_one_back = jax.vjp(norm_rows, inputs, gain_attn.astype(jnp.float32))
    normed_one = norm_one.astype(jnp.bfloat16)
    queries = jnp.dot(normed_one, w_query, preferred_element_type=jnp.float32).astype(jnp.bfloat16)
    key_rows = jnp.dot(normed_one, w_key, preferred_element_type=jnp.float32).astype(jnp.bfloat16)
    value_rows = jnp.dot(normed_one, w_value, preferred_element_type=jnp.float32).astype(
        jnp.bfloat16
    )
    query_heads = heads_view(queries)
    key_heads = heads_view(key_rows)
    value_heads = heads_view(value_rows)
    raw_scores = (
        jnp.einsum("ishd,ithd->ihst", query_heads, key_heads, preferred_element_type=jnp.float32)
        * score_scale
    )
    peak_local = jnp.max(raw_scores, axis=(0, 2, 3))
    top_row = jnp.max(raw_scores, axis=-1, keepdims=True)
    log_total = top_row + jnp.log(jnp.sum(jnp.exp(raw_scores - top_row), axis=-1, keepdims=True))
    attn_probs = jnp.exp(raw_scores - log_total)
    mixed_heads = jnp.einsum(
        "ihst,ithd->ishd",
        attn_probs.astype(jnp.bfloat16),
        value_heads,
        preferred_element_type=jnp.float32,
    )
    mixed_rows = as_rows(mixed_heads).astype(jnp.bfloat16)
    attended = tensor_total(jnp.dot(mixed_rows, w_output, preferred_element_type=jnp.float32))
    residual = inputs + attended
    head_max = lax.pmax(peak_local, "dp")
    column_factor = jnp.repeat(jnp.sqrt(jnp.minimum(1.0, threshold / head_max)), HD)[None, :]
    clipped_query = w_query.astype(jnp.float32) * column_factor
    clipped_key = w_key.astype(jnp.float32) * column_factor
    norm_two, norm_two_back = jax.vjp(norm_rows, residual, gain_moe.astype(jnp.float32))
    normed_two = norm_two.astype(jnp.bfloat16)
    logits = jnp.dot(normed_two, w_router, preferred_element_type=jnp.float32)
    expert_ids = jnp.arange(experts, dtype=jnp.int32)
    route_match = routes[:, :, None] == expert_ids[None, None, :]
    pick_hot = route_match.astype(jnp.float32)
    chosen = jnp.sum(pick_hot * logits[:, None, :], axis=-1)
    gate_vals = jax.nn.softmax(chosen, axis=-1)
    limits = jnp.sum(jnp.where(route_match, capacity[None, None, :], 0), axis=-1)
    kept_mask = slot_ids < limits
    local_block = (jnp.arange(row_count, dtype=jnp.int32) // TOK_DEV)[:, None]
    target = routes * block_slots + local_block * slot_count + slot_ids
    columns = jnp.arange(experts * block_slots, dtype=jnp.int32)[None, :]
    hot_first = ((target[:, 0:1] == columns) & kept_mask[:, 0:1]).astype(jnp.bfloat16)
    hot_second = ((target[:, 1:2] == columns) & kept_mask[:, 1:2]).astype(jnp.bfloat16)
    dispatch = hot_first + hot_second
    buffer = lax.dot_general(
        dispatch, normed_two, contract, preferred_element_type=jnp.float32
    ).astype(jnp.bfloat16)
    arrived = send_rows(buffer.reshape(experts, block_slots, -1))
    pre_act = jnp.einsum("erd,edf->erf", arrived, expert_in, preferred_element_type=jnp.float32)
    activated, gelu_back = jax.vjp(exact_gelu, pre_act)
    hidden = activated.astype(jnp.bfloat16)
    out_part = jnp.einsum("erf,efd->erd", hidden, expert_out, preferred_element_type=jnp.float32)
    returned = return_rows(out_part)
    from_first = jnp.dot(hot_first, returned, preferred_element_type=jnp.float32)
    from_second = jnp.dot(hot_second, returned, preferred_element_type=jnp.float32)
    mixture = gate_vals[:, 0:1] * from_first + gate_vals[:, 1:2] * from_second
    block_out = (residual + mixture).astype(jnp.bfloat16)
    upstream = cotangent.astype(jnp.float32)
    gate_grad = jnp.stack(
        [jnp.sum(upstream * from_first, axis=-1), jnp.sum(upstream * from_second, axis=-1)], axis=1
    )
    chosen_grad = gate_vals * (gate_grad - jnp.sum(gate_vals * gate_grad, axis=-1, keepdims=True))
    logit_grad = jnp.sum(chosen_grad[:, :, None] * pick_hot, axis=1).astype(jnp.bfloat16)
    grad_router = lax.dot_general(
        normed_two, logit_grad, contract, preferred_element_type=jnp.float32
    )
    router_back = lax.dot_general(
        logit_grad, w_router, contract_last, preferred_element_type=jnp.float32
    )
    sent_first = (gate_vals[:, 0:1] * upstream).astype(jnp.bfloat16)
    sent_second = (gate_vals[:, 1:2] * upstream).astype(jnp.bfloat16)
    answer_grad = lax.dot_general(
        hot_first, sent_first, contract, preferred_element_type=jnp.float32
    )
    answer_grad = answer_grad + lax.dot_general(
        hot_second, sent_second, contract, preferred_element_type=jnp.float32
    )
    grad_arrived = send_rows(answer_grad.astype(jnp.bfloat16).reshape(experts, block_slots, -1))
    hidden_grad = jnp.einsum(
        "erd,efd->erf", grad_arrived, expert_out, preferred_element_type=jnp.float32
    )
    pre_grad = gelu_back(hidden_grad)[0].astype(jnp.bfloat16)
    grad_expert_out = jnp.einsum(
        "erf,erd->efd", hidden, grad_arrived, preferred_element_type=jnp.float32
    )
    grad_expert_in = jnp.einsum(
        "erd,erf->edf", arrived, pre_grad, preferred_element_type=jnp.float32
    )
    input_part = jnp.einsum("erf,edf->erd", pre_grad, expert_in, preferred_element_type=jnp.float32)
    grad_returned = return_rows(input_part)
    moe_back = jnp.dot(dispatch, grad_returned, preferred_element_type=jnp.float32)
    resid_two_grad, grad_gain_moe = norm_two_back(moe_back + router_back)
    residual_grad = upstream + resid_two_grad
    att_grad = residual_grad.astype(jnp.bfloat16)
    grad_w_output = lax.dot_general(
        mixed_rows, att_grad, contract, preferred_element_type=jnp.float32
    )
    mixed_grad = lax.dot_general(
        att_grad, w_output, contract_last, preferred_element_type=jnp.float32
    ).astype(jnp.bfloat16)
    mixed_grad_heads = heads_view(mixed_grad)
    probs_again = jnp.exp(
        jnp.einsum("ishd,ithd->ihst", query_heads, key_heads, preferred_element_type=jnp.float32)
        * score_scale
        - log_total
    )
    value_grad = jnp.einsum(
        "ihst,ishd->ithd",
        probs_again.astype(jnp.bfloat16),
        mixed_grad_heads,
        preferred_element_type=jnp.float32,
    ).astype(jnp.bfloat16)
    probs_grad = jnp.einsum(
        "ishd,ithd->ihst", mixed_grad_heads, value_heads, preferred_element_type=jnp.float32
    )
    score_grad = probs_again * (
        probs_grad - jnp.sum(probs_again * probs_grad, axis=-1, keepdims=True)
    )
    score_grad = score_grad.astype(jnp.bfloat16)
    query_grad = (
        jnp.einsum("ihst,ithd->ishd", score_grad, key_heads, preferred_element_type=jnp.float32)
        * score_scale
    ).astype(jnp.bfloat16)
    key_grad = (
        jnp.einsum("ihst,ishd->ithd", score_grad, query_heads, preferred_element_type=jnp.float32)
        * score_scale
    ).astype(jnp.bfloat16)
    query_grad = as_rows(query_grad)
    key_grad = as_rows(key_grad)
    value_grad = as_rows(value_grad)
    grad_w_query = lax.dot_general(
        normed_one, query_grad, contract, preferred_element_type=jnp.float32
    )
    grad_w_key = lax.dot_general(normed_one, key_grad, contract, preferred_element_type=jnp.float32)
    grad_w_value = lax.dot_general(
        normed_one, value_grad, contract, preferred_element_type=jnp.float32
    )
    norm_grad_part = lax.dot_general(
        query_grad, w_query, contract_last, preferred_element_type=jnp.float32
    )
    norm_grad_part = norm_grad_part + lax.dot_general(
        key_grad, w_key, contract_last, preferred_element_type=jnp.float32
    )
    norm_grad_part = norm_grad_part + lax.dot_general(
        value_grad, w_value, contract_last, preferred_element_type=jnp.float32
    )
    normed_one_grad = tensor_total(norm_grad_part)
    input_ln_grad, grad_gain_attn = norm_one_back(normed_one_grad)
    grad_tokens = (residual_grad + input_ln_grad).astype(jnp.bfloat16)
    reduced = (
        *in_one_piece(
            (
                grad_w_query.astype(jnp.bfloat16),
                grad_w_key.astype(jnp.bfloat16),
                grad_w_value.astype(jnp.bfloat16),
            ),
            "dp",
            0,
            1,
        ),
        sent_and_summed(grad_w_output.astype(jnp.bfloat16), "dp", 1),
        sent_and_summed(grad_gain_attn.astype(jnp.bfloat16), "dp", 0),
        *in_one_piece_2(
            (grad_gain_moe.astype(jnp.bfloat16), grad_router.astype(jnp.bfloat16)), "dp", 0, 1
        ),
    )
    return (
        block_out,
        grad_tokens,
        reduced[4],
        reduced[5],
        reduced[0],
        reduced[1],
        reduced[2],
        reduced[3],
        reduced[6],
        grad_expert_in,
        grad_expert_out,
        clipped_query,
        clipped_key,
        head_max,
    )


def solution(mesh):
    in_specs = (
        P("dp", None),
        P(),
        P(None, "tensor"),
        P(None, "tensor"),
        P(None, "tensor"),
        P("tensor", None),
        P(),
        P(),
        P("dp", None, "tensor"),
        P("dp", "tensor", None),
        P("dp", None),
        P("dp", None),
        P(),
        P("tensor"),
        P("dp", None),
    )
    out_specs = (
        P("dp", None),
        P("dp", None),
        P("dp"),
        P("dp"),
        P("dp", "tensor"),
        P("dp", "tensor"),
        P("dp", "tensor"),
        P("tensor", "dp"),
        P("dp", None),
        P("dp", None, "tensor"),
        P("dp", "tensor", None),
        P(None, "tensor"),
        P(None, "tensor"),
        P("tensor"),
    )
    return jax.shard_map(body, mesh=mesh, in_specs=in_specs, out_specs=out_specs, check_vma=False)
```

profile of v0, /device:TPU:0, one launch (start us, length us, event | category | flops | bytes accessed | tf_op | source)
XLA Modules:
  0.0 1076.0 jit_solution(10547247930457523942)
XLA Ops:
  40.3 79.0 %all-reduce.5.cloned.1.call-done = f32[1182,768]{1,0:T(8,128)} async-done(((f32[1182,768]{1,0:T(8,128)}), f32[1182,768]{1,0:T(8,128)}) %all-reduce.5.cloned.1.call-update) | async-done | bytes 3631120 | tf_op jit(solution)/shard_map/psum | solution.py:61
  123.7 10.9 %fusion.35 = bf16[2720,768]{1,0:T(8,128)(2,1)} fusion(bf16[1182,768]{1,0:T(8,128)(2,1)S(1)} %multiply_convert_fusion.2, s32[1182]{0:T(1024)S(1)} %get-tuple-element.25, s32[1182]{0:T(1024)S(1)} %get-tuple-element.24, pred[1182]{0:T(1024)(128)(4,1)S(1)} %get-tuple-element.27, pred[1182]{0:T(1024)(128)(4,1)S(1)} %get-tuple-element.26), kind=kOutput, calls=%fused_computation.55 | convolution fusion | flops 4972540928 | bytes 6005292 | tf_op jit(solution)/shard_map/dot_general | solution.py:157
  134.6 5.1 reshape.380
  139.7 6.1 all-to-all-start
  147.1 9.4 fusion.1
  156.6 10.1 add_convert_fusion.1
  171.8 67.4 %all-to-all-done = bf16[8,340,768]{2,1,0:T(8,128)(2,1)} async-done(((bf16[8,340,768]{2,1,0:T(8,128)(2,1)}), bf16[8,340,768]{2,1,0:T(8,128)(2,1)}, u32[]{:S(2)}, u32[]{:S(2)}) %all-to-all-start) | async-done | bytes 4177952 | tf_op jit(solution)/shard_map/all_to_all | solution.py:65
  248.8 23.5 %multiply_convert_fusion = (bf16[2720,768]{1,0:T(8,128)(2,1)}, f32[2720,768]{1,0:T(8,128)}, f32[2720,768]{1,0:T(8,128)}) fusion(bf16[2720,768]{1,0:T(8,128)(2,1)} %reshape.381, bf16[1,768,768]{2,1,0:T(8,128)(2,1)S(1)} %copy-done), kind=kOutput, calls=%fused_computation.14 | convolution fusion | flops 3344424960 | bytes 26247168 | tf_op jit(solution)/shard_map/erd,edf->erf/dot_general | solution.py:161
  272.3 64.7 %all-to-all-done.2 = bf16[8,340,768]{2,1,0:T(8,128)(2,1)} async-done(((bf16[8,340,768]{2,1,0:T(8,128)(2,1)}), bf16[8,340,768]{2,1,0:T(8,128)(2,1)}, u32[]{:S(2)}, u32[]{:S(2)}) %all-to-all-start.2) | async-done | bytes 4177952 | tf_op jit(solution)/shard_map/all_to_all | solution.py:65
  342.1 11.6 %add_convert_fusion = bf16[2720,768]{1,0:T(8,128)(2,1)S(1)} fusion(f32[2720,768]{1,0:T(8,128)} %get-tuple-element.33, f32[2720,768]{1,0:T(8,128)} %get-tuple-element.44, bf16[2720,768]{1,0:T(8,128)(2,1)} %reshape.386, bf16[1,768,768]{2,1,0:T(8,128)(2,1)S(1)} %copy-done.71), kind=kOutput, calls=%fused_computation.12 | convolution fusion | flops 3237888000 | bytes 26247168 | tf_op jit(solution)/shard_map/erd,efd->erf/dot_general | solution.py:191
  353.7 5.7 convolution_bitcast_fusion
  359.4 5.6 convolution_bitcast_fusion.1
  365.0 285.4 %all-reduce.8 = (bf16[1,2720,768]{2,1,0:T(8,128)(2,1)}, bf16[1,2720,768]{2,1,0:T(8,128)(2,1)}) all-reduce(f32[1,2720,768]{2,1,0:T(8,128)} %convolution_bitcast_fusion.1, f32[1,2720,768]{2,1,0:T(8,128)} %convolution_bitcast_fusion), channel_id=1, replica_groups=mesh['dp'=8,'tensor'=4] {'tensor'}, use_global_device_ids=true, to_apply=%region_11.0 | all-reduce | flops 4177920 | bytes 25067520 | tf_op jit(solution)/shard_map/psum | solution.py:71
  650.4 24.2 %copy.186 = bf16[1,2720,768]{2,0,1:T(2,128)(2,1)} copy(bf16[1,2720,768]{2,1,0:T(8,128)(2,1)} %get-tuple-element.28) | data formatting | bytes 8355840 | tf_op jit(solution)/shard_map/convert_element_type | solution.py:71
  675.2 26.9 %reduce.13 = bf16[2720,768]{1,0:T(8,128)(2,1)} reduce(bf16[2720,1,768]{2,1,0:T(2,128)(2,1)} %bitcast.117, bf16[]{:T(256)} %broadcast.261), dimensions={1}, to_apply=%bitcast.116.reduce_sub_computation | reduce | bytes 8355842
  702.1 5.1 reshape.401
  711.7 24.2 %copy.185 = bf16[1,2720,768]{2,0,1:T(2,128)(2,1)} copy(bf16[1,2720,768]{2,1,0:T(8,128)(2,1)} %get-tuple-element.29) | data formatting | bytes 8355840 | tf_op jit(solution)/shard_map/convert_element_type | solution.py:71
  736.0 26.8 %reduce.14 = bf16[2720,768]{1,0:T(8,128)(2,1)} reduce(bf16[2720,1,768]{2,1,0:T(2,128)(2,1)} %bitcast.118, bf16[]{:T(256)} %broadcast.261), dimensions={1}, to_apply=%bitcast.115.reduce_sub_computation | reduce | bytes 8355842
  767.8 37.9 %all-to-all-done.1 = bf16[8,2,130560]{2,1,0:T(2,128)(2,1)} async-done(((bf16[8,2,130560]{2,1,0:T(2,128)(2,1)}), bf16[8,2,130560]{2,1,0:T(2,128)(2,1)}, u32[]{:S(2)}, u32[]{:S(2)}) %all-to-all-start.1) | async-done | bytes 4177952 | tf_op jit(solution)/shard_map/all_to_all | solution.py:72
  810.2 8.5 convolution_bitcast_fusion.2
  818.7 8.7 reshape.402
  827.5 10.1 fusion.9
  837.7 9.1 fusion.52
  847.3 56.0 %all-to-all-done.3 = bf16[8,2,130560]{2,1,0:T(2,128)(2,1)} async-done(((bf16[8,2,130560]{2,1,0:T(2,128)(2,1)}), bf16[8,2,130560]{2,1,0:T(2,128)(2,1)}, u32[]{:S(2)}, u32[]{:S(2)}) %all-to-all-start.3) | async-done | bytes 4177952 | tf_op jit(solution)/shard_map/all_to_all | solution.py:72
  903.3 8.6 reshape.404
  911.9 12.4 %fusion.27 = f32[1182,768]{1,0:T(8,128)S(1)} fusion(s32[1182]{0:T(1024)S(1)} %get-tuple-element.25, s32[1182]{0:T(1024)S(1)} %copy-done.62, pred[1182]{0:T(1024)(128)(4,1)S(1)} %get-tuple-element.27, pred[1182]{0:T(1024)(128)(4,1)S(1)} %copy-done.69, bf16[1,2720,768]{2,0,1:T(2,128)(2,1)} %bitcast.121), kind=kOutput, calls=%fused_computation.42 | convolution fusion | flops 4970451968 | bytes 7820844 | tf_op jit(solution)/shard_map/dot_general | solution.py:203
  960.4 6.0 all-to-all-start.7
  981.4 8.5 convolution_bitcast_fusion.3
  989.9 22.1 %pmax.7 = f32[3]{0:T(128)S(1)} all-reduce(f32[3]{0:T(128)S(1)} %get-tuple-element.18), channel_id=1, replica_groups=mesh['dp'=8,'tensor'=4] {'dp'}, use_global_device_ids=true, to_apply=%region_30.31 | all-reduce | flops 3 | bytes 24 | tf_op jit(solution)/shard_map/pmax | solution.py:137
  1017.2 33.3 %all-reduce.7.cloned.1.call-done = f32[1182,768]{1,0:T(8,128)} async-done(((f32[1182,768]{1,0:T(8,128)}), f32[1182,768]{1,0:T(8,128)}) %all-reduce.7.cloned.1.call-update) | async-done | bytes 3631120 | tf_op jit(solution)/shard_map/psum | solution.py:61
  1056.4 5.5 all-to-all-start.4
  1062.0 5.5 add_convert_fusion.2
  (264 shorter events, 136.7 us)
Async XLA Ops:
  7.2 241.6 %copy-start = (bf16[1,768,768]{2,1,0:T(8,128)(2,1)S(1)}, bf16[1,768,768]{2,1,0:T(8,128)(2,1)}, u32[]{:S(2)}) copy-start(bf16[1,768,768]{2,1,0:T(8,128)(2,1)} %param.23) | copy-start | bytes 3538948
  7.2 112.1 %all-reduce.5.cloned.1.call-start = ((), (), s32[]{:S(2)}) async-start(), calls=%async_computation.8 | async-start | bytes 7274496 | tf_op jit(solution)/shard_map/psum | solution.py:61
  40.0 82.3 %copy-start.56 = (f32[768]{0:T(1024)}, f32[768]{0:T(1024)S(1)}, u32[]{:S(2)}) copy-start(f32[768]{0:T(1024)S(1)} %convert_element_type.181) | copy-start | bytes 9220
  40.2 106.9 %copy-start.61 = (s32[1182]{0:T(1024)}, s32[1182]{0:T(1024)S(1)}, u32[]{:S(2)}) copy-start(s32[1182]{0:T(1024)S(1)} %get-tuple-element.24) | copy-start | bytes 14188
  40.3 106.8 %copy-start.68 = (pred[1182]{0:T(1024)(128)(4,1)}, pred[1182]{0:T(1024)(128)(4,1)S(1)}, u32[]{:S(2)}) copy-start(pred[1182]{0:T(1024)(128)(4,1)S(1)} %get-tuple-element.26) | copy-start | bytes 3550
  122.3 12.3 %copy-start.54 = (f32[1182]{0:T(1024)}, f32[1182]{0:T(1024)S(1)}, u32[]{:S(2)}) copy-start(f32[1182]{0:T(1024)S(1)} %multiply_reduce_fusion.3) | copy-start | bytes 14188
  122.3 12.3 %copy-start.46 = (f32[1182]{0:T(1024)}, f32[1182]{0:T(1024)S(1)}, u32[]{:S(2)}) copy-start(f32[1182]{0:T(1024)S(1)} %fusion.94) | copy-start | bytes 14188
  123.7 22.1 %copy-start.11 = (bf16[1182,768]{1,0:T(8,128)(2,1)}, bf16[1182,768]{1,0:T(8,128)(2,1)S(1)}, u32[]{:S(2)}) copy-start(bf16[1182,768]{1,0:T(8,128)(2,1)S(1)} %multiply_convert_fusion.2) | copy-start | bytes 5446660
  139.7 99.5 %all-to-all-start = ((bf16[8,340,768]{2,1,0:T(8,128)(2,1)}), bf16[8,340,768]{2,1,0:T(8,128)(2,1)}, u32[]{:S(2)}, u32[]{:S(2)}) async-start(bf16[8,340,768]{2,1,0:T(8,128)(2,1)} %reshape.380), calls=%async_computation | async-start | bytes 8454144 | tf_op jit(solution)/shard_map/all_to_all | solution.py:65
  239.2 97.8 %all-to-all-start.2 = ((bf16[8,340,768]{2,1,0:T(8,128)(2,1)}), bf16[8,340,768]{2,1,0:T(8,128)(2,1)}, u32[]{:S(2)}, u32[]{:S(2)}) async-start(bf16[8,340,768]{2,1,0:T(8,128)(2,1)} %reshape.385), calls=%async_computation.2 | async-start | bytes 8454144 | tf_op jit(solution)/shard_map/all_to_all | solution.py:65
  272.3 69.8 %copy-start.71 = (bf16[1,768,768]{2,1,0:T(8,128)(2,1)S(1)}, bf16[1,768,768]{2,1,0:T(8,128)(2,1)}, u32[]{:S(2)}) copy-start(bf16[1,768,768]{2,1,0:T(8,128)(2,1)} %param.24) | copy-start | bytes 3538948
  707.2 98.5 %all-to-all-start.1 = ((bf16[8,2,130560]{2,1,0:T(2,128)(2,1)}), bf16[8,2,130560]{2,1,0:T(2,128)(2,1)}, u32[]{:S(2)}, u32[]{:S(2)}) async-start(bf16[8,2,130560]{2,1,0:T(2,128)(2,1)} %reshape.401), calls=%async_computation.1 | async-start | bytes 8355840 | tf_op jit(solution)/shard_map/all_to_all | solution.py:72
  805.7 97.7 %all-to-all-start.3 = ((bf16[8,2,130560]{2,1,0:T(2,128)(2,1)}), bf16[8,2,130560]{2,1,0:T(2,128)(2,1)}, u32[]{:S(2)}, u32[]{:S(2)}) async-start(bf16[8,2,130560]{2,1,0:T(2,128)(2,1)} %reshape.403), calls=%async_computation.3 | async-start | bytes 8355840 | tf_op jit(solution)/shard_map/all_to_all | solution.py:72
  827.4 10.2 copy-start.5
  827.4 10.2 copy-start.14
  911.9 12.5 %copy-start.6 = (f32[1182,768]{1,0:T(8,128)S(1)}, f32[1182,768]{1,0:T(8,128)}, u32[]{:S(2)}) copy-start(f32[1182,768]{1,0:T(8,128)} %copy-done.4) | copy-start | bytes 10893316
  911.9 12.5 %copy-start.39 = (f32[1182]{0:T(1024)S(1)}, f32[1182]{0:T(1024)}, u32[]{:S(2)}) copy-start(f32[1182]{0:T(1024)} %copy-done.38) | copy-start | bytes 14188
  911.9 12.5 %copy-start.47 = (f32[1182]{0:T(1024)S(1)}, f32[1182]{0:T(1024)}, u32[]{:S(2)}) copy-start(f32[1182]{0:T(1024)} %copy-done.46) | copy-start | bytes 14188
  911.9 12.5 %copy-start.57 = (f32[768]{0:T(1024)S(1)}, f32[768]{0:T(1024)}, u32[]{:S(2)}) copy-start(f32[768]{0:T(1024)} %copy-done.56) | copy-start | bytes 9220
  911.9 12.5 %copy-start.59 = (bf16[768,8]{0,1:T(8,128)(2,1)S(1)}, bf16[768,8]{0,1:T(8,128)(2,1)}, u32[]{:S(2)}) copy-start(bf16[768,8]{0,1:T(8,128)(2,1)} %param.22) | copy-start | bytes 36868
  946.9 13.5 %all-to-all-start.5 = ((bf16[8,2,432]{2,1,0:T(2,128)(2,1)}), bf16[8,2,432]{2,1,0:T(2,128)(2,1)S(1)}, u32[]{:S(2)}, u32[]{:S(2)}) async-start(bf16[8,2,432]{2,1,0:T(2,128)(2,1)} %reshape.405), calls=%async_computation.5 | async-start | bytes 32768 | tf_op jit(solution)/shard_map/all_to_all | solution.py:25
  960.4 17.4 %all-to-all-start.7 = ((bf16[8,192,96]{2,1,0:T(8,128)(2,1)}), bf16[8,192,96]{2,1,0:T(8,128)(2,1)S(1)}, u32[]{:S(2)}, u32[]{:S(2)}) async-start(bf16[8,192,96]{2,1,0:T(8,128)(2,1)} %bitcast.114), calls=%async_computation.7 | async-start | bytes 786432 | tf_op jit(solution)/shard_map/all_to_all | solution.py:25
  966.4 84.1 %all-reduce.7.cloned.1.call-start = ((), (), s32[]{:S(2)}) async-start(), calls=%async_computation.9 | async-start | bytes 7274496 | tf_op jit(solution)/shard_map/psum | solution.py:61
  977.8 38.5 %all-to-all-start.6 = ((bf16[8,96,576]{2,1,0:T(8,128)(2,1)}), bf16[8,96,576]{2,1,0:T(8,128)(2,1)S(1)}, u32[]{:S(2)}, u32[]{:S(2)}) async-start(bf16[8,96,576]{2,1,0:T(8,128)(2,1)} %bitcast.9), calls=%async_computation.6 | async-start | bytes 1966080 | tf_op jit(solution)/shard_map/all_to_all | solution.py:25
  981.4 30.5 %copy-start.72 = (f32[3]{0:T(128)S(1)}, f32[3]{0:T(128)}, u32[]{:S(2)}) copy-start(f32[3]{0:T(128)} %param.28) | copy-start | bytes 40
  989.9 60.6 %copy-start.8 = (bf16[1182,768]{1,0:T(8,128)(2,1)S(1)}, bf16[1182,768]{1,0:T(8,128)(2,1)}, u32[]{:S(2)}) copy-start(bf16[1182,768]{1,0:T(8,128)(2,1)} %param.15) | copy-start | bytes 5446660
  989.9 60.6 %copy-start.34 = (f32[1182]{0:T(1024)S(1)}, f32[1182]{0:T(1024)}, u32[]{:S(2)}) copy-start(f32[1182]{0:T(1024)} %copy-done.33) | copy-start | bytes 14188
  989.9 60.6 %copy-start.51 = (f32[768]{0:T(1024)S(1)}, f32[768]{0:T(1024)}, u32[]{:S(2)}) copy-start(f32[768]{0:T(1024)} %copy-done.50) | copy-start | bytes 9220
  1012.0 41.6 %copy-start.73 = (f32[3]{0:T(128)}, f32[3]{0:T(128)S(1)}, u32[]{:S(2)}) copy-start(f32[3]{0:T(128)S(1)} %pmax.7) | copy-start | bytes 40
  1016.3 37.3 %copy-start.53 = (f32[1182]{0:T(1024)S(1)}, f32[1182]{0:T(1024)}, u32[]{:S(2)}) copy-start(f32[1182]{0:T(1024)} %copy-done.52) | copy-start | bytes 14188
  1016.3 37.3 %copy-start.45 = (f32[1182]{0:T(1024)S(1)}, f32[1182]{0:T(1024)}, u32[]{:S(2)}) copy-start(f32[1182]{0:T(1024)} %copy-done.44) | copy-start | bytes 14188
  1056.4 12.0 %all-to-all-start.4 = ((bf16[8,1,96]{2,1,0:T(2,128)(2,1)}), bf16[8,1,96]{2,1,0:T(2,128)(2,1)S(1)}, u32[]{:S(2)}, u32[]{:S(2)}) async-start(bf16[8,1,96]{2,1,0:T(2,128)(2,1)} %convert_element_type.221), calls=%async_computation.4 | async-start | bytes 8192 | tf_op jit(solution)/shard_map/all_to_all | solution.py:25
  (54 other events, 282.4 us)
Sparse Core Ops, SparseCore 0:
  40.1 79.1 all-reduce.4
  973.5 76.9 all-reduce.6
where the time goes:
time: 1080 us
  waiting for transfers between devices  344 us (32%)
  blocking collectives  307 us (28%)
  matrix products  164 us (15%)
  local copies, waits for them, and re-layouts  123 us (11%)
  other arithmetic  83 us (8%)
  starting transfers between devices  38.8 us (4%)
  between operations  15.5 us (1%)
    psum x1, blocking collectives, return_rows(): summed = lax.psum(partial_value, 'tensor').astype(jnp.bfloat16)  285 us
    all_to_all x2, waiting for transfers between devices, send_rows(): lax.all_to_all(buffer, 'dp', split_axis=0, concat_axis=1, tiled=True)  132 us
    psum x2, waiting for transfers between devices, tensor_total(): return lax.psum(partial_value, 'tensor')  112 us
    all_to_all x2, waiting for transfers between devices, return_rows(): lax.all_to_all(summed, 'dp', split_axis=1, concat_axis=0, tiled=True)  93.9 us
    unnamed x3, other arithmetic  53.7 us
    convert_element_type x2, local copies, waits for them, and re-layouts, return_rows(): summed = lax.psum(partial_value, 'tensor').astype(jnp.bfloat16)  48.5 us
    unnamed x159, local copies, waits for them, and re-layouts  34.4 us
    dot_general x1, matrix products, body(): jnp.einsum('erd,edf->erf', arrived, expert_in, preferred_element_type=jnp...  23.5 us
  transfers between devices with their start and end apart: 10, of which 8 were waited for; matrix products, arithmetic and copies ran while one was open for 17% of the time, Pallas kernels for 0%

commit v1 on v0

v1 whole, which is shorter than its diff:
```python
import functools
import math

import jax
import jax.numpy as jnp
from jax import lax
from jax.experimental import pallas as pl
from jax.experimental.pallas import tpu as pltpu
from jax.sharding import PartitionSpec as P

HD = 64
SEQ = 197
PIECE = 208
TOK_DEV = 1182
EPSILON = 1e-06
MESH = pl.DeviceIdType.MESH
VMEM_LIMIT = 60 * 2**20
VMEM = pltpu.VMEM
LOW, FULL = jnp.bfloat16, jnp.float32


def dot_plain(a, b):
    return jnp.dot(a, b, preferred_element_type=FULL)


def dot_last(a, b):
    return lax.dot_general(a, b, (((1,), (1,)), ((), ())), preferred_element_type=FULL)


def dot_first(a, b):
    return lax.dot_general(a, b, (((0,), (0,)), ((), ())), preferred_element_type=FULL)


def normalized(rows):
    centered = rows - jnp.mean(rows, axis=-1, keepdims=True)
    factor = lax.rsqrt(jnp.mean(centered * centered, axis=-1, keepdims=True) + EPSILON)
    return centered * factor, factor


def normalized_back(u, unit, factor):
    first = jnp.mean(u, axis=-1, keepdims=True)
    second = jnp.mean(u * unit, axis=-1, keepdims=True)
    return factor * (u - first - unit * second)


def same_index(size):
    rows = lax.broadcasted_iota(jnp.int32, (size, size), 0)
    return rows == lax.broadcasted_iota(jnp.int32, (size, size), 1)


def row_to_column(row):
    return jnp.sum(jnp.where(same_index(row.shape[1]), row, 0.0), axis=1, keepdims=True)


def column_to_row(column):
    return jnp.sum(jnp.where(same_index(column.shape[0]), column, 0.0), axis=0, keepdims=True)


def attention_probs(queries, keys):
    scores = dot_last(queries, keys) * HD**-0.5
    real = lax.broadcasted_iota(jnp.int32, scores.shape, 1) < SEQ
    scores = jnp.where(real, scores, -1e30)
    top = jnp.max(scores, axis=1, keepdims=True)
    powers = jnp.exp(scores - top)
    return powers * (1.0 / jnp.sum(powers, axis=1, keepdims=True)), top


def partner(dp, k, n):
    other, weight = 0, 1
    while weight < n:
        other = other + ((dp // weight + k // weight) % 2) * weight
        weight *= 2
    return other


def places():
    dp = lax.axis_index("dp")
    t = lax.axis_index("tensor")
    return dp, t, t % 2, t // 2, t + 1 - 2 * (t % 2), (t + 2) % 4


def remote(src, dst, sends, recvs, device):
    return pltpu.make_async_remote_copy(
        src_ref=src,
        dst_ref=dst,
        send_sem=sends,
        recv_sem=recvs,
        device_id=device,
        device_id_type=MESH,
    )


def signal(sem, device):
    pl.semaphore_signal(sem, inc=1, device_id=device, device_id_type=MESH)


def greet(n, dp, t, others):
    barrier = pltpu.get_barrier_semaphore()

    def one(k, carry):
        signal(barrier, (partner(dp, k, n), t))
        return carry

    lax.fori_loop(1, n, one, 0)
    for other in others:
        signal(barrier, (dp, other))


def await_greetings(n, others):
    pl.semaphore_wait(pltpu.get_barrier_semaphore(), n - 1 + len(others))


def image_rows(image):
    return pl.ds(pl.multiple_of(image * PIECE, PIECE), PIECE)


def dma(*shape):
    return pltpu.SemaphoreType.DMA(shape)


def near_count(n):
    return min(4, n)


class Spread:
    def __init__(self, n, hp, place, near_out, far_out, arrived, zs, zr, xs, xr, cs, cr, own):
        self.n, self.hp, self.near = n, hp, near_count(n)
        self.place, self.near_out, self.far_out, self.arrived = place, near_out, far_out, arrived
        self.zs, self.zr, self.xs, self.xr, self.cs, self.cr, self.own = zs, zr, xs, xr, cs, cr, own
        self.dp, self.t, self.half, self.side, self.mate, self.far = places()
        self.width = far_out.shape[2]

    def rows(self, owner):
        return pl.ds(pl.multiple_of(owner * self.hp, self.hp), self.hp)

    def columns(self, owner):
        return pl.ds(pl.multiple_of(owner * self.width, self.width), self.width)

    def peer(self, k):
        return (partner(self.dp, k, self.n), self.t)

    def own_copy(self):
        return pltpu.make_async_copy(
            self.near_out.at[0], self.arrived.at[0, self.rows(self.half)], self.own
        )

    def near_copy(self, k):
        return remote(
            self.near_out.at[k],
            self.arrived.at[k, self.rows(self.half)],
            self.zs.at[k],
            self.zr.at[k],
            self.peer(k),
        )

    def far_copy(self, k):
        return remote(
            self.far_out.at[k - self.near],
            self.arrived.at[k, self.rows(self.half), self.columns(self.side)],
            self.zs.at[k],
            self.zr.at[k],
            self.peer(k),
        )

    def side_copy(self, k, side):
        part = self.arrived.at[k, self.rows(self.half), self.columns(side)]
        return remote(part, part, self.xs.at[k], self.xr.at[k], (self.dp, self.far))

    def pair_copy(self, k, half):
        part = self.arrived.at[k, self.rows(half)]
        return remote(part, part, self.cs.at[k], self.cr.at[k], (self.dp, self.mate))

    def send(self, k, rows_ref):
        slots = lax.broadcasted_iota(jnp.int32, (self.hp, rows_ref.shape[0]), 0) + k * self.hp
        is_first = self.place[0:1, :] == slots
        is_second = self.place[1:2, :] == slots
        hot = jnp.where(is_first | is_second, 1.0, 0.0).astype(LOW)

        @pl.when(k < self.near)
        def _():
            self.near_out[k] = dot_plain(hot, rows_ref[...]).astype(LOW)

            @pl.when(k == 0)
            def _():
                self.own_copy().start()

            @pl.when(k > 0)
            def _():
                self.near_copy(k).start()

        @pl.when(k >= self.near)
        def _():
            mine = rows_ref[:, self.columns(self.side)]
            self.far_out[k - self.near] = dot_plain(hot, mine).astype(LOW)
            self.far_copy(k).start()

        return is_first, is_second

    def first_hop(self, k):
        @pl.when(k == 0)
        def _():
            self.own_copy().wait()

        @pl.when((k > 0) & (k < self.near))
        def _():
            self.near_copy(k).wait_recv()

        @pl.when(k >= self.near)
        def _():
            self.far_copy(k).wait_recv()
            self.side_copy(k, self.side).start()

    def second_hop(self, k):
        @pl.when(k >= self.near)
        def _():
            self.side_copy(k, 1 - self.side).wait_recv()

        self.pair_copy(k, self.half).start()

    def last_hop(self, k):
        self.pair_copy(k, 1 - self.half).wait_recv()

    def sent(self, k):
        @pl.when((k > 0) & (k < self.near))
        def _():
            self.near_copy(k).wait_send()

        @pl.when(k >= self.near)
        def _():
            self.far_copy(k).wait_send()
            self.side_copy(k, self.side).wait_send()

        self.pair_copy(k, self.half).wait_send()

    @staticmethod
    def scratch(n, hp, width):
        near = near_count(n)
        return [VMEM((near, hp, 2 * width), LOW), VMEM((n - near, hp, width), LOW)]

    @staticmethod
    def semaphores(n):
        return [dma(n), dma(n), dma(n), dma(n), dma(n), dma(n), pltpu.SemaphoreType.DMA]


class Total:
    def __init__(self, part_out, pair_in, far_out, far_in, ps, pr, fs, fr):
        self.part_out, self.pair_in, self.far_out, self.far_in = part_out, pair_in, far_out, far_in
        self.ps, self.pr, self.fs, self.fr = ps, pr, fs, fr
        self.dp, _, _, _, self.mate, self.far = places()

    def pair_copy(self, j):
        return remote(
            self.part_out.at[j], self.pair_in.at[j], self.ps.at[j], self.pr.at[j], (self.dp, self.mate)
        )

    def far_copy(self, j):
        return remote(
            self.far_out.at[j], self.far_in.at[j], self.fs.at[j], self.fr.at[j], (self.dp, self.far)
        )

    def give(self, j, rows):
        self.part_out[j] = rows
        self.pair_copy(j).start()

    def take(self, j, rows):
        self.pair_copy(j).wait_recv()
        self.far_out[j] = (rows + self.pair_in[j]).astype(LOW)
        self.far_copy(j).start()

    def result(self, j):
        self.far_copy(j).wait_recv()
        return self.far_out[j].astype(FULL) + self.far_in[j].astype(FULL)

    def sent(self, j):
        self.pair_copy(j).wait_send()
        self.far_copy(j).wait_send()

    @staticmethod
    def scratch(model):
        wide, slim = VMEM((3, PIECE, model), FULL), VMEM((3, PIECE, model), LOW)
        return [wide, wide, slim, slim, dma(3), dma(3), dma(3), dma(3)]


def front_kernel(
    n,
    hp,
    tokens_ref,
    upstream_ref,
    place_ref,
    gain_one_ref,
    gain_two_ref,
    query_w_ref,
    key_w_ref,
    value_w_ref,
    output_w_ref,
    normed_one_ref,
    query_ref,
    key_ref,
    value_ref,
    mixed_ref,
    residual_ref,
    normed_two_ref,
    peak_ref,
    spread_ref,
    *scratch,
):
    dp, t, half, side, mate, far = places()
    heads = query_w_ref.shape[1] // HD
    spread = Spread(n, hp, place_ref, *scratch[:2], spread_ref, *scratch[2:9])
    total = Total(*scratch[9:17])
    ns, nr = scratch[17:19]
    greet(n, dp, t, (mate, far))
    peak_ref[...] = jnp.full(peak_ref.shape, -1e30, FULL)

    def image_forward(image):
        rows = image_rows(image)
        unit, _ = normalized(tokens_ref[rows, :].astype(FULL))
        normed = (unit * gain_one_ref[...]).astype(LOW)
        normed_one_ref[rows, :] = normed
        queries = dot_plain(normed, query_w_ref[...]).astype(LOW)
        keys = dot_plain(normed, key_w_ref[...]).astype(LOW)
        values = dot_plain(normed, value_w_ref[...]).astype(LOW)
        query_ref[rows, :] = queries
        key_ref[rows, :] = keys
        value_ref[rows, :] = values
        mixed = []
        for h in range(heads):
            cols = slice(h * HD, (h + 1) * HD)
            probs, top = attention_probs(queries[:, cols], keys[:, cols])
            real = lax.broadcasted_iota(jnp.int32, top.shape, 0) < SEQ
            best = jnp.max(jnp.where(real, top, -1e30), axis=0, keepdims=True)
            peak_ref[h : h + 1, :] = jnp.maximum(peak_ref[h : h + 1, :], best)
            mixed.append(dot_plain(probs.astype(LOW), values[:, cols]))
        mixed = jnp.concatenate(mixed, axis=1).astype(LOW)
        mixed_ref[rows, :] = mixed
        return dot_plain(mixed, output_w_ref[...])

    def normed_copy(j, owner):
        rows = normed_two_ref.at[image_rows(2 * j + owner)]
        return remote(rows, rows, ns.at[j], nr.at[j], (dp, mate))

    def finish(j):
        rows = image_rows(2 * j + half)
        residual = tokens_ref[rows, :].astype(FULL) + total.result(j)
        residual_ref[rows, :] = residual
        unit, _ = normalized(residual)
        normed_two_ref[rows, :] = (unit * gain_two_ref[...]).astype(LOW)
        normed_copy(j, half).start()

    per_step = -(-n // 3)

    def step(j, carry):
        given = image_forward(2 * j + 1 - half)

        @pl.when(j == 0)
        def _():
            await_greetings(n, (mate, far))

        total.give(j, given)
        total.take(j, image_forward(2 * j + half))

        def dispatch(i, inner):
            @pl.when(i < n)
            def _():
                spread.send((i + spread.near) % n, upstream_ref)

            return inner

        lax.fori_loop(j * per_step, (j + 1) * per_step, dispatch, 0)

        @pl.when(j >= 1)
        def _():
            finish(j - 1)

        return carry

    lax.fori_loop(0, 3, step, 0)

    def each(body, first=0):
        def one(k, carry):
            body(k)
            return carry

        lax.fori_loop(first, n, one, 0)

    each(spread.first_hop)
    finish(2)
    each(spread.second_hop)
    each(spread.last_hop)
    each(spread.sent)
    for j in range(3):
        total.sent(j)
        normed_copy(j, half).wait_send()
        normed_copy(j, 1 - half).wait_recv()


def run_front(n, hp, tokens, upstream, place, gains, weights):
    rows, model = tokens.shape
    heads_width = weights[0].shape[1]
    vmem = pl.BlockSpec(memory_space=VMEM)
    shape = jax.ShapeDtypeStruct
    slim = shape((rows, heads_width), LOW)
    return pl.pallas_call(
        functools.partial(front_kernel, n, hp),
        out_shape=(
            shape((rows, model), LOW),
            slim,
            slim,
            slim,
            slim,
            shape((rows, model), FULL),
            shape((rows, model), LOW),
            shape((8, 128), FULL),
            shape((n, 2 * hp, model), LOW),
        ),
        in_specs=[vmem] * 9,
        out_specs=[vmem] * 9,
        scratch_shapes=[
            *Spread.scratch(n, hp, model // 2),
            *Spread.semaphores(n),
            *Total.scratch(model),
            dma(3),
            dma(3),
        ],
        compiler_params=pltpu.CompilerParams(
            collective_id=0, has_side_effects=True, vmem_limit_bytes=VMEM_LIMIT
        ),
        name="front",
    )(tokens, upstream, place, *gains, *weights)


def expert_kernel(
    n,
    hp,
    place_ref,
    gate_ref,
    normed_ref,
    first_ref,
    second_ref,
    peak_ref,
    upstream_hbm,
    answer_ref,
    back_ref,
    gate_sum_ref,
    grad_first_ref,
    grad_second_ref,
    top_ref,
    *scratch,
):
    dp, t, half, side, mate, far = places()
    arrived = scratch[2]
    spread = Spread(n, hp, place_ref, *scratch[:10])
    (
        upstream,
        hidden_all,
        pre_grad_all,
        parts,
        pair_in,
        kept,
        far_out,
        far_in,
        final,
        gate_out,
        gate_in,
        sum_out,
        sum_in,
        sums,
        peaks,
        us,
        ps,
        pr,
        fs,
        fr,
        rs,
        rr,
        ms,
        mr,
        gs,
        gr,
        hs,
        hr,
        ks,
        kr,
        qs,
        qr,
        ss,
        sr,
    ) = scratch[10:]
    model = normed_ref.shape[1]
    width = model // 2
    backs = (answer_ref, back_ref)
    greet(n, dp, t, [(t + d) % 4 for d in (1, 2, 3)])
    fetch = pltpu.make_async_copy(upstream_hbm, upstream, us)
    fetch.start()

    def gate_copy(k):
        return remote(gate_out.at[k], gate_in.at[k, half], gs.at[k], gr.at[k], spread.peer(k))

    def gate_pair_copy(k, owner):
        tile = gate_in.at[k, owner]
        return remote(tile, tile, hs.at[k], hr.at[k], (dp, mate))

    def part_copy(k):
        return remote(
            parts.at[k % 3, :, spread.rows(1 - half)],
            pair_in.at[k],
            ps.at[k % 3],
            pr.at[k],
            (dp, mate),
        )

    def far_copy(k):
        return remote(far_out.at[k % 3], far_in.at[k], fs.at[k % 3], fr.at[k], (dp, far))

    def return_copy(k, j):
        return remote(
            final.at[j, k],
            backs[j].at[k, spread.rows(half)],
            rs.at[j, k],
            rr.at[j, k],
            spread.peer(k),
        )

    def mate_copy(k, j, owner):
        rows = backs[j].at[k, spread.rows(owner)]
        return remote(rows, rows, ms.at[j, k], mr.at[j, k], (dp, mate))

    def sum_copy(k):
        return remote(sum_out.at[k], sum_in.at[k], ks.at[k], kr.at[k], spread.peer(k))

    def peak_copy(k):
        return remote(peak_ref, peaks.at[k], qs.at[k], qr.at[k], spread.peer(k))

    def share_copy(d, owner):
        return remote(
            sums.at[owner], sums.at[owner], ss.at[d - 1], sr.at[d - 1], (dp, (t + d) % 4)
        )

    def loop(body, first=0, last=n):
        def one(k, carry):
            body(k)
            return carry

        lax.fori_loop(first, last, one, 0)

    await_greetings(n, (1, 2, 3))

    def dispatch(k):
        is_first, is_second = spread.send(k, normed_ref)
        gate = jnp.sum(
            jnp.where(is_first, gate_ref[0:1, :], 0.0) + jnp.where(is_second, gate_ref[1:2, :], 0.0),
            axis=1,
            keepdims=True,
        )
        tile = jnp.broadcast_to(column_to_row(gate), (8, hp))

        @pl.when(k == 0)
        def _():
            gate_in[0, half] = tile

        @pl.when(k > 0)
        def _():
            gate_out[k] = tile
            gate_copy(k).start()
            peak_copy(k).start()

    loop(dispatch)
    fetch.wait()

    def chunk(k):
        gate = jnp.concatenate(
            [row_to_column(gate_in[k, 0, 0:1, :]), row_to_column(gate_in[k, 1, 0:1, :])], axis=0
        )
        gradient = upstream[k].astype(FULL)
        answer_grad = (gradient * gate).astype(LOW)
        pre = dot_plain(arrived[k], first_ref[...])
        share = 0.5 * (1.0 + lax.erf(pre * math.sqrt(0.5)))
        slope = share + pre * (jnp.exp(-0.5 * pre * pre) * (1.0 / math.sqrt(2.0 * math.pi)))
        hidden = (pre * share).astype(LOW)
        hidden_all[k] = hidden
        answer = dot_plain(hidden, second_ref[...])
        parts[k % 3, 0] = answer.astype(LOW)
        gate_sum = jnp.sum(answer * gradient, axis=1, keepdims=True)
        upstream[k] = answer_grad
        pre_grad = (dot_last(answer_grad, second_ref[...]) * slope).astype(LOW)
        pre_grad_all[k] = pre_grad
        parts[k % 3, 1] = dot_last(pre_grad, first_ref[...]).astype(LOW)
        tile = jnp.broadcast_to(column_to_row(gate_sum), (8, 2 * hp))

        @pl.when(k == 0)
        def _():
            sum_in[0] = tile

        @pl.when(k > 0)
        def _():
            sum_out[k] = tile
            sum_copy(k).start()

    def step(i):
        @pl.when(i < n)
        def _():
            spread.first_hop(i)

        @pl.when((i >= 1) & (i < n + 1))
        def _():
            k = i - 1
            spread.second_hop(k)

            @pl.when(k > 0)
            def _():
                gate_copy(k).wait_recv()

            gate_pair_copy(k, half).start()

        @pl.when((i >= 2) & (i < n + 2))
        def _():
            k = i - 2
            spread.last_hop(k)
            gate_pair_copy(k, 1 - half).wait_recv()

            @pl.when(k >= 3)
            def _():
                part_copy(k - 3).wait_send()

            chunk(k)
            part_copy(k).start()

        @pl.when((i >= 3) & (i < n + 3))
        def _():
            k = i - 3
            part_copy(k).wait_recv()

            @pl.when(k >= 3)
            def _():
                far_copy(k - 3).wait_send()

            for j in range(2):
                whole = parts[k % 3, j, spread.rows(half), :].astype(FULL) + pair_in[k, j].astype(FULL)
                low, high = whole[:, :width], whole[:, width:]
                kept[k % 3, j] = jnp.where(side == 0, low, high)
                far_out[k % 3, j] = jnp.where(side == 0, high, low).astype(LOW)
            far_copy(k).start()

        @pl.when(i >= 4)
        def _():
            k = i - 4
            far_copy(k).wait_recv()
            for j in range(2):
                rows = (kept[k % 3, j] + far_in[k, j].astype(FULL)).astype(LOW)

                @pl.when(k == 0)
                def _():
                    backs[j][0, spread.rows(half), :] = rows

                @pl.when(k > 0)
                def _():
                    final[j, k] = rows
                    return_copy(k, j).start()

    loop(step, 0, n + 4)

    tile = 256

    def grads(m):
        cols = pl.ds(pl.multiple_of(m * tile, tile), tile)
        rows_in = arrived[:, :, cols].reshape(n * 2 * hp, tile)
        grad_first_ref[cols, :] = dot_first(rows_in, pre_grad_all[...].reshape(n * 2 * hp, -1))
        hidden = hidden_all[:, :, cols].reshape(n * 2 * hp, tile)
        grad_second_ref[cols, :] = dot_first(hidden, upstream[...].reshape(n * 2 * hp, model))

    loop(grads, 0, model // tile)

    peaks[0] = peak_ref[...]

    def collect(k):
        for j in (1, 0):

            @pl.when(k > 0)
            def _():
                return_copy(k, j).wait_recv()

            mate_copy(k, j, half).start()

        @pl.when(k > 0)
        def _():
            peak_copy(k).wait_recv()
            sum_copy(k).wait_recv()

        sums[t, pl.ds(k, 1), :] = sum_in[k, 0:1, :]

    loop(collect)
    for d in (1, 2, 3):
        share_copy(d, t).start()
    top_ref[...] = jnp.max(peaks[...], axis=0)
    for d in (1, 2, 3):
        share_copy(d, (t + 4 - d) % 4).wait_recv()
    gate_sum_ref[...] = (sums[0] + sums[1]) + (sums[2] + sums[3])

    def finish(k):
        for j in range(2):
            mate_copy(k, j, 1 - half).wait_recv()
            mate_copy(k, j, half).wait_send()

            @pl.when(k > 0)
            def _():
                return_copy(k, j).wait_send()

        spread.sent(k)
        gate_pair_copy(k, half).wait_send()

        @pl.when(k > 0)
        def _():
            gate_copy(k).wait_send()
            sum_copy(k).wait_send()
            peak_copy(k).wait_send()

        @pl.when(k >= n - 3)
        def _():
            part_copy(k).wait_send()
            far_copy(k).wait_send()

    loop(finish)
    for d in (1, 2, 3):
        share_copy(d, t).wait_send()


def run_experts(n, hp, place, gates, normed, first, second, peak, upstream):
    model = normed.shape[1]
    width = model // 2
    hidden = first.shape[1]
    vmem = pl.BlockSpec(memory_space=VMEM)
    shape = jax.ShapeDtypeStruct
    return pl.pallas_call(
        functools.partial(expert_kernel, n, hp),
        out_shape=(
            shape((n, 2 * hp, width), LOW),
            shape((n, 2 * hp, width), LOW),
            shape((n, 2 * hp), FULL),
            shape((model, hidden), FULL),
            shape((hidden, model), FULL),
            shape(peak.shape, FULL),
        ),
        in_specs=[vmem] * 6 + [pl.BlockSpec(memory_space=pl.ANY)],
        out_specs=[vmem] * 6,
        scratch_shapes=[
            *Spread.scratch(n, hp, width),
            VMEM((n, 2 * hp, model), LOW),
            *Spread.semaphores(n),
            VMEM((n, 2 * hp, model), LOW),
            VMEM((n, 2 * hp, hidden), LOW),
            VMEM((n, 2 * hp, hidden), LOW),
            VMEM((3, 2, 2 * hp, model), LOW),
            VMEM((n, 2, hp, model), LOW),
            VMEM((3, 2, hp, width), FULL),
            VMEM((3, 2, hp, width), LOW),
            VMEM((n, 2, hp, width), LOW),
            VMEM((2, n, hp, width), LOW),
            VMEM((n, 8, hp), FULL),
            VMEM((n, 2, 8, hp), FULL),
            VMEM((n, 8, 2 * hp), FULL),
            VMEM((n, 8, 2 * hp), FULL),
            VMEM((4, n, 2 * hp), FULL),
            VMEM((n, *peak.shape), FULL),
            pltpu.SemaphoreType.DMA,
            dma(3), dma(n), dma(3), dma(n), dma(2, n), dma(2, n), dma(2, n), dma(2, n),
            dma(n), dma(n), dma(n), dma(n), dma(n), dma(n), dma(n), dma(n), dma(3), dma(3),
        ],
        compiler_params=pltpu.CompilerParams(
            collective_id=1, has_side_effects=True, vmem_limit_bytes=VMEM_LIMIT
        ),
        name="experts",
    )(place, gates, normed, first, second, peak, upstream)


def back_kernel(
    n,
    answer_ref,
    back_ref,
    gate_sum_ref,
    index_ref,
    residual_ref,
    upstream_ref,
    normed_one_ref,
    query_ref,
    key_ref,
    value_ref,
    mixed_ref,
    tokens_ref,
    gain_one_ref,
    gain_two_ref,
    query_w_ref,
    key_w_ref,
    value_w_ref,
    output_w_ref,
    router_ref,
    block_ref,
    grad_tokens_ref,
    weights_ref,
    small_ref,
    *scratch,
):
    dp, t, half, side, mate, far = places()
    (
        moe_mine,
        moe_other,
        block_mine,
        block_other,
        attention_grad,
        residual_grad,
        query_grad,
        key_grad,
        value_grad,
        gain_two_sum,
        gain_one_sum,
        gain_one_all,
        router_sum,
        router_in,
        gain_two_in,
        totals,
        pieces,
        pieces_in,
        as_,
        ar,
        bs,
        br,
        ts,
        tr,
        cs,
        cr,
        gs,
        gr,
        ws,
        wr,
        ls,
        lr,
        os_,
        or_,
    ) = scratch[:34]
    total = Total(*scratch[34:])
    heads = query_w_ref.shape[1] // HD
    model = tokens_ref.shape[1]
    width = model // 2
    slots = answer_ref.shape[0]
    piece = pieces.shape[1]
    greet(n, dp, t, [(t + d) % 4 for d in (1, 2, 3)])

    def moe_copy(j):
        return remote(moe_mine.at[j], moe_other.at[j], as_.at[j], ar.at[j], (dp, far))

    def block_copy(j):
        return remote(block_mine.at[j], block_other.at[j], bs.at[j], br.at[j], (dp, far))

    def attention_copy(j, owner):
        rows = attention_grad.at[image_rows(2 * j + owner)]
        return remote(rows, rows, ts.at[j], tr.at[j], (dp, mate))

    def tokens_copy(j, owner):
        rows = grad_tokens_ref.at[image_rows(2 * j + owner)]
        return remote(rows, rows, cs.at[j], cr.at[j], (dp, mate))

    def block_pair_copy(j, owner):
        rows = block_ref.at[image_rows(2 * j + owner)]
        return remote(rows, rows, ls.at[j], lr.at[j], (dp, mate))

    def gain_copy(d, owner):
        return remote(
            gain_one_all.at[owner], gain_one_all.at[owner], gs.at[d - 1], gr.at[d - 1], (dp, (t + d) % 4)
        )

    def router_copy():
        return remote(router_sum, router_in, os_.at[0], or_.at[0], (dp, mate))

    def gain_two_copy():
        return remote(gain_two_sum, gain_two_in, os_.at[1], or_.at[1], (dp, mate))

    def piece_copy(k):
        return remote(
            pieces.at[k], pieces_in.at[k], ws.at[k], wr.at[k], (partner(dp, k, n), t)
        )

    def loop(body, first, last):
        def one(k, carry):
            body(k)
            return carry

        lax.fori_loop(first, last, one, 0)

    def both_sides(mine, other):
        low = jnp.where(side == 0, mine, other)
        high = jnp.where(side == 0, other, mine)
        return jnp.concatenate([low, high], axis=1)

    def hots(rows):
        columns = lax.broadcasted_iota(jnp.int32, (PIECE, slots), 1)
        return index_ref[rows, 0:1] == columns, index_ref[rows, 1:2] == columns

    def as_low(mask):
        return jnp.where(mask, 1.0, 0.0).astype(LOW)

    gain_two_sum[...] = jnp.zeros_like(gain_two_sum)
    gain_one_sum[...] = jnp.zeros_like(gain_one_sum)
    router_sum[...] = jnp.zeros_like(router_sum)
    await_greetings(n, (1, 2, 3))

    def combine(j):
        first, second = hots(image_rows(2 * j + half))
        moe_mine[j] = dot_plain(as_low(first | second), back_ref[...]).astype(LOW)
        moe_copy(j).start()

    loop(combine, 0, 3)

    def gates_of(rows, normed):
        logits = dot_plain(normed, router_ref[...])
        lanes = lax.broadcasted_iota(jnp.int32, logits.shape, 1)
        hot_one = index_ref[rows, 2:3] == lanes
        hot_two = index_ref[rows, 3:4] == lanes
        one = jnp.sum(jnp.where(hot_one, logits, 0.0), axis=1, keepdims=True)
        two = jnp.sum(jnp.where(hot_two, logits, 0.0), axis=1, keepdims=True)
        top = jnp.maximum(one, two)
        one, two = jnp.exp(one - top), jnp.exp(two - top)
        return one / (one + two), two / (one + two), hot_one, hot_two

    def moe_back(j):
        rows = image_rows(2 * j + half)
        unit, factor = normalized(residual_ref[rows, :])
        normed = (unit * gain_two_ref[...]).astype(LOW)
        gate_one, gate_two, hot_one, hot_two = gates_of(rows, normed)
        first, second = hots(rows)
        slot_sums = gate_sum_ref[0:1, :]
        grad_one = jnp.sum(jnp.where(first, slot_sums, 0.0), axis=1, keepdims=True)
        grad_two = jnp.sum(jnp.where(second, slot_sums, 0.0), axis=1, keepdims=True)
        mean = gate_one * grad_one + gate_two * grad_two
        logit_grad = jnp.where(hot_one, gate_one * (grad_one - mean), 0.0)
        logit_grad = logit_grad + jnp.where(hot_two, gate_two * (grad_two - mean), 0.0)
        logit_grad = logit_grad.astype(LOW)
        router_sum[...] += dot_first(normed, logit_grad)
        normed_grad = dot_last(logit_grad, router_ref[...])
        moe_copy(j).wait_recv()
        normed_grad = normed_grad + both_sides(moe_mine[j].astype(FULL), moe_other[j].astype(FULL))
        gain_two_sum[...] += jnp.sum((normed_grad * unit).reshape(PIECE // 8, 8, model), axis=0)
        grad = normalized_back(normed_grad * gain_two_ref[...], unit, factor)
        grad = grad + upstream_ref[rows, :].astype(FULL)
        residual_grad[j] = grad
        attention_grad[rows, :] = grad.astype(LOW)
        attention_copy(j, half).start()

    loop(moe_back, 0, 3)
    router_copy().start()
    gain_two_copy().start()

    def image_back(image):
        rows = image_rows(image)
        mixed_grad = dot_last(attention_grad[rows, :], output_w_ref[...]).astype(LOW)
        queries, keys, values = query_ref[rows, :], key_ref[rows, :], value_ref[rows, :]
        query_parts, key_parts, value_parts = [], [], []
        for h in range(heads):
            cols = slice(h * HD, (h + 1) * HD)
            probs, _ = attention_probs(queries[:, cols], keys[:, cols])
            value_parts.append(dot_first(probs.astype(LOW), mixed_grad[:, cols]))
            probs_grad = dot_last(mixed_grad[:, cols], values[:, cols])
            level = jnp.sum(probs * probs_grad, axis=1, keepdims=True)
            score_grad = (probs * (probs_grad - level)).astype(LOW)
            query_parts.append(dot_plain(score_grad, keys[:, cols]) * HD**-0.5)
            key_parts.append(dot_first(score_grad, queries[:, cols]) * HD**-0.5)
        grads = [jnp.concatenate(p, axis=1).astype(LOW) for p in (query_parts, key_parts, value_parts)]
        query_grad[rows, :], key_grad[rows, :], value_grad[rows, :] = grads
        part = dot_last(grads[0], query_w_ref[...])
        part = part + dot_last(grads[1], key_w_ref[...])
        part = part + dot_last(grads[2], value_w_ref[...])
        unit, _ = normalized(tokens_ref[rows, :].astype(FULL))
        gain_one_sum[...] += jnp.sum((part * unit).reshape(PIECE // 8, 8, model), axis=0)
        return part

    def block_rows(j):
        rows = image_rows(2 * j + half)
        residual = residual_ref[rows, :]
        unit, _ = normalized(residual)
        gate_one, gate_two, _, _ = gates_of(rows, (unit * gain_two_ref[...]).astype(LOW))
        first, second = hots(rows)
        from_first = dot_plain(as_low(first), answer_ref[...])
        from_second = dot_plain(as_low(second), answer_ref[...])
        mine = jnp.where(side == 0, residual[:, :width], residual[:, width:])
        block_mine[j] = (mine + (gate_one * from_first + gate_two * from_second)).astype(LOW)
        block_copy(j).start()

    def attention_back(j):
        attention_copy(j, 1 - half).wait_recv()
        total.give(j, image_back(2 * j + 1 - half))
        total.take(j, image_back(2 * j + half))
        block_rows(j)

    loop(attention_back, 0, 3)

    gain_one_all[t] = gain_one_sum[...]
    for d in (1, 2, 3):
        gain_copy(d, t).start()
    normed_one = normed_one_ref[...]
    totals[:, :model] = jnp.concatenate(
        [
            dot_first(normed_one, query_grad[...]),
            dot_first(normed_one, key_grad[...]),
            dot_first(normed_one, value_grad[...]),
            dot_first(attention_grad[...], mixed_ref[...]),
        ],
        axis=1,
    )
    router_copy().wait_recv()
    gain_two_copy().wait_recv()
    for d in (1, 2, 3):
        gain_copy(d, (t + 4 - d) % 4).wait_recv()
    lanes = lax.broadcasted_iota(jnp.int32, (model, 128), 1)

    def column_of(eight):
        row = jnp.sum(eight, axis=0, keepdims=True)
        return jnp.concatenate(
            [row_to_column(row[:, i : i + 256]) for i in range(0, model, 256)], axis=0
        )

    gain_one_total = (gain_one_all[0] + gain_one_all[1]) + (gain_one_all[2] + gain_one_all[3])
    totals[:, model:] = (
        router_sum[...]
        + router_in[...]
        + jnp.where(lanes == 126, column_of(gain_one_total), 0.0)
        + jnp.where(lanes == 127, column_of(gain_two_sum[...] + gain_two_in[...]), 0.0)
    )

    def send_piece(k):
        at = partner(dp, k, n) * piece
        grain = math.gcd(piece, 8)
        span = -(-(piece + 8 - grain) // 8) * 8
        taken = totals[pl.ds(pl.multiple_of(at // 8 * 8, 8), span), :]
        rows = taken[:piece]
        for shift in range(grain, 8, grain):
            rows = jnp.where(at % 8 == shift, taken[shift : shift + piece], rows)
        pieces[k] = rows.astype(LOW)

        @pl.when(k > 0)
        def _():
            piece_copy(k).start()

    loop(send_piece, 0, n)

    def tokens_back(j):
        rows = image_rows(2 * j + half)
        normed_grad = total.result(j)
        unit, factor = normalized(tokens_ref[rows, :].astype(FULL))
        grad = normalized_back(normed_grad * gain_one_ref[...], unit, factor)
        grad_tokens_ref[rows, :] = (residual_grad[j] + grad).astype(LOW)
        tokens_copy(j, half).start()
        block_copy(j).wait_recv()
        block_ref[rows, :] = both_sides(block_mine[j], block_other[j])
        block_pair_copy(j, half).start()

    loop(tokens_back, 0, 3)
    pieces_in[0] = pieces[0]

    def arrive(k):
        piece_copy(k).wait_recv()

    loop(arrive, 1, n)
    whole = jnp.sum(pieces_in[...].astype(FULL), axis=0)
    weights_ref[...] = whole[:, :model]
    small_ref[...] = whole[:, model:]

    for j in range(3):
        moe_copy(j).wait_send()
        block_copy(j).wait_send()
        attention_copy(j, half).wait_send()
        total.sent(j)
        tokens_copy(j, half).wait_send()
        tokens_copy(j, 1 - half).wait_recv()
        block_pair_copy(j, half).wait_send()
        block_pair_copy(j, 1 - half).wait_recv()
        gain_copy(j + 1, t).wait_send()
    router_copy().wait_send()
    gain_two_copy().wait_send()

    def left(k):
        piece_copy(k).wait_send()

    loop(left, 1, n)


def run_back(n, *operands):
    tokens = operands[11]
    rows, model = tokens.shape
    heads_width = operands[7].shape[1]
    width = model // 2
    piece = model // n
    vmem = pl.BlockSpec(memory_space=VMEM)
    shape = jax.ShapeDtypeStruct
    slim = VMEM((3, PIECE, width), LOW)
    heads = VMEM((rows, heads_width), LOW)
    eight = VMEM((8, model), FULL)
    return pl.pallas_call(
        functools.partial(back_kernel, n),
        out_shape=(
            shape((rows, model), LOW),
            shape((rows, model), LOW),
            shape((piece, model), FULL),
            shape((piece, 128), FULL),
        ),
        in_specs=[vmem] * len(operands),
        out_specs=[vmem] * 4,
        scratch_shapes=[
            slim, slim, slim, slim,
            VMEM((rows, model), LOW),
            VMEM((3, PIECE, model), FULL),
            heads, heads, heads,
            eight, eight,
            VMEM((4, 8, model), FULL),
            VMEM((model, 128), FULL),
            VMEM((model, 128), FULL),
            eight,
            VMEM((model, model + 128), FULL),
            VMEM((n, piece, model + 128), LOW),
            VMEM((n, piece, model + 128), LOW),
            dma(3), dma(3), dma(3), dma(3), dma(3), dma(3), dma(3), dma(3), dma(3), dma(3),
            dma(n), dma(n), dma(3), dma(3), dma(2), dma(2),
            *Total.scratch(model),
        ],
        compiler_params=pltpu.CompilerParams(
            collective_id=2, has_side_effects=True, vmem_limit_bytes=VMEM_LIMIT
        ),
        name="back",
    )(*operands)


def body(
    tokens,
    gain_attn,
    w_query,
    w_key,
    w_value,
    w_output,
    gain_moe,
    w_router,
    expert_in,
    expert_out,
    routes,
    slot_ids,
    capacity,
    threshold,
    cotangent,
):
    n = lax.axis_size("dp")
    row_count, model = tokens.shape
    images = row_count // SEQ
    heads_here = w_query.shape[1] // HD
    slot_count = 23 * TOK_DEV // (10 * n) + 1
    per_half = -(-slot_count // 2)
    hp = -(-per_half // 16) * 16
    dp_here = lax.axis_index("dp")
    half_here = lax.axis_index("tensor") % 2

    def padded(rows, fill=0):
        split = rows.reshape(images, SEQ, -1)
        split = jnp.pad(split, ((0, 0), (0, PIECE - SEQ), (0, 0)), constant_values=fill)
        return split.reshape(images * PIECE, -1)

    def unpadded(rows):
        return rows.reshape(images, PIECE, -1)[:, :SEQ].reshape(row_count, -1)

    expert_ids = jnp.arange(n, dtype=jnp.int32)
    limits = jnp.sum(
        jnp.where(routes[:, :, None] == expert_ids, capacity[None, None, :], 0), axis=-1
    )
    kept = slot_ids < limits
    step = jnp.bitwise_xor(routes, dp_here)
    slot_half = slot_ids // per_half
    in_half = slot_ids % per_half
    place = jnp.where(kept & (slot_half == half_here), step * hp + in_half, -1)
    position = jnp.where(kept, step * (2 * hp) + slot_half * hp + in_half, -1)
    index = padded(jnp.concatenate([position, routes, place], axis=1), -1)
    place_rows = jnp.pad(index[:, 4:6].T, ((0, 6), (0, 0)), constant_values=-1)
    route_rows = index[:, 2:4].T

    tokens_in = padded(tokens)
    upstream = padded(cotangent)
    gain_one = gain_attn.astype(FULL)[None]
    gain_two = gain_moe.astype(FULL)[None]
    weights = (w_query, w_key, w_value, w_output)
    normed_one, query, key, value, mixed, residual, normed_two, peak, spread = run_front(
        n, hp, tokens_in, upstream, place_rows, (gain_one, gain_two), weights
    )
    logit_rows = lax.dot_general(
        w_router, normed_two, (((0,), (1,)), ((), ())), preferred_element_type=FULL
    )
    chosen = jnp.stack(
        [jnp.sum(jnp.where(expert_ids[:, None] == route_rows[k], logit_rows, 0.0), axis=0) for k in (0, 1)]
    )
    gate_rows = jnp.pad(jax.nn.softmax(chosen, axis=0), ((0, 6), (0, 0)))
    answers, back, gate_sums, grad_first, grad_second, top = run_experts(
        n, hp, place_rows, gate_rows, normed_two, expert_in[0], expert_out[0], peak, spread
    )
    router_wide = jnp.pad(w_router, ((0, 0), (0, 128 - n)))
    block_rows, token_rows, weight_grads, small = run_back(
        n,
        answers.reshape(n * 2 * hp, -1),
        back.reshape(n * 2 * hp, -1),
        jnp.broadcast_to(gate_sums.reshape(1, -1), (8, n * 2 * hp)),
        index,
        residual,
        upstream,
        normed_one,
        query,
        key,
        value,
        mixed,
        tokens_in,
        gain_one,
        gain_two,
        *weights,
        router_wide,
    )
    head_max = top[:heads_here, 0]
    column_factor = jnp.repeat(jnp.sqrt(jnp.minimum(1.0, threshold / head_max)), HD)[None, :]
    wide = w_query.shape[1]
    return (
        unpadded(block_rows),
        unpadded(token_rows),
        small[:, 126],
        small[:, 127],
        weight_grads[:, :wide],
        weight_grads[:, wide : 2 * wide],
        weight_grads[:, 2 * wide : 3 * wide],
        weight_grads[:, 3 * wide :].T,
        small[:, :n],
        grad_first[None],
        grad_second[None],
        w_query.astype(FULL) * column_factor,
        w_key.astype(FULL) * column_factor,
        head_max,
    )


def solution(mesh):
    in_specs = (
        P("dp", None),
        P(),
        P(None, "tensor"),
        P(None, "tensor"),
        P(None, "tensor"),
        P("tensor", None),
        P(),
        P(),
        P("dp", None, "tensor"),
        P("dp", "tensor", None),
        P("dp", None),
        P("dp", None),
        P(),
        P("tensor"),
        P("dp", None),
    )
    out_specs = (
        P("dp", None),
        P("dp", None),
        P("dp"),
        P("dp"),
        P("dp", "tensor"),
        P("dp", "tensor"),
        P("dp", "tensor"),
        P("tensor", "dp"),
        P("dp", None),
        P("dp", None, "tensor"),
        P("dp", "tensor", None),
        P(None, "tensor"),
        P(None, "tensor"),
        P("tensor"),
    )
    return jax.shard_map(body, mesh=mesh, in_specs=in_specs, out_specs=out_specs, check_vma=False)
```

time: 1080 us -> 318 us (0.29)
  waiting for transfers between devices: 344 us -> 0 us
  blocking collectives: 307 us -> 0 us
  Pallas kernels: 0 us -> 276 us
  matrix products: 164 us -> 2.14 us
  local copies, waits for them, and re-layouts: 123 us -> 29.7 us
  other arithmetic: 83 us -> 4.38 us
  starting transfers between devices: 38.8 us -> 0 us
  between operations: 15.5 us -> 0.88 us
    psum x1 -> x0, blocking collectives: 285 us -> none  [return_rows(): summed = lax.psum(partial_value, 'tensor').astype(jnp.bfloat16)]
    pallas_call x0 -> x3, Pallas kernels: none -> 276 us  [the longest x1 115 us: run_experts(): pl.pallas_call(functools.partial(expert_kernel, n, hp), out_shape=(shape(...]
    all_to_all x8 -> x0, waiting for transfers between devices: 231 us -> none  [the longest x2 132 us: send_rows(): lax.all_to_all(buffer, 'dp', split_axis=0, concat_axis=1, tiled=True)]
    dot_general x33 -> x1, matrix products: 164 us -> 2.14 us  [body(): lax.dot_general(w_router, normed_two, (((0,), (1,)), ((), ())), preferred...]
    psum x2 -> x0, waiting for transfers between devices: 112 us -> none  [tensor_total(): return lax.psum(partial_value, 'tensor')]
    unnamed x3 -> x0, other arithmetic: 53.7 us -> none
    convert_element_type x9 -> x0, local copies, waits for them, and re-layouts: 53.5 us -> none  [the longest x2 48.5 us: return_rows(): summed = lax.psum(partial_value, 'tensor').astype(jnp.bfloat16)]
    all_to_all x8 -> x0, starting transfers between devices: 38.7 us -> none  [the longest x4 19 us: sent_and_summed(): lax.all_to_all(blocks, axis, split_axis=0, concat_axis=0, tiled=True)]
  transfers between devices with their start and end apart: 10 -> 0, of which waited for: 8 -> 0; matrix products, arithmetic and copies ran while one was open for 17% -> 0% of each run, Pallas kernels for 0% -> 0%
where the time goes in v1:
time: 318 us; the launch traced here: 313 us
  Pallas kernels  276 us (87%)
  local copies, waits for them, and re-layouts  29.7 us (9%)
  other arithmetic  4.38 us (1%)
    pallas_call x1, Pallas kernels, run_experts(): pl.pallas_call(functools.partial(expert_kernel, n, hp), out_shape=(shape(...  115 us
    pallas_call x1, Pallas kernels, run_back(): pl.pallas_call(functools.partial(back_kernel, n), out_shape=(shape((rows,...  98.2 us
    pallas_call x1, Pallas kernels, run_front(): pl.pallas_call(functools.partial(front_kernel, n, hp), out_shape=(shape((...  62.9 us
    unnamed x37, local copies, waits for them, and re-layouts  8.52 us

profile of v1, /device:TPU:0, one launch (start us, length us, event | category | flops | bytes accessed | tf_op | source)
XLA Modules:
  0.0 313.2 jit_solution(12329189318665822557)
XLA Ops:
  0.7 0.8 select_reduce_fusion
  1.5 0.8 add_select_fusion
  2.3 0.8 and_select_fusion
  3.0 0.7 pad_add_fusion
  4.8 0.6 pad.24.clone.place_ref
  5.5 2.0 reshape.81
  7.5 1.4 pad.25
  8.9 2.0 reshape.83
  10.9 1.4 pad.26
  12.3 0.9 copy.57.query_w_ref
  13.2 0.9 copy.58.key_w_ref
  14.1 0.9 copy.59.value_w_ref
  16.2 62.9 %front.1 = (bf16[1248,768]{1,0:T(8,128)(2,1)}, bf16[1248,192]{1,0:T(8,128)(2,1)}, bf16[1248,192]{1,0:T(8,128)(2,1)}, bf16[1248,192]{1,0:T(8,128)(2,1)}, bf16[124...) custom-call(bf16[1248,768]{1,0:T(8,128)(2,1)} %bitcast.24, ...), custom_call_target="tpu_custom_call" | custom-call | tf_op jit(solution)/shard_map/front/pallas_call | solution.py:403
  79.8 2.1 select_reduce_fusion.1
  82.0 0.6 pad.27.gate_ref
  82.7 114.9 %experts.1 = (bf16[8,352,384]{2,1,0:T(8,128)(2,1)}, bf16[8,352,384]{2,1,0:T(8,128)(2,1)}, f32[8,352]{1,0:T(8,128)}, f32[768,768]{1,0:T(8,128)}, f32[768,768]{1,0:T(8,128)}, /*index=5*/f32[8,128]{1,0:T(8,128)}) custom-call(s32[8,1248]{1,0:T(8,128)} %pad.24.clone.place_ref, f32[8,1248]{1,0:T(8,128)} %pad.27.gate_ref, ...), custom_call_target="tpu_custom_call" | custom-call | tf_op jit(solution)/shard_map/experts/pallas_call | solution.py:733
  197.5 0.8 broadcast_in_dim.60
  198.3 0.6 broadcast_in_dim.61.gate_sum_ref
  199.1 0.7 pad.28.router_ref
  199.9 98.2 %back.1 = (bf16[1248,768]{1,0:T(8,128)(2,1)}, bf16[1248,768]{1,0:T(8,128)(2,1)}, f32[96,768]{1,0:T(8,128)}, f32[96,128]{1,0:T(8,128)}) custom-call(bf16[2816,384]{1,0:T(8,128)(2,1)} %bitcast.32, bf16[2816,384]{1,0:T(8,128)(2,1)} %bitcast.33, f32[8,2816]{1,0:T(8,128)} %broadcast_in_dim.61.gate_sum_ref, s32[1248,6]{1,0:T(8,128)} %bitcast.29, ...), custom_call_target="tpu_custom_call" | custom-call | tf_op jit(solution)/shard_map/back/pallas_call | solution.py:1095
  298.1 1.6 slice.60
  299.7 1.7 reshape.88
  301.5 1.6 slice.61
  303.1 1.7 reshape.90
  304.9 0.8 slice_bitcast_fusion.2
  305.7 0.7 copy.65
  306.4 0.7 copy.66
  307.1 0.7 slice_reduce_fusion.2
  308.1 1.2 convert_multiply_fusion
  309.3 1.4 copy.70
  310.7 1.1 copy-done.1
  311.8 1.4 copy.71
  (45 shorter events, 3.4 us)
Async XLA Ops:
  4.2 3.3 %copy-start = (s32[6,208,6]{2,1,0:T(8,128)}, s32[6,208,6]{2,1,0:T(8,128)S(1)}, u32[]{:S(2)}) copy-start(s32[6,208,6]{2,1,0:T(8,128)S(1)} %pad.23) | copy-start | bytes 89860
  10.9 1.4 copy-start.3
  10.9 2.3 copy-start.4
  10.9 3.2 %copy-start.7 = (bf16[768,192]{0,1:T(8,128)(2,1)S(1)}, bf16[768,192]{0,1:T(8,128)(2,1)}, u32[]{:S(2)}) copy-start(bf16[768,192]{0,1:T(8,128)(2,1)} %param.19) | copy-start | bytes 884740
  12.3 2.8 copy-start.9
  12.3 3.4 %copy-start.10 = (bf16[768]{0:T(1024)(128)(2,1)S(1)}, bf16[768]{0:T(1024)(128)(2,1)}, u32[]{:S(2)}) copy-start(bf16[768]{0:T(1024)(128)(2,1)} %param.21) | copy-start | bytes 4612
  16.2 63.5 %copy-start.8 = (bf16[768,8]{0,1:T(8,128)(2,1)S(1)}, bf16[768,8]{0,1:T(8,128)(2,1)}, u32[]{:S(2)}) copy-start(bf16[768,8]{0,1:T(8,128)(2,1)} %param.22) | copy-start | bytes 36868
  303.1 1.8 copy-start.5
  303.1 3.3 %copy-start.6 = (f32[96,128]{1,0:T(8,128)S(1)}, f32[96,128]{1,0:T(8,128)}, u32[]{:S(2)}) copy-start(f32[96,128]{1,0:T(8,128)} %get-tuple-element.47) | copy-start | bytes 147460
  303.1 4.7 %copy-start.11 = (f32[8,128]{1,0:T(8,128)S(1)}, f32[8,128]{1,0:T(8,128)}, u32[]{:S(2)}) copy-start(f32[8,128]{1,0:T(8,128)} %get-tuple-element.51) | copy-start | bytes 12292
  303.1 4.8 %copy-start.13 = (f32[3]{0:T(128)S(1)}, f32[3]{0:T(128)}, u32[]{:S(2)}) copy-start(f32[3]{0:T(128)} %param.28) | copy-start | bytes 40
  304.9 4.4 %copy-start.2 = (f32[768,768]{1,0:T(8,128)S(1)}, f32[768,768]{1,0:T(8,128)}, u32[]{:S(2)}) copy-start(f32[768,768]{1,0:T(8,128)} %get-tuple-element.49) | copy-start | bytes 7077892
  307.9 2.8 copy-start.12
  309.3 2.5 copy-start.1

commit v2 on v1

--- a/solution.py
+++ b/solution.py
@@ -429,6 +429,10 @@
     )(tokens, upstream, place, *gains, *weights)
 
 
+def in_turn(i, near):
+    return jnp.where(i < 2 * near, i // 2 + (i % 2) * near, i)
+
+
 def expert_kernel(
     n,
     hp,
@@ -439,7 +443,8 @@
     second_ref,
     peak_ref,
     upstream_hbm,
-    answer_ref,
+    answer_out,
+    answer_kept,
     back_ref,
     gate_sum_ref,
     grad_first_ref,
@@ -488,7 +493,7 @@
     ) = scratch[10:]
     model = normed_ref.shape[1]
     width = model // 2
-    backs = (answer_ref, back_ref)
+    near = spread.near
     greet(n, dp, t, [(t + d) % 4 for d in (1, 2, 3)])
     fetch = pltpu.make_async_copy(upstream_hbm, upstream, us)
     fetch.start()
@@ -500,30 +505,26 @@
         tile = gate_in.at[k, owner]
         return remote(tile, tile, hs.at[k], hr.at[k], (dp, mate))
 
-    def part_copy(k):
+    def part_copy(i, k):
         return remote(
-            parts.at[k % 3, :, spread.rows(1 - half)],
+            parts.at[i % 3, :, spread.rows(1 - half)],
             pair_in.at[k],
-            ps.at[k % 3],
+            ps.at[i % 3],
             pr.at[k],
             (dp, mate),
         )
 
-    def far_copy(k):
-        return remote(far_out.at[k % 3], far_in.at[k], fs.at[k % 3], fr.at[k], (dp, far))
-
-    def return_copy(k, j):
+    def far_copy(i, k):
+        return remote(far_out.at[i % 3], far_in.at[k], fs.at[i % 3], fr.at[k], (dp, far))
+
+    def return_copy(k):
         return remote(
-            final.at[j, k],
-            backs[j].at[k, spread.rows(half)],
-            rs.at[j, k],
-            rr.at[j, k],
-            spread.peer(k),
+            final.at[k], back_ref.at[k, spread.rows(half)], rs.at[k], rr.at[k], spread.peer(k)
         )
 
-    def mate_copy(k, j, owner):
-        rows = backs[j].at[k, spread.rows(owner)]
-        return remote(rows, rows, ms.at[j, k], mr.at[j, k], (dp, mate))
+    def mate_copy(k, owner):
+        rows = back_ref.at[k, spread.rows(owner)]
+        return remote(rows, rows, ms.at[k], mr.at[k], (dp, mate))
 
     def sum_copy(k):
         return remote(sum_out.at[k], sum_in.at[k], ks.at[k], kr.at[k], spread.peer(k))
@@ -545,7 +546,8 @@
 
     await_greetings(n, (1, 2, 3))
 
-    def dispatch(k):
+    def dispatch(i):
+        k = (i + near) % n
         is_first, is_second = spread.send(k, normed_ref)
         gate = jnp.sum(
             jnp.where(is_first, gate_ref[0:1, :], 0.0) + jnp.where(is_second, gate_ref[1:2, :], 0.0),
@@ -562,12 +564,11 @@
         def _():
             gate_out[k] = tile
             gate_copy(k).start()
-            peak_copy(k).start()
 
     loop(dispatch)
     fetch.wait()
 
-    def chunk(k):
+    def chunk(i, k):
         gate = jnp.concatenate(
             [row_to_column(gate_in[k, 0, 0:1, :]), row_to_column(gate_in[k, 1, 0:1, :])], axis=0
         )
@@ -579,12 +580,12 @@
         hidden = (pre * share).astype(LOW)
         hidden_all[k] = hidden
         answer = dot_plain(hidden, second_ref[...])
-        parts[k % 3, 0] = answer.astype(LOW)
+        parts[i % 3, 0] = answer.astype(LOW)
         gate_sum = jnp.sum(answer * gradient, axis=1, keepdims=True)
         upstream[k] = answer_grad
         pre_grad = (dot_last(answer_grad, second_ref[...]) * slope).astype(LOW)
         pre_grad_all[k] = pre_grad
-        parts[k % 3, 1] = dot_last(pre_grad, first_ref[...]).astype(LOW)
+        parts[i % 3, 1] = dot_last(pre_grad, first_ref[...]).astype(LOW)
         tile = jnp.broadcast_to(column_to_row(gate_sum), (8, 2 * hp))
 
         @pl.when(k == 0)
@@ -595,15 +596,16 @@
         def _():
             sum_out[k] = tile
             sum_copy(k).start()
+            peak_copy(k).start()
 
     def step(i):
         @pl.when(i < n)
         def _():
-            spread.first_hop(i)
+            spread.first_hop(in_turn(i, near))
 
         @pl.when((i >= 1) & (i < n + 1))
         def _():
-            k = i - 1
+            k = in_turn(i - 1, near)
             spread.second_hop(k)
 
             @pl.when(k > 0)
@@ -614,48 +616,53 @@
 
         @pl.when((i >= 2) & (i < n + 2))
         def _():
-            k = i - 2
+            k = in_turn(i - 2, near)
             spread.last_hop(k)
             gate_pair_copy(k, 1 - half).wait_recv()
 
-            @pl.when(k >= 3)
+            @pl.when(i >= 5)
             def _():
-                part_copy(k - 3).wait_send()
-
-            chunk(k)
-            part_copy(k).start()
+                part_copy(i - 5, in_turn(i - 5, near)).wait_send()
+
+            chunk(i - 2, k)
+            part_copy(i - 2, k).start()
 
         @pl.when((i >= 3) & (i < n + 3))
         def _():
-            k = i - 3
-            part_copy(k).wait_recv()
-
-            @pl.when(k >= 3)
+            k = in_turn(i - 3, near)
+            part_copy(i - 3, k).wait_recv()
+
+            @pl.when(i >= 6)
             def _():
-                far_copy(k - 3).wait_send()
-
-            for j in range(2):
-                whole = parts[k % 3, j, spread.rows(half), :].astype(FULL) + pair_in[k, j].astype(FULL)
+                far_copy(i - 6, in_turn(i - 6, near)).wait_send()
+
+            for j in (1, 0):
+                whole = parts[i % 3, j, spread.rows(half), :].astype(FULL) + pair_in[k, j].astype(FULL)
                 low, high = whole[:, :width], whole[:, width:]
-                kept[k % 3, j] = jnp.where(side == 0, low, high)
-                far_out[k % 3, j] = jnp.where(side == 0, high, low).astype(LOW)
-            far_copy(k).start()
+                stays = jnp.where(side == 0, low, high)
+                goes = jnp.where(side == 0, high, low).astype(LOW)
+                if j:
+                    kept[i % 3] = stays
+                    far_out[i % 3] = goes
+                    far_copy(i - 3, k).start()
+                else:
+                    answer_kept[k] = stays
+                    answer_out[k] = goes
 
         @pl.when(i >= 4)
         def _():
-            k = i - 4
-            far_copy(k).wait_recv()
-            for j in range(2):
-                rows = (kept[k % 3, j] + far_in[k, j].astype(FULL)).astype(LOW)
-
-                @pl.when(k == 0)
-                def _():
-                    backs[j][0, spread.rows(half), :] = rows
-
-                @pl.when(k > 0)
-                def _():
-                    final[j, k] = rows
-                    return_copy(k, j).start()
+            k = in_turn(i - 4, near)
+            far_copy(i - 4, k).wait_recv()
+            rows = (kept[(i - 4) % 3] + far_in[k].astype(FULL)).astype(LOW)
+
+            @pl.when(k == 0)
+            def _():
+                back_ref[0, spread.rows(half), :] = rows
+
+            @pl.when(k > 0)
+            def _():
+                final[k] = rows
+                return_copy(k).start()
 
     loop(step, 0, n + 4)
 
@@ -672,15 +679,7 @@
 
     peaks[0] = peak_ref[...]
 
-    def collect(k):
-        for j in (1, 0):
-
-            @pl.when(k > 0)
-            def _():
-                return_copy(k, j).wait_recv()
-
-            mate_copy(k, j, half).start()
-
+    def collect_sums(k):
         @pl.when(k > 0)
         def _():
             peak_copy(k).wait_recv()
@@ -688,36 +687,43 @@
 
         sums[t, pl.ds(k, 1), :] = sum_in[k, 0:1, :]
 
-    loop(collect)
+    loop(collect_sums)
     for d in (1, 2, 3):
         share_copy(d, t).start()
     top_ref[...] = jnp.max(peaks[...], axis=0)
+
+    def collect(i):
+        k = in_turn(i, near)
+
+        @pl.when(k > 0)
+        def _():
+            return_copy(k).wait_recv()
+
+        mate_copy(k, half).start()
+
+    loop(collect)
     for d in (1, 2, 3):
         share_copy(d, (t + 4 - d) % 4).wait_recv()
     gate_sum_ref[...] = (sums[0] + sums[1]) + (sums[2] + sums[3])
 
-    def finish(k):
-        for j in range(2):
-            mate_copy(k, j, 1 - half).wait_recv()
-            mate_copy(k, j, half).wait_send()
-
-            @pl.when(k > 0)
-            def _():
-                return_copy(k, j).wait_send()
-
+    def finish(i):
+        k = in_turn(i, near)
+        mate_copy(k, 1 - half).wait_recv()
+        mate_copy(k, half).wait_send()
         spread.sent(k)
         gate_pair_copy(k, half).wait_send()
 
         @pl.when(k > 0)
         def _():
+            return_copy(k).wait_send()
             gate_copy(k).wait_send()
             sum_copy(k).wait_send()
             peak_copy(k).wait_send()
 
-        @pl.when(k >= n - 3)
-        def _():
-            part_copy(k).wait_send()
-            far_copy(k).wait_send()
+        @pl.when(i >= n - 3)
+        def _():
+            part_copy(i, k).wait_send()
+            far_copy(i, k).wait_send()
 
     loop(finish)
     for d in (1, 2, 3):
@@ -733,7 +739,8 @@
     return pl.pallas_call(
         functools.partial(expert_kernel, n, hp),
         out_shape=(
-            shape((n, 2 * hp, width), LOW),
+            shape((n, hp, width), LOW),
+            shape((n, hp, width), FULL),
             shape((n, 2 * hp, width), LOW),
             shape((n, 2 * hp), FULL),
             shape((model, hidden), FULL),
@@ -741,7 +748,7 @@
             shape(peak.shape, FULL),
         ),
         in_specs=[vmem] * 6 + [pl.BlockSpec(memory_space=pl.ANY)],
-        out_specs=[vmem] * 6,
+        out_specs=[vmem] * 7,
         scratch_shapes=[
             *Spread.scratch(n, hp, width),
             VMEM((n, 2 * hp, model), LOW),
@@ -751,10 +758,10 @@
             VMEM((n, 2 * hp, hidden), LOW),
             VMEM((3, 2, 2 * hp, model), LOW),
             VMEM((n, 2, hp, model), LOW),
-            VMEM((3, 2, hp, width), FULL),
-            VMEM((3, 2, hp, width), LOW),
-            VMEM((n, 2, hp, width), LOW),
-            VMEM((2, n, hp, width), LOW),
+            VMEM((3, hp, width), FULL),
+            VMEM((3, hp, width), LOW),
+            VMEM((n, hp, width), LOW),
+            VMEM((n, hp, width), LOW),
             VMEM((n, 8, hp), FULL),
             VMEM((n, 2, 8, hp), FULL),
             VMEM((n, 8, 2 * hp), FULL),
@@ -762,7 +769,7 @@
             VMEM((4, n, 2 * hp), FULL),
             VMEM((n, *peak.shape), FULL),
             pltpu.SemaphoreType.DMA,
-            dma(3), dma(n), dma(3), dma(n), dma(2, n), dma(2, n), dma(2, n), dma(2, n),
+            dma(3), dma(n), dma(3), dma(n), dma(n), dma(n), dma(n), dma(n),
             dma(n), dma(n), dma(n), dma(n), dma(n), dma(n), dma(n), dma(n), dma(3), dma(3),
         ],
         compiler_params=pltpu.CompilerParams(
@@ -774,31 +781,34 @@
 
 def back_kernel(
     n,
-    answer_ref,
+    hp,
     back_ref,
     gate_sum_ref,
     index_ref,
     residual_ref,
     upstream_ref,
-    normed_one_ref,
-    query_ref,
-    key_ref,
-    value_ref,
-    mixed_ref,
-    tokens_ref,
     gain_one_ref,
     gain_two_ref,
-    query_w_ref,
-    key_w_ref,
-    value_w_ref,
     output_w_ref,
     router_ref,
-    block_ref,
-    grad_tokens_ref,
-    weights_ref,
-    small_ref,
-    *scratch,
+    answer_out,
+    *refs,
 ):
+    later, outs, scratch = refs[:10], refs[10:15], refs[15:]
+    block_ref, grad_tokens_ref, weights_ref, small_ref, gain_ref = outs
+    held, scratch = scratch[:10], scratch[10:]
+    (
+        answer_kept,
+        normed_one_ref,
+        query_ref,
+        key_ref,
+        value_ref,
+        mixed_ref,
+        tokens_ref,
+        query_w_ref,
+        key_w_ref,
+        value_w_ref,
+    ) = held
     dp, t, half, side, mate, far = places()
     (
         moe_mine,
@@ -811,14 +821,22 @@
         key_grad,
         value_grad,
         gain_two_sum,
+        gain_two_in,
         gain_one_sum,
         gain_one_all,
+        gain_rows,
         router_sum,
         router_in,
-        gain_two_in,
         totals,
+        totals_two,
         pieces,
         pieces_in,
+        small_pieces,
+        small_in,
+        answer_far,
+        answer_final,
+        answers,
+        hs,
         as_,
         ar,
         bs,
@@ -835,14 +853,31 @@
         lr,
         os_,
         or_,
-    ) = scratch[:34]
-    total = Total(*scratch[34:])
+        vs,
+        vr,
+        ds,
+        dr,
+        es,
+        er,
+        fs,
+        fr,
+        ks,
+        kr,
+    ) = scratch[:52]
+    total = Total(*scratch[52:])
     heads = query_w_ref.shape[1] // HD
-    model = tokens_ref.shape[1]
+    model = upstream_ref.shape[1]
     width = model // 2
-    slots = answer_ref.shape[0]
+    slots = back_ref.shape[0]
     piece = pieces.shape[1]
+    near = near_count(n)
     greet(n, dp, t, [(t + d) % 4 for d in (1, 2, 3)])
+    fetches = [pltpu.make_async_copy(a, b, hs.at[i]) for i, (a, b) in enumerate(zip(later, held))]
+    for fetch in fetches:
+        fetch.start()
+
+    def peer(k):
+        return (partner(dp, k, n), t)
 
     def moe_copy(j):
         return remote(moe_mine.at[j], moe_other.at[j], as_.at[j], ar.at[j], (dp, far))
@@ -867,6 +902,9 @@
             gain_one_all.at[owner], gain_one_all.at[owner], gs.at[d - 1], gr.at[d - 1], (dp, (t + d) % 4)
         )
 
+    def gain_row_copy(k):
+        return remote(gain_rows.at[0], gain_rows.at[k], ks.at[k], kr.at[k], peer(k))
+
     def router_copy():
         return remote(router_sum, router_in, os_.at[0], or_.at[0], (dp, mate))
 
@@ -874,11 +912,24 @@
         return remote(gain_two_sum, gain_two_in, os_.at[1], or_.at[1], (dp, mate))
 
     def piece_copy(k):
-        return remote(
-            pieces.at[k], pieces_in.at[k], ws.at[k], wr.at[k], (partner(dp, k, n), t)
-        )
-
-    def loop(body, first, last):
+        return remote(pieces.at[k], pieces_in.at[k], ws.at[k], wr.at[k], peer(k))
+
+    def small_copy(k):
+        return remote(small_pieces.at[k], small_in.at[k], vs.at[k], vr.at[k], peer(k))
+
+    def answer_rows(k, owner):
+        return answers.at[pl.ds(pl.multiple_of((2 * k + owner) * hp, hp), hp)]
+
+    def answer_side_copy(k):
+        return remote(answer_out.at[k], answer_far.at[k], ds.at[k], dr.at[k], (dp, far))
+
+    def answer_copy(k):
+        return remote(answer_final.at[k], answer_rows(k, half), es.at[k], er.at[k], peer(k))
+
+    def answer_pair_copy(k, owner):
+        return remote(answer_rows(k, owner), answer_rows(k, owner), fs.at[k], fr.at[k], (dp, mate))
+
+    def loop(body, first=0, last=n):
         def one(k, carry):
             body(k)
             return carry
@@ -900,14 +951,19 @@
     gain_two_sum[...] = jnp.zeros_like(gain_two_sum)
     gain_one_sum[...] = jnp.zeros_like(gain_one_sum)
     router_sum[...] = jnp.zeros_like(router_sum)
-    await_greetings(n, (1, 2, 3))
 
     def combine(j):
         first, second = hots(image_rows(2 * j + half))
         moe_mine[j] = dot_plain(as_low(first | second), back_ref[...]).astype(LOW)
+
+        @pl.when(j == 0)
+        def _():
+            await_greetings(n, (1, 2, 3))
+
         moe_copy(j).start()
 
     loop(combine, 0, 3)
+    loop(lambda k: answer_side_copy((k + near) % n).start())
 
     def gates_of(rows, normed):
         logits = dot_plain(normed, router_ref[...])
@@ -947,6 +1003,8 @@
     loop(moe_back, 0, 3)
     router_copy().start()
     gain_two_copy().start()
+    for fetch in fetches:
+        fetch.wait()
 
     def image_back(image):
         rows = image_rows(image)
@@ -964,12 +1022,134 @@
             key_parts.append(dot_first(score_grad, queries[:, cols]) * HD**-0.5)
         grads = [jnp.concatenate(p, axis=1).astype(LOW) for p in (query_parts, key_parts, value_parts)]
         query_grad[rows, :], key_grad[rows, :], value_grad[rows, :] = grads
-        part = dot_last(grads[0], query_w_ref[...])
-        part = part + dot_last(grads[1], key_w_ref[...])
-        part = part + dot_last(grads[2], value_w_ref[...])
+
+    def answer_turn(k):
+        answer_side_copy(k).wait_recv()
+        rows = (answer_kept[k] + answer_far[k].astype(FULL)).astype(LOW)
+
+        @pl.when(k == 0)
+        def _():
+            answer_rows(0, half)[...] = rows
+
+        @pl.when(k > 0)
+        def _():
+            answer_final[k] = rows
+            answer_copy(k).start()
+
+    per_image = -(-n // 4)
+
+    def attention_back(i):
+        j = i % 3
+
+        @pl.when(i >= 3)
+        def _():
+            attention_copy(j, 1 - half).wait_recv()
+
+        image_back(2 * j + jnp.where(i < 3, half, 1 - half))
+
+        def turn(m):
+            @pl.when(m < n)
+            def _():
+                answer_turn((m + near) % n)
+
+        @pl.when(i >= 2)
+        def _():
+            loop(turn, (i - 2) * per_image, (i - 1) * per_image)
+
+    loop(attention_back, 0, 6)
+
+    normed_one = normed_one_ref[...]
+    totals[:, : 3 * query_grad.shape[1]] = jnp.concatenate(
+        [
+            dot_first(normed_one, query_grad[...]),
+            dot_first(normed_one, key_grad[...]),
+            dot_first(normed_one, value_grad[...]),
+        ],
+        axis=1,
+    )
+
+    def my_piece(source, k):
+        at = partner(dp, k, n) * piece
+        grain = math.gcd(piece, 8)
+        span = -(-(piece + 8 - grain) // 8) * 8
+        taken = source[pl.ds(pl.multiple_of(at // 8 * 8, 8), span), :]
+        rows = taken[:piece]
+        for shift in range(grain, 8, grain):
+            rows = jnp.where(at % 8 == shift, taken[shift : shift + piece], rows)
+        return rows.astype(LOW)
+
+    def send_piece(i):
+        k = (i + near) % n
+        pieces[k] = my_piece(totals, k)
+
+        @pl.when(k > 0)
+        def _():
+            piece_copy(k).start()
+
+    loop(send_piece)
+
+    def grad_part(image):
+        rows = image_rows(image)
+        part = dot_last(query_grad[rows, :], query_w_ref[...])
+        part = part + dot_last(key_grad[rows, :], key_w_ref[...])
+        part = part + dot_last(value_grad[rows, :], value_w_ref[...])
         unit, _ = normalized(tokens_ref[rows, :].astype(FULL))
         gain_one_sum[...] += jnp.sum((part * unit).reshape(PIECE // 8, 8, model), axis=0)
         return part
+
+    def sum_images(j):
+        total.give(j, grad_part(2 * j + 1 - half))
+        total.take(j, grad_part(2 * j + half))
+
+    loop(sum_images, 0, 3)
+    gain_one_all[t] = gain_one_sum[...]
+    for d in (1, 2, 3):
+        gain_copy(d, t).start()
+
+    router_copy().wait_recv()
+    gain_two_copy().wait_recv()
+    lanes = lax.broadcasted_iota(jnp.int32, (model, 128), 1)
+    row = jnp.sum(gain_two_sum[...] + gain_two_in[...], axis=0, keepdims=True)
+    column = jnp.concatenate(
+        [row_to_column(row[:, i : i + 256]) for i in range(0, model, 256)], axis=0
+    )
+    totals_two[...] = jnp.concatenate(
+        [
+            router_sum[...] + router_in[...] + jnp.where(lanes == 127, column, 0.0),
+            dot_first(attention_grad[...], mixed_ref[...]),
+        ],
+        axis=1,
+    )
+
+    def send_small(i):
+        k = (i + near) % n
+        small_pieces[k] = my_piece(totals_two, k)
+
+        @pl.when(k > 0)
+        def _():
+            small_copy(k).start()
+
+    loop(send_small)
+
+    def answers_here(i):
+        k = in_turn(i, near)
+
+        @pl.when(k > 0)
+        def _():
+            answer_copy(k).wait_recv()
+
+        answer_pair_copy(k, half).start()
+
+    loop(answers_here)
+    for d in (1, 2, 3):
+        gain_copy(d, (t + 4 - d) % 4).wait_recv()
+    gain_rows[0] = (gain_one_all[0] + gain_one_all[1]) + (gain_one_all[2] + gain_one_all[3])
+
+    def send_gain(k):
+        gain_row_copy(k).start()
+
+    loop(send_gain, 1)
+    loop(lambda k: answer_pair_copy(k, 1 - half).wait_recv())
 
     def block_rows(j):
         rows = image_rows(2 * j + half)
@@ -977,68 +1157,13 @@
         unit, _ = normalized(residual)
         gate_one, gate_two, _, _ = gates_of(rows, (unit * gain_two_ref[...]).astype(LOW))
         first, second = hots(rows)
-        from_first = dot_plain(as_low(first), answer_ref[...])
-        from_second = dot_plain(as_low(second), answer_ref[...])
+        from_first = dot_plain(as_low(first), answers[...])
+        from_second = dot_plain(as_low(second), answers[...])
         mine = jnp.where(side == 0, residual[:, :width], residual[:, width:])
         block_mine[j] = (mine + (gate_one * from_first + gate_two * from_second)).astype(LOW)
         block_copy(j).start()
 
-    def attention_back(j):
-        attention_copy(j, 1 - half).wait_recv()
-        total.give(j, image_back(2 * j + 1 - half))
-        total.take(j, image_back(2 * j + half))
-        block_rows(j)
-
-    loop(attention_back, 0, 3)
-
-    gain_one_all[t] = gain_one_sum[...]
-    for d in (1, 2, 3):
-        gain_copy(d, t).start()
-    normed_one = normed_one_ref[...]
-    totals[:, :model] = jnp.concatenate(
-        [
-            dot_first(normed_one, query_grad[...]),
-            dot_first(normed_one, key_grad[...]),
-            dot_first(normed_one, value_grad[...]),
-            dot_first(attention_grad[...], mixed_ref[...]),
-        ],
-        axis=1,
-    )
-    router_copy().wait_recv()
-    gain_two_copy().wait_recv()
-    for d in (1, 2, 3):
-        gain_copy(d, (t + 4 - d) % 4).wait_recv()
-    lanes = lax.broadcasted_iota(jnp.int32, (model, 128), 1)
-
-    def column_of(eight):
-        row = jnp.sum(eight, axis=0, keepdims=True)
-        return jnp.concatenate(
-            [row_to_column(row[:, i : i + 256]) for i in range(0, model, 256)], axis=0
-        )
-
-    gain_one_total = (gain_one_all[0] + gain_one_all[1]) + (gain_one_all[2] + gain_one_all[3])
-    totals[:, model:] = (
-        router_sum[...]
-        + router_in[...]
-        + jnp.where(lanes == 126, column_of(gain_one_total), 0.0)
-        + jnp.where(lanes == 127, column_of(gain_two_sum[...] + gain_two_in[...]), 0.0)
-    )
-
-    def send_piece(k):
-        at = partner(dp, k, n) * piece
-        grain = math.gcd(piece, 8)
-        span = -(-(piece + 8 - grain) // 8) * 8
-        taken = totals[pl.ds(pl.multiple_of(at // 8 * 8, 8), span), :]
-        rows = taken[:piece]
-        for shift in range(grain, 8, grain):
-            rows = jnp.where(at % 8 == shift, taken[shift : shift + piece], rows)
-        pieces[k] = rows.astype(LOW)
-
-        @pl.when(k > 0)
-        def _():
-            piece_copy(k).start()
-
-    loop(send_piece, 0, n)
+    loop(block_rows, 0, 3)
 
     def tokens_back(j):
         rows = image_rows(2 * j + half)
@@ -1047,20 +1172,27 @@
         grad = normalized_back(normed_grad * gain_one_ref[...], unit, factor)
         grad_tokens_ref[rows, :] = (residual_grad[j] + grad).astype(LOW)
         tokens_copy(j, half).start()
+
+    loop(tokens_back, 0, 3)
+
+    def block_back(j):
         block_copy(j).wait_recv()
-        block_ref[rows, :] = both_sides(block_mine[j], block_other[j])
+        block_ref[image_rows(2 * j + half), :] = both_sides(block_mine[j], block_other[j])
         block_pair_copy(j, half).start()
 
-    loop(tokens_back, 0, 3)
+    loop(block_back, 0, 3)
     pieces_in[0] = pieces[0]
+    small_in[0] = small_pieces[0]
 
     def arrive(k):
         piece_copy(k).wait_recv()
-
-    loop(arrive, 1, n)
-    whole = jnp.sum(pieces_in[...].astype(FULL), axis=0)
-    weights_ref[...] = whole[:, :model]
-    small_ref[...] = whole[:, model:]
+        small_copy(k).wait_recv()
+        gain_row_copy(k).wait_recv()
+
+    loop(arrive, 1)
+    weights_ref[...] = jnp.sum(pieces_in[...].astype(FULL), axis=0)
+    small_ref[...] = jnp.sum(small_in[...].astype(FULL), axis=0)
+    gain_ref[...] = jnp.sum(gain_rows[...], axis=0)
 
     for j in range(3):
         moe_copy(j).wait_send()
@@ -1076,15 +1208,23 @@
     gain_two_copy().wait_send()
 
     def left(k):
-        piece_copy(k).wait_send()
-
-    loop(left, 1, n)
-
-
-def run_back(n, *operands):
-    tokens = operands[11]
-    rows, model = tokens.shape
-    heads_width = operands[7].shape[1]
+        answer_side_copy(k).wait_send()
+        answer_pair_copy(k, half).wait_send()
+
+        @pl.when(k > 0)
+        def _():
+            piece_copy(k).wait_send()
+            small_copy(k).wait_send()
+            gain_row_copy(k).wait_send()
+            answer_copy(k).wait_send()
+
+    loop(left)
+
+
+def run_back(n, hp, first, later):
+    upstream = first[4]
+    rows, model = upstream.shape
+    heads_width = later[2].shape[1]
     width = model // 2
     piece = model // n
     vmem = pl.BlockSpec(memory_space=VMEM)
@@ -1092,38 +1232,50 @@
     slim = VMEM((3, PIECE, width), LOW)
     heads = VMEM((rows, heads_width), LOW)
     eight = VMEM((8, model), FULL)
+    wide, narrow = 3 * heads_width, heads_width + 128
+    quarter = VMEM((n, hp, width), LOW)
+    three, many = dma(3), dma(n)
     return pl.pallas_call(
-        functools.partial(back_kernel, n),
+        functools.partial(back_kernel, n, hp),
         out_shape=(
             shape((rows, model), LOW),
             shape((rows, model), LOW),
-            shape((piece, model), FULL),
-            shape((piece, 128), FULL),
+            shape((piece, wide), FULL),
+            shape((piece, narrow), FULL),
+            shape((8, model), FULL),
         ),
-        in_specs=[vmem] * len(operands),
-        out_specs=[vmem] * 4,
+        in_specs=[vmem] * len(first) + [pl.BlockSpec(memory_space=pl.ANY)] * len(later),
+        out_specs=[vmem] * 5,
         scratch_shapes=[
+            *[VMEM(a.shape, a.dtype) for a in later],
             slim, slim, slim, slim,
             VMEM((rows, model), LOW),
             VMEM((3, PIECE, model), FULL),
             heads, heads, heads,
-            eight, eight,
+            eight, eight, eight,
             VMEM((4, 8, model), FULL),
+            VMEM((n, 8, model), FULL),
             VMEM((model, 128), FULL),
             VMEM((model, 128), FULL),
-            eight,
-            VMEM((model, model + 128), FULL),
-            VMEM((n, piece, model + 128), LOW),
-            VMEM((n, piece, model + 128), LOW),
-            dma(3), dma(3), dma(3), dma(3), dma(3), dma(3), dma(3), dma(3), dma(3), dma(3),
-            dma(n), dma(n), dma(3), dma(3), dma(2), dma(2),
+            VMEM((model, wide), FULL),
+            VMEM((model, narrow), FULL),
+            VMEM((n, piece, wide), LOW),
+            VMEM((n, piece, wide), LOW),
+            VMEM((n, piece, narrow), LOW),
+            VMEM((n, piece, narrow), LOW),
+            quarter, quarter,
+            VMEM((n * 2 * hp, width), LOW),
+            dma(len(later)),
+            three, three, three, three, three, three, three, three, three, three,
+            many, many, three, three, dma(2), dma(2),
+            many, many, many, many, many, many, many, many, many, many,
             *Total.scratch(model),
         ],
         compiler_params=pltpu.CompilerParams(
             collective_id=2, has_side_effects=True, vmem_limit_bytes=VMEM_LIMIT
         ),
         name="back",
-    )(*operands)
+    )(*first, *later)
 
 
 def body(
@@ -1190,41 +1342,51 @@
         [jnp.sum(jnp.where(expert_ids[:, None] == route_rows[k], logit_rows, 0.0), axis=0) for k in (0, 1)]
     )
     gate_rows = jnp.pad(jax.nn.softmax(chosen, axis=0), ((0, 6), (0, 0)))
-    answers, back, gate_sums, grad_first, grad_second, top = run_experts(
+    answer_out, answer_kept, back, gate_sums, grad_first, grad_second, top = run_experts(
         n, hp, place_rows, gate_rows, normed_two, expert_in[0], expert_out[0], peak, spread
     )
     router_wide = jnp.pad(w_router, ((0, 0), (0, 128 - n)))
-    block_rows, token_rows, weight_grads, small = run_back(
+    block_rows, token_rows, weight_grads, small, gain_rows = run_back(
         n,
-        answers.reshape(n * 2 * hp, -1),
-        back.reshape(n * 2 * hp, -1),
-        jnp.broadcast_to(gate_sums.reshape(1, -1), (8, n * 2 * hp)),
-        index,
-        residual,
-        upstream,
-        normed_one,
-        query,
-        key,
-        value,
-        mixed,
-        tokens_in,
-        gain_one,
-        gain_two,
-        *weights,
-        router_wide,
+        hp,
+        (
+            back.reshape(n * 2 * hp, -1),
+            jnp.broadcast_to(gate_sums.reshape(1, -1), (8, n * 2 * hp)),
+            index,
+            residual,
+            upstream,
+            gain_one,
+            gain_two,
+            w_output,
+            router_wide,
+            answer_out,
+        ),
+        (
+            answer_kept,
+            normed_one,
+            query,
+            key,
+            value,
+            mixed,
+            tokens_in,
+            w_query,
+            w_key,
+            w_value,
+        ),
     )
     head_max = top[:heads_here, 0]
     column_factor = jnp.repeat(jnp.sqrt(jnp.minimum(1.0, threshold / head_max)), HD)[None, :]
     wide = w_query.shape[1]
+    piece = model // n
     return (
         unpadded(block_rows),
         unpadded(token_rows),
-        small[:, 126],
+        lax.dynamic_slice_in_dim(gain_rows.sum(axis=0), dp_here * piece, piece),
         small[:, 127],
         weight_grads[:, :wide],
         weight_grads[:, wide : 2 * wide],
-        weight_grads[:, 2 * wide : 3 * wide],
-        weight_grads[:, 3 * wide :].T,
+        weight_grads[:, 2 * wide :],
+        small[:, 128:].T,
         small[:, :n],
         grad_first[None],
         grad_second[None],

time: 318 us -> 275 us (0.86); the launches traced: 313 us -> 274 us
  Pallas kernels: 276 us -> 235 us
    pallas_call x1, Pallas kernels: 115 us -> 80.5 us  [run_experts(): pl.pallas_call(functools.partial(expert_kernel, n, hp), out_shape=(shape(...]
    pallas_call x1, Pallas kernels: 98.2 us -> 91.1 us  [run_back(): pl.pallas_call(functools.partial(back_kernel, n, hp), out_shape=(shape((r...]
    unnamed x37 -> x35, local copies, waits for them, and re-layouts: 8.52 us -> 9.38 us
where the time goes in v2:
time: 275 us; the launch traced here: 274 us
  Pallas kernels  235 us (85%)
  local copies, waits for them, and re-layouts  32.3 us (12%)
  other arithmetic  4.39 us (2%)
    pallas_call x1, Pallas kernels, run_back(): pl.pallas_call(functools.partial(back_kernel, n, hp), out_shape=(shape((r...  91.1 us
    pallas_call x1, Pallas kernels, run_experts(): pl.pallas_call(functools.partial(expert_kernel, n, hp), out_shape=(shape(...  80.5 us
    pallas_call x1, Pallas kernels, run_front(): pl.pallas_call(functools.partial(front_kernel, n, hp), out_shape=(shape((...  63 us
    unnamed x35, local copies, waits for them, and re-layouts  9.38 us

profile of v2, /device:TPU:0, one launch (start us, length us, event | category | flops | bytes accessed | tf_op | source)
XLA Modules:
  0.0 274.3 jit_solution(6834240918781963305)
XLA Ops:
  0.7 0.8 select_reduce_fusion
  1.5 0.8 add_select_fusion
  2.3 0.8 and_select_fusion
  3.0 0.7 pad_add_fusion
  4.8 0.6 pad.24.clone.place_ref
  5.4 2.0 reshape.78
  7.5 1.4 pad.25
  8.9 2.0 reshape.80
  10.9 1.4 pad.26
  12.3 0.9 copy.57.query_w_ref.refs_7_
  13.2 0.9 copy.58.key_w_ref.refs_8_
  14.1 0.9 copy.59.value_w_ref.refs_9_
  16.2 63.0 %front.1 = (bf16[1248,768]{1,0:T(8,128)(2,1)}, bf16[1248,192]{1,0:T(8,128)(2,1)}, bf16[1248,192]{1,0:T(8,128)(2,1)}, bf16[1248,192]{1,0:T(8,128)(2,1)}, bf16[124...) custom-call(bf16[1248,768]{1,0:T(8,128)(2,1)} %bitcast.22, ...), custom_call_target="tpu_custom_call" | custom-call | tf_op jit(solution)/shard_map/front/pallas_call | solution.py:403
  79.2 0.6 slice_reduce_fusion
  79.9 2.1 select_reduce_fusion.1
  82.1 0.6 pad.27.gate_ref
  82.8 80.5 %experts.1 = (bf16[8,176,384]{2,1,0:T(8,128)(2,1)}, f32[8,176,384]{2,1,0:T(8,128)}, bf16[8,352,384]{2,1,0:T(8,128)(2,1)}, f32[8,352]{1,0:T(8,128)}, f32[768,768]...) custom-call(s32[8,1248]{1,0:T(8,128)} %pad.24.clone.place_ref, f32[8,1248]{1,0:T(8,128)} %pad.27.gate_ref, ...), custom_call_target="tpu_custom_call" | custom-call | tf_op jit(solution)/shard_map/experts/pallas_call | solution.py:739
  163.2 0.8 broadcast_in_dim.60
  164.0 0.6 broadcast_in_dim.61.gate_sum_ref
  164.8 0.7 pad.28.router_ref
  165.6 91.1 %back.1 = (bf16[1248,768]{1,0:T(8,128)(2,1)}, bf16[1248,768]{1,0:T(8,128)(2,1)}, f32[96,576]{1,0:T(8,128)}, f32[96,320]{1,0:T(8,128)}, f32[8,768]{1,0:T(8,128)}) custom-call(bf16[2816,384]{1,0:T(8,128)(2,1)} %bitcast.30, f32[8,2816]{1,0:T(8,128)} %broadcast_in_dim.61.gate_sum_ref, s32[1248,6]{1,0:T(8,128)} %bitcast.27, ...), custom_call_target="tpu_custom_call" | custom-call | tf_op jit(solution)/shard_map/back/pallas_call | solution.py:1238
  256.7 1.8 fusion.2
  258.5 0.7 copy.65
  259.3 1.6 slice.56
  260.9 1.7 reshape.84
  262.7 1.6 slice.57
  264.3 1.7 reshape.86
  266.1 0.7 copy.66
  267.3 0.7 slice_reduce_fusion.2
  268.3 1.2 convert_multiply_fusion
  269.5 3.4 %copy.70 = f32[1,768,768]{2,1,0:T(8,128)} copy(f32[1,768,768]{2,1,0:T(8,128)} %bitcast.29) | data formatting | bytes 4718592
  272.9 1.4 copy.71
  (46 shorter events, 3.4 us)
Async XLA Ops:
  4.2 3.3 %copy-start = (s32[6,208,6]{2,1,0:T(8,128)}, s32[6,208,6]{2,1,0:T(8,128)S(1)}, u32[]{:S(2)}) copy-start(s32[6,208,6]{2,1,0:T(8,128)S(1)} %pad.23) | copy-start | bytes 89860
  10.9 1.4 copy-start.2
  10.9 2.3 copy-start.3
  10.9 3.2 %copy-start.4 = (bf16[768,192]{0,1:T(8,128)(2,1)S(1)}, bf16[768,192]{0,1:T(8,128)(2,1)}, u32[]{:S(2)}) copy-start(bf16[768,192]{0,1:T(8,128)(2,1)} %param.19) | copy-start | bytes 884740
  12.3 2.8 %copy-start.8 = (bf16[768]{0:T(1024)(128)(2,1)S(1)}, bf16[768]{0:T(1024)(128)(2,1)}, u32[]{:S(2)}) copy-start(bf16[768]{0:T(1024)(128)(2,1)} %param.16) | copy-start | bytes 4612
  12.3 3.4 %copy-start.9 = (bf16[768]{0:T(1024)(128)(2,1)S(1)}, bf16[768]{0:T(1024)(128)(2,1)}, u32[]{:S(2)}) copy-start(bf16[768]{0:T(1024)(128)(2,1)} %param.21) | copy-start | bytes 4612
  16.2 63.6 %copy-start.6 = (bf16[768,8]{0,1:T(8,128)(2,1)S(1)}, bf16[768,8]{0,1:T(8,128)(2,1)}, u32[]{:S(2)}) copy-start(bf16[768,8]{0,1:T(8,128)(2,1)} %param.22) | copy-start | bytes 36868
  264.3 1.8 copy-start.5
  264.3 2.4 copy-start.7
  264.3 3.7 %copy-start.10 = (f32[8,128]{1,0:T(8,128)S(1)}, f32[8,128]{1,0:T(8,128)}, u32[]{:S(2)}) copy-start(f32[8,128]{1,0:T(8,128)} %get-tuple-element.55) | copy-start | bytes 12292
  264.3 3.8 %copy-start.12 = (f32[3]{0:T(128)S(1)}, f32[3]{0:T(128)}, u32[]{:S(2)}) copy-start(f32[3]{0:T(128)} %param.28) | copy-start | bytes 40
  268.2 4.7 %copy-start.11 = (f32[3]{0:T(128)}, f32[3]{0:T(128)S(1)}, u32[]{:S(2)}) copy-start(f32[3]{0:T(128)S(1)} %slice_reduce_fusion.3) | copy-start | bytes 40
  269.5 3.4 %copy-start.1 = (f32[768,768]{1,0:T(8,128)S(1)}, f32[768,768]{1,0:T(8,128)}, u32[]{:S(2)}) copy-start(f32[768,768]{1,0:T(8,128)} %get-tuple-element.54) | copy-start | bytes 7077892

commit v3 on v2

--- a/solution.py
+++ b/solution.py
@@ -170,10 +170,14 @@
         part = self.arrived.at[k, self.rows(half)]
         return remote(part, part, self.cs.at[k], self.cr.at[k], (self.dp, self.mate))
 
-    def send(self, k, rows_ref):
-        slots = lax.broadcasted_iota(jnp.int32, (self.hp, rows_ref.shape[0]), 0) + k * self.hp
+    def hot(self, k, row_count):
+        slots = lax.broadcasted_iota(jnp.int32, (self.hp, row_count), 0) + k * self.hp
         is_first = self.place[0:1, :] == slots
         is_second = self.place[1:2, :] == slots
+        return is_first, is_second
+
+    def send(self, k, rows_ref):
+        is_first, is_second = self.hot(k, rows_ref.shape[0])
         hot = jnp.where(is_first | is_second, 1.0, 0.0).astype(LOW)
 
         @pl.when(k < self.near)
@@ -281,48 +285,70 @@
         return [wide, wide, slim, slim, dma(3), dma(3), dma(3), dma(3)]
 
 
+def padded_image(rows_ref, image):
+    start = image * SEQ // 8 * 8
+    length = min(PIECE, rows_ref.shape[0] - start)
+    rows = lax.broadcasted_iota(jnp.int32, (PIECE, length), 0)
+    columns = lax.broadcasted_iota(jnp.int32, (PIECE, length), 1)
+    pick = (columns == rows + (image * SEQ - start)) & (rows < SEQ)
+    return dot_plain(jnp.where(pick, 1.0, 0.0).astype(LOW), rows_ref[start : start + length, :])
+
+
 def front_kernel(
     n,
     hp,
+    per_half,
+    capacity_ref,
+    routes_ref,
+    slot_ids_ref,
     tokens_ref,
     upstream_ref,
-    place_ref,
-    gain_one_ref,
-    gain_two_ref,
+    gains_ref,
     query_w_ref,
     key_w_ref,
     value_w_ref,
     output_w_ref,
-    normed_one_ref,
-    query_ref,
-    key_ref,
-    value_ref,
-    mixed_ref,
-    residual_ref,
-    normed_two_ref,
+    place_ref,
+    index_ref,
     peak_ref,
-    spread_ref,
-    *scratch,
+    *refs,
 ):
+    outs, spread_hbm, scratch = refs[:9], refs[9], refs[10:]
+    held, scratch = scratch[:9], scratch[9:]
+    (
+        tokens,
+        upstream,
+        normed_one,
+        query,
+        key,
+        value,
+        mixed_rows,
+        residual_rows,
+        normed_two,
+    ) = held
+    near_out, far_out, zs, zr, own, ns, nr, hs = scratch[:8]
+    total = Total(*scratch[8:])
     dp, t, half, side, mate, far = places()
-    heads = query_w_ref.shape[1] // HD
-    spread = Spread(n, hp, place_ref, *scratch[:2], spread_ref, *scratch[2:9])
-    total = Total(*scratch[9:17])
-    ns, nr = scratch[17:19]
+    heads = query_w_ref.shape[0] // HD
+    near = near_count(n)
+    width = far_out.shape[2]
+    row_count = tokens.shape[0]
     greet(n, dp, t, (mate, far))
     peak_ref[...] = jnp.full(peak_ref.shape, -1e30, FULL)
+    for image in range(row_count // PIECE):
+        tokens[image * PIECE : (image + 1) * PIECE, :] = padded_image(tokens_ref, image).astype(LOW)
 
     def image_forward(image):
         rows = image_rows(image)
-        unit, _ = normalized(tokens_ref[rows, :].astype(FULL))
-        normed = (unit * gain_one_ref[...]).astype(LOW)
-        normed_one_ref[rows, :] = normed
-        queries = dot_plain(normed, query_w_ref[...]).astype(LOW)
-        keys = dot_plain(normed, key_w_ref[...]).astype(LOW)
-        values = dot_plain(normed, value_w_ref[...]).astype(LOW)
-        query_ref[rows, :] = queries
-        key_ref[rows, :] = keys
-        value_ref[rows, :] = values
+        unit, _ = normalized(tokens[rows, :].astype(FULL))
+        normed = (unit * gains_ref[0:1, :]).astype(LOW)
+        normed_one[rows, :] = normed
+        queries = dot_last(normed, query_w_ref[...]).astype(LOW)
+        keys = dot_last(normed, key_w_ref[...]).astype(LOW)
+        values = dot_last(normed, value_w_ref[...]).astype(LOW)
+        query[rows, :] = queries
+        key[rows, :] = keys
+        value[rows, :] = values
         mixed = []
         for h in range(heads):
             cols = slice(h * HD, (h + 1) * HD)
@@ -332,21 +358,97 @@
             peak_ref[h : h + 1, :] = jnp.maximum(peak_ref[h : h + 1, :], best)
             mixed.append(dot_plain(probs.astype(LOW), values[:, cols]))
         mixed = jnp.concatenate(mixed, axis=1).astype(LOW)
-        mixed_ref[rows, :] = mixed
+        mixed_rows[rows, :] = mixed
         return dot_plain(mixed, output_w_ref[...])
 
     def normed_copy(j, owner):
-        rows = normed_two_ref.at[image_rows(2 * j + owner)]
+        rows = normed_two.at[image_rows(2 * j + owner)]
         return remote(rows, rows, ns.at[j], nr.at[j], (dp, mate))
+
+    def keep(i):
+        return pltpu.make_async_copy(held[i], outs[i], hs.at[i])
 
     def finish(j):
         rows = image_rows(2 * j + half)
-        residual = tokens_ref[rows, :].astype(FULL) + total.result(j)
-        residual_ref[rows, :] = residual
+        residual = tokens[rows, :].astype(FULL) + total.result(j)
+        residual_rows[j] = residual
         unit, _ = normalized(residual)
-        normed_two_ref[rows, :] = (unit * gain_two_ref[...]).astype(LOW)
+        normed_two[rows, :] = (unit * gains_ref[1:2, :]).astype(LOW)
         normed_copy(j, half).start()
 
+    def peer(k):
+        return (partner(dp, k, n), t)
+
+    def half_rows():
+        return pl.ds(pl.multiple_of(half * hp, hp), hp)
+
+    def side_columns():
+        return pl.ds(pl.multiple_of(side * width, width), width)
+
+    def own_copy():
+        return pltpu.make_async_copy(near_out.at[0], spread_hbm.at[0, half_rows()], own)
+
+    def near_copy(k):
+        return remote(near_out.at[k], spread_hbm.at[k, half_rows()], zs.at[k], zr.at[k], peer(k))
+
+    def far_copy(k):
+        return remote(
+            far_out.at[k - near],
+            spread_hbm.at[k, half_rows(), side_columns()],
+            zs.at[k],
+            zr.at[k],
+            peer(k),
+        )
+
+    def dispatch(k):
+        slots = lax.broadcasted_iota(jnp.int32, (hp, row_count), 0) + k * hp
+        hot = (place_ref[0:1, :] == slots) | (place_ref[1:2, :] == slots)
+        hot = jnp.where(hot, 1.0, 0.0).astype(LOW)
+
+        @pl.when(k < near)
+        def _():
+            near_out[k] = dot_plain(hot, upstream[...]).astype(LOW)
+
+            @pl.when(k == 0)
+            def _():
+                own_copy().start()
+
+            @pl.when(k > 0)
+            def _():
+                near_copy(k).start()
+
+        @pl.when(k >= near)
+        def _():
+            far_out[k - near] = dot_plain(hot, upstream[:, side_columns()]).astype(LOW)
+            far_copy(k).start()
+
+    def places_of_pairs():
+        routes, slot_ids = routes_ref[...], slot_ids_ref[...]
+        limits = jnp.zeros_like(routes)
+        for e in range(n):
+            limits = jnp.where(routes == e, capacity_ref[e], limits)
+        kept = slot_ids < limits
+        step = jnp.zeros_like(routes)
+        weight = 1
+        while weight < n:
+            step = step + (routes // weight + dp // weight) % 2 * weight
+            weight *= 2
+        upper = slot_ids >= per_half
+        in_half = slot_ids - jnp.where(upper, per_half, 0)
+        in_block = in_half + jnp.where(upper, hp, 0)
+        mine = kept & (upper == (half == 1))
+        place = jnp.where(mine, step * hp + in_half, -1)
+        position = jnp.where(kept, step * (2 * hp) + in_block, -1)
+        both = jnp.concatenate([place, position, routes, jnp.full_like(routes, -1)], axis=0)
+        fill = jnp.full((8, PIECE - SEQ), -1, jnp.int32)
+        spaced = []
+        for image in range(row_count // PIECE):
+            spaced += [both[:, image * SEQ : (image + 1) * SEQ], fill]
+        return jnp.concatenate(spaced, axis=1)
+
+    pairs = places_of_pairs()
+    place_ref[...] = pairs
+    index_ref[...] = pairs.T
     per_step = -(-n // 3)
 
     def step(j, carry):
@@ -359,14 +461,21 @@
         total.give(j, given)
         total.take(j, image_forward(2 * j + half))
 
-        def dispatch(i, inner):
+        @pl.when(j == 0)
+        def _():
+            for image in range(row_count // PIECE):
+                upstream[image * PIECE : (image + 1) * PIECE, :] = padded_image(
+                    upstream_ref, image
+                ).astype(LOW)
+
+        def turn(i, inner):
             @pl.when(i < n)
             def _():
-                spread.send((i + spread.near) % n, upstream_ref)
+                dispatch((i + near) % n)
 
             return inner
 
-        lax.fori_loop(j * per_step, (j + 1) * per_step, dispatch, 0)
+        lax.fori_loop(j * per_step, (j + 1) * per_step, turn, 0)
 
         @pl.when(j >= 1)
         def _():
@@ -375,58 +484,73 @@
         return carry
 
     lax.fori_loop(0, 3, step, 0)
-
-    def each(body, first=0):
-        def one(k, carry):
-            body(k)
-            return carry
-
-        lax.fori_loop(first, n, one, 0)
-
-    each(spread.first_hop)
+    for i in range(7):
+        keep(i).start()
     finish(2)
-    each(spread.second_hop)
-    each(spread.last_hop)
-    each(spread.sent)
+    keep(7).start()
+    own_copy().wait()
+
+    def arrive(k, carry):
+        @pl.when(k < near)
+        def _():
+            near_copy(k).wait()
+
+        @pl.when(k >= near)
+        def _():
+            far_copy(k).wait()
+
+        return carry
+
+    for j in range(3):
+        normed_copy(j, 1 - half).wait_recv()
+    keep(8).start()
+    lax.fori_loop(1, n, arrive, 0)
     for j in range(3):
         total.sent(j)
         normed_copy(j, half).wait_send()
-        normed_copy(j, 1 - half).wait_recv()
-
-
-def run_front(n, hp, tokens, upstream, place, gains, weights):
-    rows, model = tokens.shape
-    heads_width = weights[0].shape[1]
+    for i in range(9):
+        keep(i).wait()
+
+
+def run_front(n, hp, per_half, capacity, routes, slot_ids, tokens, upstream, gains, weights):
+    model = tokens.shape[1]
+    rows = tokens.shape[0] // SEQ * PIECE
+    heads_width = weights[0].shape[0]
+    near = near_count(n)
+    width = model // 2
     vmem = pl.BlockSpec(memory_space=VMEM)
+    hbm = pl.BlockSpec(memory_space=pl.ANY)
     shape = jax.ShapeDtypeStruct
-    slim = shape((rows, heads_width), LOW)
+    slim, wide = shape((rows, heads_width), LOW), shape((rows, model), LOW)
+    held = (wide, wide, wide, slim, slim, slim, slim, shape((3, PIECE, model), FULL), wide)
     return pl.pallas_call(
-        functools.partial(front_kernel, n, hp),
+        functools.partial(front_kernel, n, hp, per_half),
         out_shape=(
-            shape((rows, model), LOW),
-            slim,
-            slim,
-            slim,
-            slim,
-            shape((rows, model), FULL),
-            shape((rows, model), LOW),
+            shape((8, rows), jnp.int32),
+            shape((rows, 8), jnp.int32),
             shape((8, 128), FULL),
+            *held,
             shape((n, 2 * hp, model), LOW),
         ),
-        in_specs=[vmem] * 9,
-        out_specs=[vmem] * 9,
+        in_specs=[pl.BlockSpec(memory_space=pltpu.SMEM)] + [vmem] * 9,
+        out_specs=[vmem] * 3 + [hbm] * 10,
         scratch_shapes=[
-            *Spread.scratch(n, hp, model // 2),
-            *Spread.semaphores(n),
-            *Total.scratch(model),
+            *[VMEM(a.shape, a.dtype) for a in held],
+            VMEM((near, hp, model), LOW),
+            VMEM((n - near, hp, width), LOW),
+            dma(n),
+            dma(n),
+            pltpu.SemaphoreType.DMA,
             dma(3),
             dma(3),
+            dma(9),
+            *Total.scratch(model),
         ],
         compiler_params=pltpu.CompilerParams(
             collective_id=0, has_side_effects=True, vmem_limit_bytes=VMEM_LIMIT
         ),
         name="front",
-    )(tokens, upstream, place, *gains, *weights)
+    )(capacity, routes, slot_ids, tokens, upstream, gains, *weights)
 
 
 def in_turn(i, near):
@@ -437,24 +561,39 @@
     n,
     hp,
     place_ref,
-    gate_ref,
-    normed_ref,
-    first_ref,
-    second_ref,
+    router_ref,
     peak_ref,
+    normed_hbm,
+    first_hbm,
+    second_hbm,
     upstream_hbm,
-    answer_out,
-    answer_kept,
     back_ref,
     gate_sum_ref,
-    grad_first_ref,
-    grad_second_ref,
     top_ref,
+    answer_out_hbm,
+    answer_kept_hbm,
+    grad_first_hbm,
+    grad_second_hbm,
     *scratch,
 ):
     dp, t, half, side, mate, far = places()
     arrived = scratch[2]
     spread = Spread(n, hp, place_ref, *scratch[:10])
+    (
+        normed_ref,
+        first_ref,
+        second_ref,
+        answer_out,
+        answer_kept,
+        grad_first_ref,
+        grad_second_ref,
+        os_,
+        ws,
+        xs,
+        xr,
+        cs,
+        cr,
+    ) = scratch[44:]
     (
         upstream,
         hidden_all,
@@ -490,13 +629,38 @@
         qr,
         ss,
         sr,
-    ) = scratch[10:]
+    ) = scratch[10:44]
     model = normed_ref.shape[1]
     width = model // 2
     near = spread.near
     greet(n, dp, t, [(t + d) % 4 for d in (1, 2, 3)])
-    fetch = pltpu.make_async_copy(upstream_hbm, upstream, us)
-    fetch.start()
+    fetches = [
+        pltpu.make_async_copy(a, b, ws.at[i])
+        for i, (a, b) in enumerate(
+            ((normed_hbm, normed_ref), (first_hbm, first_ref), (second_hbm, second_ref))
+        )
+    ]
+    mine = (slice(0, near), spread.rows(half))
+    fetches.append(pltpu.make_async_copy(upstream_hbm.at[mine], upstream.at[mine], us.at[0]))
+    mine = (slice(near, n), spread.rows(half), spread.columns(side))
+    fetches.append(pltpu.make_async_copy(upstream_hbm.at[mine], upstream.at[mine], us.at[1]))
+    for fetch in fetches:
+        fetch.start()
+
+    def upstream_side_copy(k, owner):
+        part = upstream.at[k, spread.rows(half), spread.columns(owner)]
+        return remote(part, part, xs.at[k], xr.at[k], (dp, far))
+
+    def upstream_pair_copy(k, owner):
+        part = upstream.at[k, spread.rows(owner)]
+        return remote(part, part, cs.at[k], cr.at[k], (dp, mate))
+
+    def keep(i):
+        pairs = (
+            (answer_out, answer_out_hbm),
+            (answer_kept, answer_kept_hbm),
+        )
+        return pltpu.make_async_copy(*pairs[i], os_.at[i])
 
     def gate_copy(k):
         return remote(gate_out.at[k], gate_in.at[k, half], gs.at[k], gr.at[k], spread.peer(k))
@@ -544,13 +708,23 @@
 
         lax.fori_loop(first, last, one, 0)
 
+    fetches[0].wait()
+    logits = dot_last(router_ref[...], normed_ref[...])
+    rows_of = lax.broadcasted_iota(jnp.int32, logits.shape, 0)
+    one, two = (
+        jnp.sum(jnp.where(rows_of == place_ref[r : r + 1, :], logits, 0.0), axis=0, keepdims=True)
+        for r in (4, 5)
+    )
+    best = jnp.maximum(one, two)
+    one, two = jnp.exp(one - best), jnp.exp(two - best)
+    gate_one, gate_two = one / (one + two), two / (one + two)
     await_greetings(n, (1, 2, 3))
 
     def dispatch(i):
         k = (i + near) % n
         is_first, is_second = spread.send(k, normed_ref)
         gate = jnp.sum(
-            jnp.where(is_first, gate_ref[0:1, :], 0.0) + jnp.where(is_second, gate_ref[1:2, :], 0.0),
+            jnp.where(is_first, gate_one, 0.0) + jnp.where(is_second, gate_two, 0.0),
             axis=1,
             keepdims=True,
         )
@@ -566,7 +740,10 @@
             gate_copy(k).start()
 
     loop(dispatch)
-    fetch.wait()
+    for fetch in fetches[1:]:
+        fetch.wait()
+    loop(lambda k: upstream_side_copy(k, side).start(), near)
+    loop(lambda k: upstream_pair_copy(k, half).start(), 0, near)
 
     def chunk(i, k):
         gate = jnp.concatenate(
@@ -598,10 +775,32 @@
             sum_copy(k).start()
             peak_copy(k).start()
 
+    tile = 256
+    tiles = model // tile
+
+    def grad_copy(m, j):
+        cols = pl.ds(pl.multiple_of(m * tile, tile), tile)
+        ref, hbm = ((grad_first_ref, grad_first_hbm), (grad_second_ref, grad_second_hbm))[j]
+        return pltpu.make_async_copy(ref.at[cols], hbm.at[cols], os_.at[2 + 2 * m + j])
+
+    def grads(m):
+        cols = pl.ds(pl.multiple_of(m * tile, tile), tile)
+        rows_in = arrived[:, :, cols].reshape(n * 2 * hp, tile)
+        grad_first_ref[cols, :] = dot_first(rows_in, pre_grad_all[...].reshape(n * 2 * hp, -1))
+        grad_copy(m, 0).start()
+        hidden = hidden_all[:, :, cols].reshape(n * 2 * hp, tile)
+        grad_second_ref[cols, :] = dot_first(hidden, upstream[...].reshape(n * 2 * hp, model))
+        grad_copy(m, 1).start()
+
     def step(i):
         @pl.when(i < n)
         def _():
             spread.first_hop(in_turn(i, near))
+
+        @pl.when(i < n - near)
+        def _():
+            upstream_side_copy(i + near, 1 - side).wait_recv()
+            upstream_pair_copy(i + near, half).start()
 
         @pl.when((i >= 1) & (i < n + 1))
         def _():
@@ -619,6 +818,12 @@
             k = in_turn(i - 2, near)
             spread.last_hop(k)
             gate_pair_copy(k, 1 - half).wait_recv()
+            upstream_pair_copy(k, 1 - half).wait_recv()
+            upstream_pair_copy(k, half).wait_send()
+
+            @pl.when(k >= near)
+            def _():
+                upstream_side_copy(k, side).wait_send()
 
             @pl.when(i >= 5)
             def _():
@@ -626,6 +831,10 @@
 
             chunk(i - 2, k)
             part_copy(i - 2, k).start()
+
+        @pl.when((i >= n + 2) & (i < n + 2 + tiles))
+        def _():
+            grads(i - (n + 2))
 
         @pl.when((i >= 3) & (i < n + 3))
         def _():
@@ -649,7 +858,7 @@
                     answer_kept[k] = stays
                     answer_out[k] = goes
 
-        @pl.when(i >= 4)
+        @pl.when((i >= 4) & (i < n + 4))
         def _():
             k = in_turn(i - 4, near)
             far_copy(i - 4, k).wait_recv()
@@ -664,19 +873,9 @@
                 final[k] = rows
                 return_copy(k).start()
 
-    loop(step, 0, n + 4)
-
-    tile = 256
-
-    def grads(m):
-        cols = pl.ds(pl.multiple_of(m * tile, tile), tile)
-        rows_in = arrived[:, :, cols].reshape(n * 2 * hp, tile)
-        grad_first_ref[cols, :] = dot_first(rows_in, pre_grad_all[...].reshape(n * 2 * hp, -1))
-        hidden = hidden_all[:, :, cols].reshape(n * 2 * hp, tile)
-        grad_second_ref[cols, :] = dot_first(hidden, upstream[...].reshape(n * 2 * hp, model))
-
-    loop(grads, 0, model // tile)
-
+    loop(step, 0, n + 2 + tiles)
+    keep(0).start()
+    keep(1).start()
     peaks[0] = peak_ref[...]
 
     def collect_sums(k):
@@ -704,7 +903,9 @@
     loop(collect)
     for d in (1, 2, 3):
         share_copy(d, (t + 4 - d) % 4).wait_recv()
-    gate_sum_ref[...] = (sums[0] + sums[1]) + (sums[2] + sums[3])
+    whole = (sums[0] + sums[1]) + (sums[2] + sums[3])
+    whole = jnp.concatenate([whole[k : k + 1] for k in range(n)], axis=1)
+    gate_sum_ref[...] = jnp.broadcast_to(whole, gate_sum_ref.shape)
 
     def finish(i):
         k = in_turn(i, near)
@@ -728,27 +929,33 @@
     loop(finish)
     for d in (1, 2, 3):
         share_copy(d, t).wait_send()
-
-
-def run_experts(n, hp, place, gates, normed, first, second, peak, upstream):
+    keep(0).wait()
+    keep(1).wait()
+    for m in range(tiles):
+        grad_copy(m, 0).wait()
+        grad_copy(m, 1).wait()
+
+
+def run_experts(n, hp, place, router, peak, normed, first, second, upstream):
     model = normed.shape[1]
     width = model // 2
     hidden = first.shape[1]
     vmem = pl.BlockSpec(memory_space=VMEM)
+    hbm = pl.BlockSpec(memory_space=pl.ANY)
     shape = jax.ShapeDtypeStruct
     return pl.pallas_call(
         functools.partial(expert_kernel, n, hp),
         out_shape=(
+            shape((n, 2 * hp, width), LOW),
+            shape((8, n * 2 * hp), FULL),
+            shape(peak.shape, FULL),
             shape((n, hp, width), LOW),
             shape((n, hp, width), FULL),
-            shape((n, 2 * hp, width), LOW),
-            shape((n, 2 * hp), FULL),
             shape((model, hidden), FULL),
             shape((hidden, model), FULL),
-            shape(peak.shape, FULL),
         ),
-        in_specs=[vmem] * 6 + [pl.BlockSpec(memory_space=pl.ANY)],
-        out_specs=[vmem] * 7,
+        in_specs=[vmem] * 3 + [hbm] * 4,
+        out_specs=[vmem] * 3 + [hbm] * 4,
         scratch_shapes=[
             *Spread.scratch(n, hp, width),
             VMEM((n, 2 * hp, model), LOW),
@@ -768,15 +975,43 @@
             VMEM((n, 8, 2 * hp), FULL),
             VMEM((4, n, 2 * hp), FULL),
             VMEM((n, *peak.shape), FULL),
-            pltpu.SemaphoreType.DMA,
+            dma(2),
             dma(3), dma(n), dma(3), dma(n), dma(n), dma(n), dma(n), dma(n),
             dma(n), dma(n), dma(n), dma(n), dma(n), dma(n), dma(n), dma(n), dma(3), dma(3),
+            VMEM(normed.shape, LOW),
+            VMEM(first.shape, LOW),
+            VMEM(second.shape, LOW),
+            VMEM((n, hp, width), LOW),
+            VMEM((n, hp, width), FULL),
+            VMEM((model, hidden), FULL),
+            VMEM((hidden, model), FULL),
+            dma(2 + 2 * (model // 256)),
+            dma(3), dma(n), dma(n), dma(n), dma(n),
         ],
         compiler_params=pltpu.CompilerParams(
             collective_id=1, has_side_effects=True, vmem_limit_bytes=VMEM_LIMIT
         ),
         name="experts",
-    )(place, gates, normed, first, second, peak, upstream)
+    )(place, router, peak, normed, first, second, upstream)
+
+
+def unpad(rows_ref, out_ref):
+    for image in range(rows_ref.shape[0] // PIECE):
+        start = image * SEQ // 8 * 8
+        length = min(PIECE, out_ref.shape[0] - start)
+        shift = image * SEQ - start
+        rows = lax.broadcasted_iota(jnp.int32, (length, PIECE), 0)
+        columns = lax.broadcasted_iota(jnp.int32, (length, PIECE), 1)
+        pick = (rows == columns + shift) & (columns < SEQ)
+        image_part = rows_ref[image * PIECE : (image + 1) * PIECE, :]
+        moved = dot_plain(jnp.where(pick, 1.0, 0.0).astype(LOW), image_part).astype(LOW)
+        if shift:
+            before = lax.broadcasted_iota(jnp.int32, (8, moved.shape[1]), 0) < shift
+            first = jnp.where(before, out_ref[start : start + 8, :].astype(FULL), moved[:8].astype(FULL))
+            out_ref[start : start + 8, :] = first.astype(LOW)
+            out_ref[start + 8 : start + length, :] = moved[8:]
+        else:
+            out_ref[start : start + length, :] = moved
 
 
 def back_kernel(
@@ -785,19 +1020,18 @@
     back_ref,
     gate_sum_ref,
     index_ref,
-    residual_ref,
-    upstream_ref,
-    gain_one_ref,
-    gain_two_ref,
+    gains_ref,
     output_w_ref,
     router_ref,
-    answer_out,
     *refs,
 ):
-    later, outs, scratch = refs[:10], refs[10:15], refs[15:]
-    block_ref, grad_tokens_ref, weights_ref, small_ref, gain_ref = outs
-    held, scratch = scratch[:10], scratch[10:]
+    later, outs, scratch = refs[:13], refs[13:18], refs[18:]
+    block_out_ref, tokens_out_ref, weights_ref, small_ref, gain_ref = outs
+    held, scratch = scratch[:13], scratch[13:]
     (
+        residual_ref,
+        upstream_ref,
+        answer_out,
         answer_kept,
         normed_one_ref,
         query_ref,
@@ -836,6 +1070,8 @@
         answer_far,
         answer_final,
         answers,
+        block_ref,
+        grad_tokens_ref,
         hs,
         as_,
         ar,
@@ -863,9 +1099,9 @@
         fr,
         ks,
         kr,
-    ) = scratch[:52]
-    total = Total(*scratch[52:])
-    heads = query_w_ref.shape[1] // HD
+    ) = scratch[:54]
+    total = Total(*scratch[54:])
+    heads = query_w_ref.shape[0] // HD
     model = upstream_ref.shape[1]
     width = model // 2
     slots = back_ref.shape[0]
@@ -943,7 +1179,7 @@
 
     def hots(rows):
         columns = lax.broadcasted_iota(jnp.int32, (PIECE, slots), 1)
-        return index_ref[rows, 0:1] == columns, index_ref[rows, 1:2] == columns
+        return index_ref[rows, 2:3] == columns, index_ref[rows, 3:4] == columns
 
     def as_low(mask):
         return jnp.where(mask, 1.0, 0.0).astype(LOW)
@@ -963,13 +1199,15 @@
         moe_copy(j).start()
 
     loop(combine, 0, 3)
+    for fetch in fetches[:3]:
+        fetch.wait()
     loop(lambda k: answer_side_copy((k + near) % n).start())
 
     def gates_of(rows, normed):
-        logits = dot_plain(normed, router_ref[...])
+        logits = dot_last(normed, router_ref[...])
         lanes = lax.broadcasted_iota(jnp.int32, logits.shape, 1)
-        hot_one = index_ref[rows, 2:3] == lanes
-        hot_two = index_ref[rows, 3:4] == lanes
+        hot_one = index_ref[rows, 4:5] == lanes
+        hot_two = index_ref[rows, 5:6] == lanes
         one = jnp.sum(jnp.where(hot_one, logits, 0.0), axis=1, keepdims=True)
         two = jnp.sum(jnp.where(hot_two, logits, 0.0), axis=1, keepdims=True)
         top = jnp.maximum(one, two)
@@ -978,8 +1216,8 @@
 
     def moe_back(j):
         rows = image_rows(2 * j + half)
-        unit, factor = normalized(residual_ref[rows, :])
-        normed = (unit * gain_two_ref[...]).astype(LOW)
+        unit, factor = normalized(residual_ref[j])
+        normed = (unit * gains_ref[1:2, :]).astype(LOW)
         gate_one, gate_two, hot_one, hot_two = gates_of(rows, normed)
         first, second = hots(rows)
         slot_sums = gate_sum_ref[0:1, :]
@@ -990,11 +1228,11 @@
         logit_grad = logit_grad + jnp.where(hot_two, gate_two * (grad_two - mean), 0.0)
         logit_grad = logit_grad.astype(LOW)
         router_sum[...] += dot_first(normed, logit_grad)
-        normed_grad = dot_last(logit_grad, router_ref[...])
+        normed_grad = dot_plain(logit_grad, router_ref[...])
         moe_copy(j).wait_recv()
         normed_grad = normed_grad + both_sides(moe_mine[j].astype(FULL), moe_other[j].astype(FULL))
         gain_two_sum[...] += jnp.sum((normed_grad * unit).reshape(PIECE // 8, 8, model), axis=0)
-        grad = normalized_back(normed_grad * gain_two_ref[...], unit, factor)
+        grad = normalized_back(normed_grad * gains_ref[1:2, :], unit, factor)
         grad = grad + upstream_ref[rows, :].astype(FULL)
         residual_grad[j] = grad
         attention_grad[rows, :] = grad.astype(LOW)
@@ -1003,7 +1241,7 @@
     loop(moe_back, 0, 3)
     router_copy().start()
     gain_two_copy().start()
-    for fetch in fetches:
+    for fetch in fetches[3:]:
         fetch.wait()
 
     def image_back(image):
@@ -1090,9 +1328,9 @@
 
     def grad_part(image):
         rows = image_rows(image)
-        part = dot_last(query_grad[rows, :], query_w_ref[...])
-        part = part + dot_last(key_grad[rows, :], key_w_ref[...])
-        part = part + dot_last(value_grad[rows, :], value_w_ref[...])
+        part = dot_plain(query_grad[rows, :], query_w_ref[...])
+        part = part + dot_plain(key_grad[rows, :], key_w_ref[...])
+        part = part + dot_plain(value_grad[rows, :], value_w_ref[...])
         unit, _ = normalized(tokens_ref[rows, :].astype(FULL))
         gain_one_sum[...] += jnp.sum((part * unit).reshape(PIECE // 8, 8, model), axis=0)
         return part
@@ -1108,15 +1346,15 @@
 
     router_copy().wait_recv()
     gain_two_copy().wait_recv()
-    lanes = lax.broadcasted_iota(jnp.int32, (model, 128), 1)
     row = jnp.sum(gain_two_sum[...] + gain_two_in[...], axis=0, keepdims=True)
     column = jnp.concatenate(
         [row_to_column(row[:, i : i + 256]) for i in range(0, model, 256)], axis=0
     )
     totals_two[...] = jnp.concatenate(
         [
-            router_sum[...] + router_in[...] + jnp.where(lanes == 127, column, 0.0),
             dot_first(attention_grad[...], mixed_ref[...]),
+            router_sum[...] + router_in[...],
+            column,
         ],
         axis=1,
     )
@@ -1153,9 +1391,9 @@
 
     def block_rows(j):
         rows = image_rows(2 * j + half)
-        residual = residual_ref[rows, :]
+        residual = residual_ref[j]
         unit, _ = normalized(residual)
-        gate_one, gate_two, _, _ = gates_of(rows, (unit * gain_two_ref[...]).astype(LOW))
+        gate_one, gate_two, _, _ = gates_of(rows, (unit * gains_ref[1:2, :]).astype(LOW))
         first, second = hots(rows)
         from_first = dot_plain(as_low(first), answers[...])
         from_second = dot_plain(as_low(second), answers[...])
@@ -1169,7 +1407,7 @@
         rows = image_rows(2 * j + half)
         normed_grad = total.result(j)
         unit, factor = normalized(tokens_ref[rows, :].astype(FULL))
-        grad = normalized_back(normed_grad * gain_one_ref[...], unit, factor)
+        grad = normalized_back(normed_grad * gains_ref[0:1, :], unit, factor)
         grad_tokens_ref[rows, :] = (residual_grad[j] + grad).astype(LOW)
         tokens_copy(j, half).start()
 
@@ -1193,6 +1431,11 @@
     weights_ref[...] = jnp.sum(pieces_in[...].astype(FULL), axis=0)
     small_ref[...] = jnp.sum(small_in[...].astype(FULL), axis=0)
     gain_ref[...] = jnp.sum(gain_rows[...], axis=0)
+    for j in range(3):
+        tokens_copy(j, 1 - half).wait_recv()
+        block_pair_copy(j, 1 - half).wait_recv()
+    unpad(grad_tokens_ref, tokens_out_ref)
+    unpad(block_ref, block_out_ref)
 
     for j in range(3):
         moe_copy(j).wait_send()
@@ -1200,9 +1443,7 @@
         attention_copy(j, half).wait_send()
         total.sent(j)
         tokens_copy(j, half).wait_send()
-        tokens_copy(j, 1 - half).wait_recv()
         block_pair_copy(j, half).wait_send()
-        block_pair_copy(j, 1 - half).wait_recv()
         gain_copy(j + 1, t).wait_send()
     router_copy().wait_send()
     gain_two_copy().wait_send()
@@ -1221,10 +1462,10 @@
     loop(left)
 
 
-def run_back(n, hp, first, later):
-    upstream = first[4]
+def run_back(n, hp, row_count, first, later):
+    upstream = later[1]
     rows, model = upstream.shape
-    heads_width = later[2].shape[1]
+    heads_width = later[8].shape[1]
     width = model // 2
     piece = model // n
     vmem = pl.BlockSpec(memory_space=VMEM)
@@ -1232,14 +1473,14 @@
     slim = VMEM((3, PIECE, width), LOW)
     heads = VMEM((rows, heads_width), LOW)
     eight = VMEM((8, model), FULL)
-    wide, narrow = 3 * heads_width, heads_width + 128
+    wide, narrow = 3 * heads_width, heads_width + n + 1
     quarter = VMEM((n, hp, width), LOW)
     three, many = dma(3), dma(n)
     return pl.pallas_call(
         functools.partial(back_kernel, n, hp),
         out_shape=(
-            shape((rows, model), LOW),
-            shape((rows, model), LOW),
+            shape((row_count, model), LOW),
+            shape((row_count, model), LOW),
             shape((piece, wide), FULL),
             shape((piece, narrow), FULL),
             shape((8, model), FULL),
@@ -1255,8 +1496,8 @@
             eight, eight, eight,
             VMEM((4, 8, model), FULL),
             VMEM((n, 8, model), FULL),
-            VMEM((model, 128), FULL),
-            VMEM((model, 128), FULL),
+            VMEM((model, n), FULL),
+            VMEM((model, n), FULL),
             VMEM((model, wide), FULL),
             VMEM((model, narrow), FULL),
             VMEM((n, piece, wide), LOW),
@@ -1265,6 +1506,8 @@
             VMEM((n, piece, narrow), LOW),
             quarter, quarter,
             VMEM((n * 2 * hp, width), LOW),
+            VMEM((rows, model), LOW),
+            VMEM((rows, model), LOW),
             dma(len(later)),
             three, three, three, three, three, three, three, three, three, three,
             many, many, three, three, dma(2), dma(2),
@@ -1297,71 +1540,52 @@
 ):
     n = lax.axis_size("dp")
     row_count, model = tokens.shape
-    images = row_count // SEQ
     heads_here = w_query.shape[1] // HD
     slot_count = 23 * TOK_DEV // (10 * n) + 1
     per_half = -(-slot_count // 2)
     hp = -(-per_half // 16) * 16
     dp_here = lax.axis_index("dp")
-    half_here = lax.axis_index("tensor") % 2
-
-    def padded(rows, fill=0):
-        split = rows.reshape(images, SEQ, -1)
-        split = jnp.pad(split, ((0, 0), (0, PIECE - SEQ), (0, 0)), constant_values=fill)
-        return split.reshape(images * PIECE, -1)
-
-    def unpadded(rows):
-        return rows.reshape(images, PIECE, -1)[:, :SEQ].reshape(row_count, -1)
-
-    expert_ids = jnp.arange(n, dtype=jnp.int32)
-    limits = jnp.sum(
-        jnp.where(routes[:, :, None] == expert_ids, capacity[None, None, :], 0), axis=-1
-    )
-    kept = slot_ids < limits
-    step = jnp.bitwise_xor(routes, dp_here)
-    slot_half = slot_ids // per_half
-    in_half = slot_ids % per_half
-    place = jnp.where(kept & (slot_half == half_here), step * hp + in_half, -1)
-    position = jnp.where(kept, step * (2 * hp) + slot_half * hp + in_half, -1)
-    index = padded(jnp.concatenate([position, routes, place], axis=1), -1)
-    place_rows = jnp.pad(index[:, 4:6].T, ((0, 6), (0, 0)), constant_values=-1)
-    route_rows = index[:, 2:4].T
-
-    tokens_in = padded(tokens)
-    upstream = padded(cotangent)
-    gain_one = gain_attn.astype(FULL)[None]
-    gain_two = gain_moe.astype(FULL)[None]
-    weights = (w_query, w_key, w_value, w_output)
-    normed_one, query, key, value, mixed, residual, normed_two, peak, spread = run_front(
-        n, hp, tokens_in, upstream, place_rows, (gain_one, gain_two), weights
-    )
-    logit_rows = lax.dot_general(
-        w_router, normed_two, (((0,), (1,)), ((), ())), preferred_element_type=FULL
-    )
-    chosen = jnp.stack(
-        [jnp.sum(jnp.where(expert_ids[:, None] == route_rows[k], logit_rows, 0.0), axis=0) for k in (0, 1)]
-    )
-    gate_rows = jnp.pad(jax.nn.softmax(chosen, axis=0), ((0, 6), (0, 0)))
-    answer_out, answer_kept, back, gate_sums, grad_first, grad_second, top = run_experts(
-        n, hp, place_rows, gate_rows, normed_two, expert_in[0], expert_out[0], peak, spread
-    )
-    router_wide = jnp.pad(w_router, ((0, 0), (0, 128 - n)))
-    block_rows, token_rows, weight_grads, small, gain_rows = run_back(
+    gains = jnp.stack([gain_attn, gain_moe]).astype(FULL)
+    across = (w_query.T, w_key.T, w_value.T)
+    (
+        place,
+        index,
+        peak,
+        tokens_in,
+        upstream,
+        normed_one,
+        query,
+        key,
+        value,
+        mixed,
+        residual,
+        normed_two,
+        spread,
+    ) = run_front(
         n,
         hp,
+        per_half,
+        capacity,
+        routes.T,
+        slot_ids.T,
+        tokens,
+        cotangent,
+        gains,
+        (*across, w_output),
+    )
+    router = w_router.T
+    back, gate_sums, top, answer_out, answer_kept, grad_first, grad_second = run_experts(
+        n, hp, place, router, peak, normed_two, expert_in[0], expert_out[0], spread
+    )
+    block_out, grad_tokens, weight_grads, small, gain_rows = run_back(
+        n,
+        hp,
+        row_count,
+        (back.reshape(n * 2 * hp, -1), gate_sums, index, gains, w_output, router),
         (
-            back.reshape(n * 2 * hp, -1),
-            jnp.broadcast_to(gate_sums.reshape(1, -1), (8, n * 2 * hp)),
-            index,
             residual,
             upstream,
-            gain_one,
-            gain_two,
-            w_output,
-            router_wide,
             answer_out,
-        ),
-        (
             answer_kept,
             normed_one,
             query,
@@ -1369,9 +1593,7 @@
             value,
             mixed,
             tokens_in,
-            w_query,
-            w_key,
-            w_value,
+            *across,
         ),
     )
     head_max = top[:heads_here, 0]
@@ -1379,15 +1601,15 @@
     wide = w_query.shape[1]
     piece = model // n
     return (
-        unpadded(block_rows),
-        unpadded(token_rows),
+        block_out,
+        grad_tokens,
         lax.dynamic_slice_in_dim(gain_rows.sum(axis=0), dp_here * piece, piece),
-        small[:, 127],
+        small[:, wide + n],
         weight_grads[:, :wide],
         weight_grads[:, wide : 2 * wide],
         weight_grads[:, 2 * wide :],
-        small[:, 128:].T,
-        small[:, :n],
+        small[:, :wide].T,
+        small[:, wide : wide + n],
         grad_first[None],
         grad_second[None],
         w_query.astype(FULL) * column_factor,

time: 275 us -> 228 us (0.83)
  Pallas kernels: 235 us -> 208 us
  local copies, waits for them, and re-layouts: 32.3 us -> 16.4 us
    pallas_call x1, Pallas kernels: 63 us -> 44.8 us  [run_front(): pl.pallas_call(functools.partial(front_kernel, n, hp, per_half), out_shap...]
    reshape x6 -> x0, local copies, waits for them, and re-layouts: 7.86 us -> none  [the longest x4 4.37 us: padded(): split = rows.reshape(images, SEQ, -1)]
    pad x6 -> x0, local copies, waits for them, and re-layouts: 4.79 us -> none  [the longest x3 2.81 us: padded(): jnp.pad(split, ((0, 0), (0, PIECE - SEQ), (0, 0)), constant_values=fill)]
    pallas_call x1, Pallas kernels: 80.5 us -> 75.9 us  [run_experts(): pl.pallas_call(functools.partial(expert_kernel, n, hp), out_shape=(shape(...]
    pallas_call x1, Pallas kernels: 91.1 us -> 87.3 us  [run_back(): pl.pallas_call(functools.partial(back_kernel, n, hp), out_shape=(shape((r...]
    unnamed x35 -> x24, local copies, waits for them, and re-layouts: 9.38 us -> 9.83 us
where the time goes in v3:
time: 228 us
  Pallas kernels  208 us (91%)
  local copies, waits for them, and re-layouts  16.4 us (7%)
  other arithmetic  2.53 us (1%)
    pallas_call x1, Pallas kernels, run_back(): pl.pallas_call(functools.partial(back_kernel, n, hp), out_shape=(shape((r...  87.3 us
    pallas_call x1, Pallas kernels, run_experts(): pl.pallas_call(functools.partial(expert_kernel, n, hp), out_shape=(shape(...  75.9 us
    pallas_call x1, Pallas kernels, run_front(): pl.pallas_call(functools.partial(front_kernel, n, hp, per_half), out_shap...  44.8 us
    unnamed x24, local copies, waits for them, and re-layouts  9.83 us

profile of v3, /device:TPU:0, one launch (start us, length us, event | category | flops | bytes accessed | tf_op | source)
XLA Modules:
  0.0 227.6 jit_solution(2699866281720881728)
XLA Ops:
  0.6 0.7 stack.10
  1.3 0.7 stack.9
  2.0 0.6 maximum_convert_fusion.gains_ref
  2.6 44.8 %front.1 = (s32[8,1248]{1,0:T(8,128)}, s32[1248,8]{1,0:T(8,128)}, f32[8,128]{1,0:T(8,128)}, bf16[1248,768]{1,0:T(8,128)(2,1)}, bf16[1248,768]{1,0:T(8,128)(2,1)}...) custom-call(s32[8]{0:T(128)} %capacity_ref.1, ...), custom_call_target="tpu_custom_call" | custom-call | tf_op jit(solution)/shard_map/front/pallas_call | solution.py:526
  47.4 75.9 %experts.1 = (bf16[8,352,384]{2,1,0:T(8,128)(2,1)}, f32[8,2816]{1,0:T(8,128)}, f32[8,128]{1,0:T(8,128)}, bf16[8,176,384]{2,1,0:T(8,128)(2,1)}, f32[8,176,384]{2,...) custom-call(s32[8,1248]{1,0:T(8,128)} %get-tuple-element.39.place_ref, bf16[8,768]{1,0:T(8,128)(2,1)} %bitcast.24, ...), custom_call_target="tpu_custom_call" | custom-call | tf_op jit(solution)/shard_map/experts/pallas_call | solution.py:946
  123.3 0.0 copy-start.6
  123.3 0.0 copy-start.8
  123.4 0.0 copy-start
  123.4 0.0 copy-start.1
  123.4 87.3 %back.1 = (bf16[1182,768]{1,0:T(8,128)(2,1)}, bf16[1182,768]{1,0:T(8,128)(2,1)}, f32[96,576]{1,0:T(8,128)}, f32[96,201]{1,0:T(8,128)}, f32[8,768]{1,0:T(8,128)}) custom-call(bf16[2816,384]{1,0:T(8,128)(2,1)} %bitcast.19, f32[8,2816]{1,0:T(8,128)} %get-tuple-element.44.gate_sum_ref, s32[1248,8]{1,0:T(8,128)} %get-tuple-element.45.index_ref, ...), custom_call_target="tpu_custom_call" | custom-call | tf_op jit(solution)/shard_map/back/pallas_call | solution.py:1479
  210.7 0.0 copy-start.5
  210.7 2.0 fusion
  212.6 0.7 copy.31
  213.4 0.9 slice.26
  214.2 0.7 copy.32
  214.9 0.7 reduce_sum.9
  215.7 0.6 dynamic_slice.3
  216.3 1.5 slice_reduce_fusion
  217.8 0.0 copy-done.6
  217.8 0.1 slice_reduce_fusion.1
  217.9 0.0 copy-start.7
  217.9 0.1 broadcast_in_dim.11
  218.0 0.1 mul.20
  218.1 0.0 copy-done.1
  218.1 1.2 convert_multiply_fusion
  219.2 1.2 copy.37
  220.5 0.9 copy-done.4
  221.4 1.2 copy.38
  222.6 1.1 copy-done.3
  223.7 1.4 copy.39
  225.1 1.1 copy-done.2
  226.2 1.4 copy.40
  (8 shorter events, 0.0 us)
Async XLA Ops:
  123.3 94.4 %copy-start.6 = (f32[8,128]{1,0:T(8,128)S(1)}, f32[8,128]{1,0:T(8,128)}, u32[]{:S(2)}) copy-start(f32[8,128]{1,0:T(8,128)} %get-tuple-element.63) | copy-start | bytes 12292
  123.3 94.5 %copy-start.8 = (f32[3]{0:T(128)S(1)}, f32[3]{0:T(128)}, u32[]{:S(2)}) copy-start(f32[3]{0:T(128)} %param.28) | copy-start | bytes 40
  123.4 94.7 %copy-start = (bf16[768,192]{0,1:T(8,128)(2,1)S(1)}, bf16[768,192]{0,1:T(8,128)(2,1)}, u32[]{:S(2)}) copy-start(bf16[768,192]{0,1:T(8,128)(2,1)} %param.17) | copy-start | bytes 884740
  123.4 94.7 %copy-start.1 = (bf16[768,192]{0,1:T(8,128)(2,1)S(1)}, bf16[768,192]{0,1:T(8,128)(2,1)}, u32[]{:S(2)}) copy-start(bf16[768,192]{0,1:T(8,128)(2,1)} %param.18) | copy-start | bytes 884740
  210.7 8.6 %copy-start.5 = (bf16[1182,768]{1,0:T(8,128)(2,1)S(1)}, bf16[1182,768]{1,0:T(8,128)(2,1)}, u32[]{:S(2)}) copy-start(bf16[1182,768]{1,0:T(8,128)(2,1)} %get-tuple-element.112) | copy-start | bytes 5446660
  217.9 2.6 %copy-start.7 = (f32[3]{0:T(128)}, f32[3]{0:T(128)S(1)}, u32[]{:S(2)}) copy-start(f32[3]{0:T(128)S(1)} %slice_reduce_fusion.1) | copy-start | bytes 40
  219.2 2.2 copy-start.4
  221.4 2.3 %copy-start.3 = (f32[768,768]{1,0:T(8,128)S(1)}, f32[768,768]{1,0:T(8,128)}, u32[]{:S(2)}) copy-start(f32[768,768]{1,0:T(8,128)} %get-tuple-element.61) | copy-start | bytes 7077892
  223.7 2.5 %copy-start.2 = (f32[768,768]{1,0:T(8,128)S(1)}, f32[768,768]{1,0:T(8,128)}, u32[]{:S(2)}) copy-start(f32[768,768]{1,0:T(8,128)} %get-tuple-element.62) | copy-start | bytes 7077892

commit v4 on v3

--- a/solution.py
+++ b/solution.py
@@ -15,6 +15,8 @@
 EPSILON = 1e-06
 MESH = pl.DeviceIdType.MESH
 VMEM_LIMIT = 60 * 2**20
+SLOTS = 3
+LAG = 4
 VMEM = pltpu.VMEM
 LOW, FULL = jnp.bfloat16, jnp.float32
 
@@ -326,8 +328,8 @@
         residual_rows,
         normed_two,
     ) = held
-    near_out, far_out, zs, zr, own, ns, nr, hs = scratch[:8]
-    total = Total(*scratch[8:])
+    near_out, far_out, zs, zr, own, ns, nr, hs, xs, xr = scratch[:10]
+    total = Total(*scratch[10:])
     dp, t, half, side, mate, far = places()
     heads = query_w_ref.shape[0] // HD
     near = near_count(n)
@@ -399,6 +401,16 @@
             zr.at[k],
             peer(k),
         )
+
+    def side_copy(k, owner):
+        columns = pl.ds(pl.multiple_of(owner * width, width), width)
+        part = spread_hbm.at[k, half_rows(), columns]
+        return remote(part, part, xs.at[k], xr.at[k], (dp, far))
+
+    def forward(k, carry):
+        far_copy(k).wait_recv()
+        side_copy(k, side).start()
+        return carry
 
     def dispatch(k):
         slots = lax.broadcasted_iota(jnp.int32, (hp, row_count), 0) + k * hp
@@ -449,8 +461,6 @@
     pairs = places_of_pairs()
     place_ref[...] = pairs
     index_ref[...] = pairs.T
-    per_step = -(-n // 3)
-
     def step(j, carry):
         given = image_forward(2 * j + 1 - half)
 
@@ -468,14 +478,17 @@
                     upstream_ref, image
                 ).astype(LOW)
 
-        def turn(i, inner):
-            @pl.when(i < n)
-            def _():
-                dispatch((i + near) % n)
-
+        def turn(k, inner):
+            dispatch(k)
             return inner
 
-        lax.fori_loop(j * per_step, (j + 1) * per_step, turn, 0)
+        @pl.when(j == 0)
+        def _():
+            lax.fori_loop(near, n, turn, 0)
+
+        @pl.when(j == 1)
+        def _():
+            lax.fori_loop(0, near, turn, 0)
 
         @pl.when(j >= 1)
         def _():
@@ -486,25 +499,28 @@
     lax.fori_loop(0, 3, step, 0)
     for i in range(7):
         keep(i).start()
+    early = n - (n - near) // 4
+    lax.fori_loop(near, early, forward, 0)
     finish(2)
+    lax.fori_loop(early, n, forward, 0)
     keep(7).start()
     own_copy().wait()
 
     def arrive(k, carry):
-        @pl.when(k < near)
-        def _():
-            near_copy(k).wait()
-
-        @pl.when(k >= near)
-        def _():
-            far_copy(k).wait()
-
+        near_copy(k).wait()
+        return carry
+
+    def far_arrive(k, carry):
+        far_copy(k).wait_send()
+        side_copy(k, side).wait_send()
+        side_copy(k, 1 - side).wait_recv()
         return carry
 
     for j in range(3):
         normed_copy(j, 1 - half).wait_recv()
     keep(8).start()
-    lax.fori_loop(1, n, arrive, 0)
+    lax.fori_loop(1, near, arrive, 0)
+    lax.fori_loop(near, n, far_arrive, 0)
     for j in range(3):
         total.sent(j)
         normed_copy(j, half).wait_send()
@@ -544,6 +560,8 @@
             dma(3),
             dma(3),
             dma(9),
+            dma(n),
+            dma(n),
             *Total.scratch(model),
         ],
         compiler_params=pltpu.CompilerParams(
@@ -572,6 +590,7 @@
     top_ref,
     answer_out_hbm,
     answer_kept_hbm,
+    answer_ready_hbm,
     grad_first_hbm,
     grad_second_hbm,
     *scratch,
@@ -589,10 +608,12 @@
         grad_second_ref,
         os_,
         ws,
+        cs,
+        cr,
+        answer_far,
+        answer_ready,
         xs,
         xr,
-        cs,
-        cr,
     ) = scratch[44:]
     (
         upstream,
@@ -640,25 +661,25 @@
             ((normed_hbm, normed_ref), (first_hbm, first_ref), (second_hbm, second_ref))
         )
     ]
-    mine = (slice(0, near), spread.rows(half))
+    mine = (slice(0, n), spread.rows(half))
     fetches.append(pltpu.make_async_copy(upstream_hbm.at[mine], upstream.at[mine], us.at[0]))
-    mine = (slice(near, n), spread.rows(half), spread.columns(side))
-    fetches.append(pltpu.make_async_copy(upstream_hbm.at[mine], upstream.at[mine], us.at[1]))
     for fetch in fetches:
         fetch.start()
-
-    def upstream_side_copy(k, owner):
-        part = upstream.at[k, spread.rows(half), spread.columns(owner)]
-        return remote(part, part, xs.at[k], xr.at[k], (dp, far))
 
     def upstream_pair_copy(k, owner):
         part = upstream.at[k, spread.rows(owner)]
         return remote(part, part, cs.at[k], cr.at[k], (dp, mate))
 
+    def answer_side_copy(k):
+        return remote(
+            answer_out.at[k], answer_far.at[k - near], xs.at[k], xr.at[k], (dp, far)
+        )
+
     def keep(i):
         pairs = (
-            (answer_out, answer_out_hbm),
-            (answer_kept, answer_kept_hbm),
+            (answer_out.at[slice(0, near)], answer_out_hbm),
+            (answer_kept.at[slice(0, near)], answer_kept_hbm),
+            (answer_ready, answer_ready_hbm),
         )
         return pltpu.make_async_copy(*pairs[i], os_.at[i])
 
@@ -679,7 +700,7 @@
         )
 
     def far_copy(i, k):
-        return remote(far_out.at[i % 3], far_in.at[k], fs.at[i % 3], fr.at[k], (dp, far))
+        return remote(far_out.at[i % SLOTS], far_in.at[k], fs.at[i % SLOTS], fr.at[k], (dp, far))
 
     def return_copy(k):
         return remote(
@@ -742,8 +763,7 @@
     loop(dispatch)
     for fetch in fetches[1:]:
         fetch.wait()
-    loop(lambda k: upstream_side_copy(k, side).start(), near)
-    loop(lambda k: upstream_pair_copy(k, half).start(), 0, near)
+    loop(lambda i: upstream_pair_copy(in_turn(i, near), half).start())
 
     def chunk(i, k):
         gate = jnp.concatenate(
@@ -781,7 +801,7 @@
     def grad_copy(m, j):
         cols = pl.ds(pl.multiple_of(m * tile, tile), tile)
         ref, hbm = ((grad_first_ref, grad_first_hbm), (grad_second_ref, grad_second_hbm))[j]
-        return pltpu.make_async_copy(ref.at[cols], hbm.at[cols], os_.at[2 + 2 * m + j])
+        return pltpu.make_async_copy(ref.at[cols], hbm.at[cols], os_.at[3 + 2 * m + j])
 
     def grads(m):
         cols = pl.ds(pl.multiple_of(m * tile, tile), tile)
@@ -797,11 +817,6 @@
         def _():
             spread.first_hop(in_turn(i, near))
 
-        @pl.when(i < n - near)
-        def _():
-            upstream_side_copy(i + near, 1 - side).wait_recv()
-            upstream_pair_copy(i + near, half).start()
-
         @pl.when((i >= 1) & (i < n + 1))
         def _():
             k = in_turn(i - 1, near)
@@ -821,10 +836,6 @@
             upstream_pair_copy(k, 1 - half).wait_recv()
             upstream_pair_copy(k, half).wait_send()
 
-            @pl.when(k >= near)
-            def _():
-                upstream_side_copy(k, side).wait_send()
-
             @pl.when(i >= 5)
             def _():
                 part_copy(i - 5, in_turn(i - 5, near)).wait_send()
@@ -832,37 +843,33 @@
             chunk(i - 2, k)
             part_copy(i - 2, k).start()
 
-        @pl.when((i >= n + 2) & (i < n + 2 + tiles))
-        def _():
-            grads(i - (n + 2))
-
         @pl.when((i >= 3) & (i < n + 3))
         def _():
             k = in_turn(i - 3, near)
             part_copy(i - 3, k).wait_recv()
 
-            @pl.when(i >= 6)
+            @pl.when(i >= 3 + SLOTS)
             def _():
-                far_copy(i - 6, in_turn(i - 6, near)).wait_send()
+                far_copy(i - 3 - SLOTS, in_turn(i - 3 - SLOTS, near)).wait_send()
 
             for j in (1, 0):
-                whole = parts[i % 3, j, spread.rows(half), :].astype(FULL) + pair_in[k, j].astype(FULL)
+                whole = parts[(i - 3) % 3, j, spread.rows(half), :].astype(FULL) + pair_in[k, j].astype(FULL)
                 low, high = whole[:, :width], whole[:, width:]
                 stays = jnp.where(side == 0, low, high)
                 goes = jnp.where(side == 0, high, low).astype(LOW)
                 if j:
-                    kept[i % 3] = stays
-                    far_out[i % 3] = goes
+                    kept[(i - 3) % SLOTS] = stays
+                    far_out[(i - 3) % SLOTS] = goes
                     far_copy(i - 3, k).start()
                 else:
                     answer_kept[k] = stays
                     answer_out[k] = goes
 
-        @pl.when((i >= 4) & (i < n + 4))
-        def _():
-            k = in_turn(i - 4, near)
-            far_copy(i - 4, k).wait_recv()
-            rows = (kept[(i - 4) % 3] + far_in[k].astype(FULL)).astype(LOW)
+        @pl.when((i >= LAG) & (i < n + LAG))
+        def _():
+            k = in_turn(i - LAG, near)
+            far_copy(i - LAG, k).wait_recv()
+            rows = (kept[(i - LAG) % SLOTS] + far_in[k].astype(FULL)).astype(LOW)
 
             @pl.when(k == 0)
             def _():
@@ -873,7 +880,15 @@
                 final[k] = rows
                 return_copy(k).start()
 
-    loop(step, 0, n + 2 + tiles)
+        @pl.when(i == n + 2)
+        def _():
+            loop(lambda k: answer_side_copy(k).start(), near)
+
+        @pl.when((i >= n + 2) & (i < n + 2 + tiles))
+        def _():
+            grads(i - (n + 2))
+
+    loop(step, 0, n + max(LAG, 2 + tiles))
     keep(0).start()
     keep(1).start()
     peaks[0] = peak_ref[...]
@@ -901,6 +916,13 @@
         mate_copy(k, half).start()
 
     loop(collect)
+
+    def answers_whole(k):
+        answer_side_copy(k).wait_recv()
+        answer_ready[k - near] = (answer_kept[k] + answer_far[k - near].astype(FULL)).astype(LOW)
+
+    loop(answers_whole, near)
+    keep(2).start()
     for d in (1, 2, 3):
         share_copy(d, (t + 4 - d) % 4).wait_recv()
     whole = (sums[0] + sums[1]) + (sums[2] + sums[3])
@@ -924,13 +946,17 @@
         @pl.when(i >= n - 3)
         def _():
             part_copy(i, k).wait_send()
+
+        @pl.when(i >= n - SLOTS)
+        def _():
             far_copy(i, k).wait_send()
 
     loop(finish)
     for d in (1, 2, 3):
         share_copy(d, t).wait_send()
-    keep(0).wait()
-    keep(1).wait()
+    loop(lambda k: answer_side_copy(k).wait_send(), near)
+    for i in range(3):
+        keep(i).wait()
     for m in range(tiles):
         grad_copy(m, 0).wait()
         grad_copy(m, 1).wait()
@@ -940,6 +966,7 @@
     model = normed.shape[1]
     width = model // 2
     hidden = first.shape[1]
+    near = near_count(n)
     vmem = pl.BlockSpec(memory_space=VMEM)
     hbm = pl.BlockSpec(memory_space=pl.ANY)
     shape = jax.ShapeDtypeStruct
@@ -949,13 +976,14 @@
             shape((n, 2 * hp, width), LOW),
             shape((8, n * 2 * hp), FULL),
             shape(peak.shape, FULL),
-            shape((n, hp, width), LOW),
-            shape((n, hp, width), FULL),
+            shape((near, hp, width), LOW),
+            shape((near, hp, width), FULL),
+            shape((n - near, hp, width), LOW),
             shape((model, hidden), FULL),
             shape((hidden, model), FULL),
         ),
         in_specs=[vmem] * 3 + [hbm] * 4,
-        out_specs=[vmem] * 3 + [hbm] * 4,
+        out_specs=[vmem] * 3 + [hbm] * 5,
         scratch_shapes=[
             *Spread.scratch(n, hp, width),
             VMEM((n, 2 * hp, model), LOW),
@@ -965,8 +993,8 @@
             VMEM((n, 2 * hp, hidden), LOW),
             VMEM((3, 2, 2 * hp, model), LOW),
             VMEM((n, 2, hp, model), LOW),
-            VMEM((3, hp, width), FULL),
-            VMEM((3, hp, width), LOW),
+            VMEM((SLOTS, hp, width), FULL),
+            VMEM((SLOTS, hp, width), LOW),
             VMEM((n, hp, width), LOW),
             VMEM((n, hp, width), LOW),
             VMEM((n, 8, hp), FULL),
@@ -975,8 +1003,8 @@
             VMEM((n, 8, 2 * hp), FULL),
             VMEM((4, n, 2 * hp), FULL),
             VMEM((n, *peak.shape), FULL),
-            dma(2),
-            dma(3), dma(n), dma(3), dma(n), dma(n), dma(n), dma(n), dma(n),
+            dma(1),
+            dma(3), dma(n), dma(SLOTS), dma(n), dma(n), dma(n), dma(n), dma(n),
             dma(n), dma(n), dma(n), dma(n), dma(n), dma(n), dma(n), dma(n), dma(3), dma(3),
             VMEM(normed.shape, LOW),
             VMEM(first.shape, LOW),
@@ -985,8 +1013,11 @@
             VMEM((n, hp, width), FULL),
             VMEM((model, hidden), FULL),
             VMEM((hidden, model), FULL),
-            dma(2 + 2 * (model // 256)),
-            dma(3), dma(n), dma(n), dma(n), dma(n),
+            dma(3 + 2 * (model // 256)),
+            dma(3), dma(n), dma(n),
+            VMEM((n - near, hp, width), LOW),
+            VMEM((n - near, hp, width), LOW),
+            dma(n), dma(n),
         ],
         compiler_params=pltpu.CompilerParams(
             collective_id=1, has_side_effects=True, vmem_limit_bytes=VMEM_LIMIT
@@ -1023,6 +1054,7 @@
     gains_ref,
     output_w_ref,
     router_ref,
+    answer_ready,
     *refs,
 ):
     later, outs, scratch = refs[:13], refs[13:18], refs[18:]
@@ -1162,6 +1194,9 @@
     def answer_copy(k):
         return remote(answer_final.at[k], answer_rows(k, half), es.at[k], er.at[k], peer(k))
 
+    def far_answer_copy(k):
+        return remote(answer_ready.at[k - near], answer_rows(k, half), es.at[k], er.at[k], peer(k))
+
     def answer_pair_copy(k, owner):
         return remote(answer_rows(k, owner), answer_rows(k, owner), fs.at[k], fr.at[k], (dp, mate))
 
@@ -1195,13 +1230,14 @@
         @pl.when(j == 0)
         def _():
             await_greetings(n, (1, 2, 3))
+            loop(lambda k: far_answer_copy(k).start(), near)
 
         moe_copy(j).start()
 
     loop(combine, 0, 3)
     for fetch in fetches[:3]:
         fetch.wait()
-    loop(lambda k: answer_side_copy((k + near) % n).start())
+    loop(lambda k: answer_side_copy((k + 1) % near).start(), 0, near)
 
     def gates_of(rows, normed):
         logits = dot_last(normed, router_ref[...])
@@ -1274,28 +1310,74 @@
             answer_final[k] = rows
             answer_copy(k).start()
 
-    per_image = -(-n // 4)
-
-    def attention_back(i):
-        j = i % 3
-
-        @pl.when(i >= 3)
-        def _():
-            attention_copy(j, 1 - half).wait_recv()
-
-        image_back(2 * j + jnp.where(i < 3, half, 1 - half))
-
-        def turn(m):
-            @pl.when(m < n)
+    def grad_part(image):
+        rows = image_rows(image)
+        part = dot_plain(query_grad[rows, :], query_w_ref[...])
+        part = part + dot_plain(key_grad[rows, :], key_w_ref[...])
+        part = part + dot_plain(value_grad[rows, :], value_w_ref[...])
+        unit, _ = normalized(tokens_ref[rows, :].astype(FULL))
+        gain_one_sum[...] += jnp.sum((part * unit).reshape(PIECE // 8, 8, model), axis=0)
+        return part
+
+    def my_piece(source, k):
+        at = partner(dp, k, n) * piece
+        grain = math.gcd(piece, 8)
+        span = -(-(piece + 8 - grain) // 8) * 8
+        taken = source[pl.ds(pl.multiple_of(at // 8 * 8, 8), span), :]
+        rows = taken[:piece]
+        for shift in range(grain, 8, grain):
+            rows = jnp.where(at % 8 == shift, taken[shift : shift + piece], rows)
+        return rows.astype(LOW)
+
+    def small_grads():
+        router_copy().wait_recv()
+        gain_two_copy().wait_recv()
+        row = jnp.sum(gain_two_sum[...] + gain_two_in[...], axis=0, keepdims=True)
+        column = jnp.concatenate(
+            [row_to_column(row[:, i : i + 256]) for i in range(0, model, 256)], axis=0
+        )
+        totals_two[...] = jnp.concatenate(
+            [
+                dot_first(attention_grad[...], mixed_ref[...]),
+                router_sum[...] + router_in[...],
+                column,
+            ],
+            axis=1,
+        )
+
+        def send_small(i):
+            k = (i + near) % n
+            small_pieces[k] = my_piece(totals_two, k)
+
+            @pl.when(k > 0)
             def _():
-                answer_turn((m + near) % n)
-
-        @pl.when(i >= 2)
-        def _():
-            loop(turn, (i - 2) * per_image, (i - 1) * per_image)
-
-    loop(attention_back, 0, 6)
-
+                small_copy(k).start()
+
+        loop(send_small)
+
+    for j in range(3):
+        attention_copy(j, 1 - half).wait_recv()
+
+    def attention_back(j):
+        for owner in (1 - half, half):
+            image_back(2 * j + owner)
+        total.give(j, grad_part(2 * j + 1 - half))
+        total.take(j, grad_part(2 * j + half))
+        answer_turn((j + 1) % near)
+
+        @pl.when(j == 1)
+        def _():
+            small_grads()
+
+        @pl.when(j == 2)
+        def _():
+            answer_turn(0)
+
+    loop(attention_back, 0, 3)
+
+    gain_one_all[t] = jnp.sum(gain_one_sum[...], axis=0, keepdims=True)
+    for d in (1, 2, 3):
+        gain_copy(d, t).start()
     normed_one = normed_one_ref[...]
     totals[:, : 3 * query_grad.shape[1]] = jnp.concatenate(
         [
@@ -1306,16 +1388,6 @@
         axis=1,
     )
 
-    def my_piece(source, k):
-        at = partner(dp, k, n) * piece
-        grain = math.gcd(piece, 8)
-        span = -(-(piece + 8 - grain) // 8) * 8
-        taken = source[pl.ds(pl.multiple_of(at // 8 * 8, 8), span), :]
-        rows = taken[:piece]
-        for shift in range(grain, 8, grain):
-            rows = jnp.where(at % 8 == shift, taken[shift : shift + piece], rows)
-        return rows.astype(LOW)
-
     def send_piece(i):
         k = (i + near) % n
         pieces[k] = my_piece(totals, k)
@@ -1326,67 +1398,21 @@
 
     loop(send_piece)
 
-    def grad_part(image):
-        rows = image_rows(image)
-        part = dot_plain(query_grad[rows, :], query_w_ref[...])
-        part = part + dot_plain(key_grad[rows, :], key_w_ref[...])
-        part = part + dot_plain(value_grad[rows, :], value_w_ref[...])
-        unit, _ = normalized(tokens_ref[rows, :].astype(FULL))
-        gain_one_sum[...] += jnp.sum((part * unit).reshape(PIECE // 8, 8, model), axis=0)
-        return part
-
-    def sum_images(j):
-        total.give(j, grad_part(2 * j + 1 - half))
-        total.take(j, grad_part(2 * j + half))
-
-    loop(sum_images, 0, 3)
-    gain_one_all[t] = gain_one_sum[...]
-    for d in (1, 2, 3):
-        gain_copy(d, t).start()
-
-    router_copy().wait_recv()
-    gain_two_copy().wait_recv()
-    row = jnp.sum(gain_two_sum[...] + gain_two_in[...], axis=0, keepdims=True)
-    column = jnp.concatenate(
-        [row_to_column(row[:, i : i + 256]) for i in range(0, model, 256)], axis=0
-    )
-    totals_two[...] = jnp.concatenate(
-        [
-            dot_first(attention_grad[...], mixed_ref[...]),
-            router_sum[...] + router_in[...],
-            column,
-        ],
-        axis=1,
-    )
-
-    def send_small(i):
-        k = (i + near) % n
-        small_pieces[k] = my_piece(totals_two, k)
-
-        @pl.when(k > 0)
-        def _():
-            small_copy(k).start()
-
-    loop(send_small)
 
     def answers_here(i):
         k = in_turn(i, near)
 
-        @pl.when(k > 0)
+        @pl.when((k > 0) & (k < near))
         def _():
             answer_copy(k).wait_recv()
 
+        @pl.when(k >= near)
+        def _():
+            far_answer_copy(k).wait_recv()
+
         answer_pair_copy(k, half).start()
 
     loop(answers_here)
-    for d in (1, 2, 3):
-        gain_copy(d, (t + 4 - d) % 4).wait_recv()
-    gain_rows[0] = (gain_one_all[0] + gain_one_all[1]) + (gain_one_all[2] + gain_one_all[3])
-
-    def send_gain(k):
-        gain_row_copy(k).start()
-
-    loop(send_gain, 1)
     loop(lambda k: answer_pair_copy(k, 1 - half).wait_recv())
 
     def block_rows(j):
@@ -1412,13 +1438,27 @@
         tokens_copy(j, half).start()
 
     loop(tokens_back, 0, 3)
+    for d in (1, 2, 3):
+        gain_copy(d, (t + 4 - d) % 4).wait_recv()
+    gain_rows[0] = (gain_one_all[0] + gain_one_all[1]) + (gain_one_all[2] + gain_one_all[3])
+
+    def send_gain(k):
+        gain_row_copy(k).start()
+
+    loop(send_gain, 1)
 
     def block_back(j):
         block_copy(j).wait_recv()
         block_ref[image_rows(2 * j + half), :] = both_sides(block_mine[j], block_other[j])
         block_pair_copy(j, half).start()
 
+    for j in range(3):
+        tokens_copy(j, 1 - half).wait_recv()
+    unpad(grad_tokens_ref, tokens_out_ref)
     loop(block_back, 0, 3)
+    for j in range(3):
+        block_pair_copy(j, 1 - half).wait_recv()
+    unpad(block_ref, block_out_ref)
     pieces_in[0] = pieces[0]
     small_in[0] = small_pieces[0]
 
@@ -1431,11 +1471,6 @@
     weights_ref[...] = jnp.sum(pieces_in[...].astype(FULL), axis=0)
     small_ref[...] = jnp.sum(small_in[...].astype(FULL), axis=0)
     gain_ref[...] = jnp.sum(gain_rows[...], axis=0)
-    for j in range(3):
-        tokens_copy(j, 1 - half).wait_recv()
-        block_pair_copy(j, 1 - half).wait_recv()
-    unpad(grad_tokens_ref, tokens_out_ref)
-    unpad(block_ref, block_out_ref)
 
     for j in range(3):
         moe_copy(j).wait_send()
@@ -1449,7 +1484,18 @@
     gain_two_copy().wait_send()
 
     def left(k):
-        answer_side_copy(k).wait_send()
+        @pl.when(k < near)
+        def _():
+            answer_side_copy(k).wait_send()
+
+        @pl.when((k > 0) & (k < near))
+        def _():
+            answer_copy(k).wait_send()
+
+        @pl.when(k >= near)
+        def _():
+            far_answer_copy(k).wait_send()
+
         answer_pair_copy(k, half).wait_send()
 
         @pl.when(k > 0)
@@ -1457,7 +1503,6 @@
             piece_copy(k).wait_send()
             small_copy(k).wait_send()
             gain_row_copy(k).wait_send()
-            answer_copy(k).wait_send()
 
     loop(left)
 
@@ -1474,7 +1519,7 @@
     heads = VMEM((rows, heads_width), LOW)
     eight = VMEM((8, model), FULL)
     wide, narrow = 3 * heads_width, heads_width + n + 1
-    quarter = VMEM((n, hp, width), LOW)
+    quarter = VMEM((near_count(n), hp, width), LOW)
     three, many = dma(3), dma(n)
     return pl.pallas_call(
         functools.partial(back_kernel, n, hp),
@@ -1483,9 +1528,9 @@
             shape((row_count, model), LOW),
             shape((piece, wide), FULL),
             shape((piece, narrow), FULL),
-            shape((8, model), FULL),
+            shape((1, model), FULL),
         ),
-        in_specs=[vmem] * len(first) + [pl.BlockSpec(memory_space=pl.ANY)] * len(later),
+        in_specs=[vmem] * (len(first) - 1) + [pl.BlockSpec(memory_space=pl.ANY)] * (1 + len(later)),
         out_specs=[vmem] * 5,
         scratch_shapes=[
             *[VMEM(a.shape, a.dtype) for a in later],
@@ -1494,8 +1539,8 @@
             VMEM((3, PIECE, model), FULL),
             heads, heads, heads,
             eight, eight, eight,
-            VMEM((4, 8, model), FULL),
-            VMEM((n, 8, model), FULL),
+            VMEM((4, 1, model), FULL),
+            VMEM((n, 1, model), FULL),
             VMEM((model, n), FULL),
             VMEM((model, n), FULL),
             VMEM((model, wide), FULL),
@@ -1574,14 +1619,14 @@
         (*across, w_output),
     )
     router = w_router.T
-    back, gate_sums, top, answer_out, answer_kept, grad_first, grad_second = run_experts(
+    back, gate_sums, top, answer_out, answer_kept, answer_ready, grad_first, grad_second = run_experts(
         n, hp, place, router, peak, normed_two, expert_in[0], expert_out[0], spread
     )
     block_out, grad_tokens, weight_grads, small, gain_rows = run_back(
         n,
         hp,
         row_count,
-        (back.reshape(n * 2 * hp, -1), gate_sums, index, gains, w_output, router),
+        (back.reshape(n * 2 * hp, -1), gate_sums, index, gains, w_output, router, answer_ready),
         (
             residual,
             upstream,
@@ -1603,7 +1648,7 @@
     return (
         block_out,
         grad_tokens,
-        lax.dynamic_slice_in_dim(gain_rows.sum(axis=0), dp_here * piece, piece),
+        lax.dynamic_slice_in_dim(gain_rows[0], dp_here * piece, piece),
         small[:, wide + n],
         weight_grads[:, :wide],
         weight_grads[:, wide : 2 * wide],

time: 228 us -> 216 us (0.947)
  Pallas kernels: 208 us -> 195 us
    pallas_call x1, Pallas kernels: 87.3 us -> 69.2 us  [run_back(): pl.pallas_call(functools.partial(back_kernel, n, hp), out_shape=(shape((r...]
    pallas_call x1, Pallas kernels: 75.9 us -> 78.9 us  [run_experts(): pl.pallas_call(functools.partial(expert_kernel, n, hp), out_shape=(shape(...]
where the time goes in v4:
time: 216 us; the launch traced here: 215 us
  Pallas kernels  195 us (90%)
  local copies, waits for them, and re-layouts  17 us (8%)
    pallas_call x1, Pallas kernels, run_experts(): pl.pallas_call(functools.partial(expert_kernel, n, hp), out_shape=(shape(...  78.9 us
    pallas_call x1, Pallas kernels, run_back(): pl.pallas_call(functools.partial(back_kernel, n, hp), out_shape=(shape((r...  69.2 us
    pallas_call x1, Pallas kernels, run_front(): pl.pallas_call(functools.partial(front_kernel, n, hp, per_half), out_shap...  47 us
    unnamed x24, local copies, waits for them, and re-layouts  9.83 us

profile of v4, /device:TPU:0, one launch (start us, length us, event | category | flops | bytes accessed | tf_op | source)
XLA Modules:
  0.0 214.7 jit_solution(6083012034007875117)
XLA Ops:
  0.6 0.7 stack.10
  1.3 0.7 stack.9
  2.0 0.6 maximum_convert_fusion.gains_ref
  2.6 47.0 %front.1 = (s32[8,1248]{1,0:T(8,128)}, s32[1248,8]{1,0:T(8,128)}, f32[8,128]{1,0:T(8,128)}, bf16[1248,768]{1,0:T(8,128)(2,1)}, bf16[1248,768]{1,0:T(8,128)(2,1)}...) custom-call(s32[8]{0:T(128)} %capacity_ref.1, ...), custom_call_target="tpu_custom_call" | custom-call | tf_op jit(solution)/shard_map/front/pallas_call | solution.py:542
  49.6 78.9 %experts.1 = (bf16[8,352,384]{2,1,0:T(8,128)(2,1)}, f32[8,2816]{1,0:T(8,128)}, f32[8,128]{1,0:T(8,128)}, bf16[4,176,384]{2,1,0:T(8,128)(2,1)}, f32[4,176,384]{2,...) custom-call(s32[8,1248]{1,0:T(8,128)} %get-tuple-element.40.place_ref, ...), custom_call_target="tpu_custom_call" | custom-call | tf_op jit(solution)/shard_map/experts/pallas_call | solution.py:973
  128.6 0.0 copy-start.6
  128.6 0.0 copy-start.8
  128.6 0.0 copy-start
  128.6 0.0 copy-start.1
  128.6 69.2 %back.1 = (bf16[1182,768]{1,0:T(8,128)(2,1)}, bf16[1182,768]{1,0:T(8,128)(2,1)}, f32[96,576]{1,0:T(8,128)}, f32[96,201]{1,0:T(8,128)}, f32[1,768]{1,0:T(1,128)}) custom-call(bf16[2816,384]{1,0:T(8,128)(2,1)} %bitcast.21, f32[8,2816]{1,0:T(8,128)} %get-tuple-element.45.gate_sum_ref, s32[1248,8]{1,0:T(8,128)} %get-tuple-element.46.index_ref, ...), custom_call_target="tpu_custom_call" | custom-call | tf_op jit(solution)/shard_map/back/pallas_call | solution.py:1524
  197.9 0.0 copy-start.5
  197.9 2.0 fusion
  199.8 0.7 copy.31
  200.6 0.9 slice.26
  201.5 0.7 copy.32
  202.1 1.2 dynamic-slice_bitcast_fusion
  203.3 1.5 slice_reduce_fusion
  204.8 0.0 copy-done.6
  204.8 0.1 slice_reduce_fusion.1
  204.9 0.0 copy-done.8
  204.9 0.0 copy-start.7
  205.0 0.1 broadcast_in_dim.11
  205.0 0.1 mul.20
  205.1 0.0 copy-done.1
  205.1 1.2 convert_multiply_fusion
  206.3 1.2 copy.37
  207.5 0.9 copy-done.4
  208.4 1.2 copy.38
  209.7 1.1 copy-done.3
  210.8 1.4 copy.39
  212.2 1.1 copy-done.2
  213.3 1.4 copy.40
  (7 shorter events, 0.0 us)
Async XLA Ops:
  128.6 76.2 %copy-start.6 = (f32[8,128]{1,0:T(8,128)S(1)}, f32[8,128]{1,0:T(8,128)}, u32[]{:S(2)}) copy-start(f32[8,128]{1,0:T(8,128)} %get-tuple-element.65) | copy-start | bytes 12292
  128.6 76.4 %copy-start.8 = (f32[3]{0:T(128)S(1)}, f32[3]{0:T(128)}, u32[]{:S(2)}) copy-start(f32[3]{0:T(128)} %param.28) | copy-start | bytes 40
  128.6 76.5 %copy-start = (bf16[768,192]{0,1:T(8,128)(2,1)S(1)}, bf16[768,192]{0,1:T(8,128)(2,1)}, u32[]{:S(2)}) copy-start(bf16[768,192]{0,1:T(8,128)(2,1)} %param.17) | copy-start | bytes 884740
  128.6 76.5 %copy-start.1 = (bf16[768,192]{0,1:T(8,128)(2,1)S(1)}, bf16[768,192]{0,1:T(8,128)(2,1)}, u32[]{:S(2)}) copy-start(bf16[768,192]{0,1:T(8,128)(2,1)} %param.18) | copy-start | bytes 884740
  197.9 8.4 %copy-start.5 = (bf16[1182,768]{1,0:T(8,128)(2,1)S(1)}, bf16[1182,768]{1,0:T(8,128)(2,1)}, u32[]{:S(2)}) copy-start(bf16[1182,768]{1,0:T(8,128)(2,1)} %get-tuple-element.114) | copy-start | bytes 5446660
  204.9 2.6 %copy-start.7 = (f32[3]{0:T(128)}, f32[3]{0:T(128)S(1)}, u32[]{:S(2)}) copy-start(f32[3]{0:T(128)S(1)} %slice_reduce_fusion.1) | copy-start | bytes 40
  206.3 2.2 %copy-start.4 = (bf16[1182,768]{1,0:T(8,128)(2,1)S(1)}, bf16[1182,768]{1,0:T(8,128)(2,1)}, u32[]{:S(2)}) copy-start(bf16[1182,768]{1,0:T(8,128)(2,1)} %get-tuple-element.115) | copy-start | bytes 5446660
  208.4 2.3 %copy-start.3 = (f32[768,768]{1,0:T(8,128)S(1)}, f32[768,768]{1,0:T(8,128)}, u32[]{:S(2)}) copy-start(f32[768,768]{1,0:T(8,128)} %get-tuple-element.63) | copy-start | bytes 7077892
  210.8 2.5 %copy-start.2 = (f32[768,768]{1,0:T(8,128)S(1)}, f32[768,768]{1,0:T(8,128)}, u32[]{:S(2)}) copy-start(f32[768,768]{1,0:T(8,128)} %get-tuple-element.64) | copy-start | bytes 7077892

commit v5 on v4

--- a/solution.py
+++ b/solution.py
@@ -1566,6 +1566,100 @@
     )(*first, *later)
 
 
+def results_kernel(
+    threshold_ref,
+    weights_ref,
+    small_ref,
+    gain_row_ref,
+    top_ref,
+    query_w_ref,
+    key_w_ref,
+    *refs,
+):
+    moved_in, moved_out = refs[:4], refs[4:8]
+    (
+        gain_one_ref,
+        gain_two_ref,
+        query_ref,
+        key_ref,
+        value_ref,
+        output_ref,
+        router_ref,
+        clipped_query_ref,
+        clipped_key_ref,
+        head_max_ref,
+        *held,
+        sems,
+    ) = refs[8:]
+    fetches, copies = [], []
+    for i, (source, target) in enumerate(zip(moved_in, moved_out)):
+        rows = source.shape[0]
+        cut = rows // 16 * 8
+        for part, at in enumerate((slice(0, cut), slice(cut, rows))):
+            sem = sems.at[2 * i + part]
+            fetches.append(pltpu.make_async_copy(source.at[at], held[i].at[at], sem))
+            sem = sems.at[8 + 2 * i + part]
+            copies.append(pltpu.make_async_copy(held[i].at[at], target.at[at], sem))
+    for fetch in fetches:
+        fetch.start()
+    for fetch, copy in zip(fetches, copies):
+        fetch.wait()
+        copy.start()
+    piece, wide = query_ref.shape
+    heads = head_max_ref.shape[0]
+    query_ref[...] = weights_ref[:, :wide]
+    key_ref[...] = weights_ref[:, wide : 2 * wide]
+    value_ref[...] = weights_ref[:, 2 * wide :]
+    small = small_ref[...]
+    output_ref[...] = small[:, :wide].T
+    n = router_ref.shape[0]
+    router_ref[...] = small[:, wide : wide + n].T
+    gain_two_ref[...] = column_to_row(small[:, wide + n :])[0]
+    model = gain_row_ref.shape[1]
+    lanes = lax.broadcasted_iota(jnp.int32, (piece, model), 1)
+    mine = lax.broadcasted_iota(jnp.int32, (piece, model), 0) + lax.axis_index("dp") * piece
+    column = jnp.sum(jnp.where(lanes == mine, gain_row_ref[...], 0.0), axis=1, keepdims=True)
+    gain_one_ref[...] = column_to_row(column)[0]
+    head_max_ref[...] = column_to_row(top_ref[:, 0:1])[0, :heads]
+    for h in range(heads):
+        rows = slice(h * HD, (h + 1) * HD)
+        factor = jnp.sqrt(jnp.minimum(1.0, threshold_ref[h] / top_ref[h : h + 1, 0:1]))
+        clipped_query_ref[rows, :] = query_w_ref[rows, :].astype(FULL) * factor
+        clipped_key_ref[rows, :] = key_w_ref[rows, :].astype(FULL) * factor
+    for copy in copies:
+        copy.wait()
+
+
+def run_results(n, threshold, weights, small, gain_row, top, query_w, key_w, moved):
+    wide, model = query_w.shape
+    piece = weights.shape[0]
+    shape = jax.ShapeDtypeStruct
+    vmem = pl.BlockSpec(memory_space=VMEM)
+    hbm = pl.BlockSpec(memory_space=pl.ANY)
+    grad, clipped = shape((piece, wide), FULL), shape((wide, model), FULL)
+    return pl.pallas_call(
+        results_kernel,
+        out_shape=(
+            *[shape(a.shape, a.dtype) for a in moved],
+            shape((piece,), FULL),
+            shape((piece,), FULL),
+            grad,
+            grad,
+            grad,
+            shape((wide, piece), FULL),
+            shape((n, piece), FULL),
+            clipped,
+            clipped,
+            shape(threshold.shape, FULL),
+        ),
+        in_specs=[pl.BlockSpec(memory_space=pltpu.SMEM)] + [vmem] * 6 + [hbm] * 4,
+        out_specs=[hbm] * 4 + [vmem] * 10,
+        scratch_shapes=[*[VMEM(a.shape, a.dtype) for a in moved], dma(16)],
+        compiler_params=pltpu.CompilerParams(vmem_limit_bytes=VMEM_LIMIT),
+        name="results",
+    )(threshold, weights, small, gain_row, top, query_w, key_w, *moved)
+
+
 def body(
     tokens,
     gain_attn,
@@ -1585,11 +1679,9 @@
 ):
     n = lax.axis_size("dp")
     row_count, model = tokens.shape
-    heads_here = w_query.shape[1] // HD
     slot_count = 23 * TOK_DEV // (10 * n) + 1
     per_half = -(-slot_count // 2)
     hp = -(-per_half // 16) * 16
-    dp_here = lax.axis_index("dp")
     gains = jnp.stack([gain_attn, gain_moe]).astype(FULL)
     across = (w_query.T, w_key.T, w_value.T)
     (
@@ -1641,24 +1733,45 @@
             *across,
         ),
     )
-    head_max = top[:heads_here, 0]
-    column_factor = jnp.repeat(jnp.sqrt(jnp.minimum(1.0, threshold / head_max)), HD)[None, :]
-    wide = w_query.shape[1]
-    piece = model // n
+    (
+        block_out,
+        grad_tokens,
+        grad_first,
+        grad_second,
+        gain_one,
+        gain_two,
+        grad_query,
+        grad_key,
+        grad_value,
+        grad_output,
+        grad_router,
+        clipped_query,
+        clipped_key,
+        head_max,
+    ) = run_results(
+        n,
+        threshold,
+        weight_grads,
+        small,
+        gain_rows,
+        top,
+        *across[:2],
+        (block_out, grad_tokens, grad_first, grad_second),
+    )
     return (
         block_out,
         grad_tokens,
-        lax.dynamic_slice_in_dim(gain_rows[0], dp_here * piece, piece),
-        small[:, wide + n],
-        weight_grads[:, :wide],
-        weight_grads[:, wide : 2 * wide],
-        weight_grads[:, 2 * wide :],
-        small[:, :wide].T,
-        small[:, wide : wide + n],
+        gain_one,
+        gain_two,
+        grad_query,
+        grad_key,
+        grad_value,
+        grad_output,
+        grad_router.T,
         grad_first[None],
         grad_second[None],
-        w_query.astype(FULL) * column_factor,
-        w_key.astype(FULL) * column_factor,
+        clipped_query.T,
+        clipped_key.T,
         head_max,
     )
 

time: 216 us -> 208 us (0.963)
  local copies, waits for them, and re-layouts: 17 us -> 1.37 us
  Pallas kernels: 195 us -> 204 us
    unnamed x24 -> x0, local copies, waits for them, and re-layouts: 9.83 us -> none
    pallas_call x0 -> x1, Pallas kernels: none -> 8.77 us  [run_results(): pl.pallas_call(results_kernel, out_shape=(*[shape(a.shape, a.dtype) for a...]
    slice x4 -> x0, local copies, waits for them, and re-layouts: 4.45 us -> none  [the longest x1 1.96 us: body(): weight_grads[:, 2 * wide:]]
where the time goes in v5:
time: 208 us; the launch traced here: 207 us
  Pallas kernels  204 us (98%)
    pallas_call x1, Pallas kernels, run_experts(): pl.pallas_call(functools.partial(expert_kernel, n, hp), out_shape=(shape(...  79 us
    pallas_call x1, Pallas kernels, run_back(): pl.pallas_call(functools.partial(back_kernel, n, hp), out_shape=(shape((r...  69.2 us
    pallas_call x1, Pallas kernels, run_front(): pl.pallas_call(functools.partial(front_kernel, n, hp, per_half), out_shap...  47 us
    pallas_call x1, Pallas kernels, run_results(): pl.pallas_call(results_kernel, out_shape=(*[shape(a.shape, a.dtype) for a...  8.77 us

profile of v5, /device:TPU:0, one launch (start us, length us, event | category | flops | bytes accessed | tf_op | source)
XLA Modules:
  0.0 206.8 jit_solution(11608949396180275854)
XLA Ops:
  0.6 0.7 stack.9
  1.3 0.7 stack.10
  2.0 0.6 maximum_convert_fusion.gains_ref
  2.6 47.0 %front.1 = (s32[8,1248]{1,0:T(8,128)}, s32[1248,8]{1,0:T(8,128)}, f32[8,128]{1,0:T(8,128)}, bf16[1248,768]{1,0:T(8,128)(2,1)}, bf16[1248,768]{1,0:T(8,128)(2,1)}...) custom-call(s32[8]{0:T(128)} %capacity_ref.1, ...), custom_call_target="tpu_custom_call" | custom-call | tf_op jit(solution)/shard_map/front/pallas_call | solution.py:542
  49.6 79.0 %experts.1 = (bf16[8,352,384]{2,1,0:T(8,128)(2,1)}, f32[8,2816]{1,0:T(8,128)}, f32[8,128]{1,0:T(8,128)}, bf16[4,176,384]{2,1,0:T(8,128)(2,1)}, f32[4,176,384]{2,...) custom-call(s32[8,1248]{1,0:T(8,128)} %get-tuple-element.54.place_ref, ...), custom_call_target="tpu_custom_call" | custom-call | tf_op jit(solution)/shard_map/experts/pallas_call | solution.py:973
  128.6 69.2 %back.1 = (bf16[1182,768]{1,0:T(8,128)(2,1)}, bf16[1182,768]{1,0:T(8,128)(2,1)}, f32[96,576]{1,0:T(8,128)}, f32[96,201]{1,0:T(8,128)}, f32[1,768]{1,0:T(1,128)}) custom-call(bf16[2816,384]{1,0:T(8,128)(2,1)} %bitcast.20, f32[8,2816]{1,0:T(8,128)} %get-tuple-element.59.gate_sum_ref, s32[1248,8]{1,0:T(8,128)} %get-tuple-element.60.index_ref, ...), custom_call_target="tpu_custom_call" | custom-call | tf_op jit(solution)/shard_map/back/pallas_call | solution.py:1524
  197.8 8.8 %results.1 = (bf16[1182,768]{1,0:T(8,128)(2,1)}, bf16[1182,768]{1,0:T(8,128)(2,1)}, f32[768,768]{1,0:T(8,128)}, f32[768,768]{1,0:T(8,128)}, f32[96]{0:T(128)}, /...) custom-call(f32[3]{0:T(128)} %threshold_ref.1, ...), custom_call_target="tpu_custom_call" | custom-call | tf_op jit(solution)/shard_map/results/pallas_call | solution.py:1640

commit v6 on v5

--- a/solution.py
+++ b/solution.py
@@ -11,6 +11,7 @@
 HD = 64
 SEQ = 197
 PIECE = 208
+SENT = slice(0, 200)
 TOK_DEV = 1182
 EPSILON = 1e-06
 MESH = pl.DeviceIdType.MESH
@@ -248,11 +249,17 @@
         return [dma(n), dma(n), dma(n), dma(n), dma(n), dma(n), pltpu.SemaphoreType.DMA]
 
 
+def clear_unsent(rows_in):
+    count, rows, width = rows_in.shape
+    rows_in[:, SENT.stop :, :] = jnp.zeros((count, rows - SENT.stop, width), rows_in.dtype)
+
+
 class Total:
     def __init__(self, part_out, pair_in, far_out, far_in, ps, pr, fs, fr):
         self.part_out, self.pair_in, self.far_out, self.far_in = part_out, pair_in, far_out, far_in
         self.ps, self.pr, self.fs, self.fr = ps, pr, fs, fr
         self.dp, _, _, _, self.mate, self.far = places()
+        clear_unsent(far_in)
 
     def pair_copy(self, j):
         return remote(
@@ -261,7 +268,11 @@
 
     def far_copy(self, j):
         return remote(
-            self.far_out.at[j], self.far_in.at[j], self.fs.at[j], self.fr.at[j], (self.dp, self.far)
+            self.far_out.at[j, SENT],
+            self.far_in.at[j, SENT],
+            self.fs.at[j],
+            self.fr.at[j],
+            (self.dp, self.far),
         )
 
     def give(self, j, rows):
@@ -742,7 +753,7 @@
     await_greetings(n, (1, 2, 3))
 
     def dispatch(i):
-        k = (i + near) % n
+        k = in_turn((i + 1) % n, near)
         is_first, is_second = spread.send(k, normed_ref)
         gate = jnp.sum(
             jnp.where(is_first, gate_one, 0.0) + jnp.where(is_second, gate_two, 0.0),
@@ -1148,10 +1159,10 @@
         return (partner(dp, k, n), t)
 
     def moe_copy(j):
-        return remote(moe_mine.at[j], moe_other.at[j], as_.at[j], ar.at[j], (dp, far))
+        return remote(moe_mine.at[j, SENT], moe_other.at[j, SENT], as_.at[j], ar.at[j], (dp, far))
 
     def block_copy(j):
-        return remote(block_mine.at[j], block_other.at[j], bs.at[j], br.at[j], (dp, far))
+        return remote(block_mine.at[j, SENT], block_other.at[j, SENT], bs.at[j], br.at[j], (dp, far))
 
     def attention_copy(j, owner):
         rows = attention_grad.at[image_rows(2 * j + owner)]
@@ -1219,6 +1230,8 @@
     def as_low(mask):
         return jnp.where(mask, 1.0, 0.0).astype(LOW)
 
+    clear_unsent(moe_other)
+    clear_unsent(block_other)
     gain_two_sum[...] = jnp.zeros_like(gain_two_sum)
     gain_one_sum[...] = jnp.zeros_like(gain_one_sum)
     router_sum[...] = jnp.zeros_like(router_sum)
@@ -1346,7 +1359,7 @@
         )
 
         def send_small(i):
-            k = (i + near) % n
+            k = in_turn((i + 1) % n, near)
             small_pieces[k] = my_piece(totals_two, k)
 
             @pl.when(k > 0)
@@ -1389,7 +1402,7 @@
     )
 
     def send_piece(i):
-        k = (i + near) % n
+        k = in_turn((i + 1) % n, near)
         pieces[k] = my_piece(totals, k)
 
         @pl.when(k > 0)
@@ -1568,15 +1581,9 @@
 
 def results_kernel(
     threshold_ref,
-    weights_ref,
-    small_ref,
-    gain_row_ref,
-    top_ref,
-    query_w_ref,
-    key_w_ref,
     *refs,
 ):
-    moved_in, moved_out = refs[:4], refs[4:8]
+    small_in, moved_in, moved_out, refs = refs[:6], refs[6:10], refs[10:14], refs[14:]
     (
         gain_one_ref,
         gain_two_ref,
@@ -1590,7 +1597,9 @@
         head_max_ref,
         *held,
         sems,
-    ) = refs[8:]
+    ) = refs
+    held, own = held[:4], held[4:]
+    weights_ref, small_ref, gain_row_ref, top_ref, query_w_ref, key_w_ref = own
     fetches, copies = [], []
     for i, (source, target) in enumerate(zip(moved_in, moved_out)):
         rows = source.shape[0]
@@ -1600,11 +1609,16 @@
             fetches.append(pltpu.make_async_copy(source.at[at], held[i].at[at], sem))
             sem = sems.at[8 + 2 * i + part]
             copies.append(pltpu.make_async_copy(held[i].at[at], target.at[at], sem))
-    for fetch in fetches:
+    small_fetches = [
+        pltpu.make_async_copy(a, b, sems.at[16 + i]) for i, (a, b) in enumerate(zip(small_in, own))
+    ]
+    for fetch in fetches + small_fetches:
         fetch.start()
     for fetch, copy in zip(fetches, copies):
         fetch.wait()
         copy.start()
+    for fetch in small_fetches:
+        fetch.wait()
     piece, wide = query_ref.shape
     heads = head_max_ref.shape[0]
     query_ref[...] = weights_ref[:, :wide]
@@ -1652,9 +1666,15 @@
             clipped,
             shape(threshold.shape, FULL),
         ),
-        in_specs=[pl.BlockSpec(memory_space=pltpu.SMEM)] + [vmem] * 6 + [hbm] * 4,
+        in_specs=[pl.BlockSpec(memory_space=pltpu.SMEM)] + [hbm] * 10,
         out_specs=[hbm] * 4 + [vmem] * 10,
-        scratch_shapes=[*[VMEM(a.shape, a.dtype) for a in moved], dma(16)],
+        scratch_shapes=[
+            *[
+                VMEM(a.shape, a.dtype)
+                for a in (*moved, weights, small, gain_row, top, query_w, key_w)
+            ],
+            dma(22),
+        ],
         compiler_params=pltpu.CompilerParams(vmem_limit_bytes=VMEM_LIMIT),
         name="results",
     )(threshold, weights, small, gain_row, top, query_w, key_w, *moved)

time: 208 us -> 199 us (0.957)
  Pallas kernels: 204 us -> 196 us
    pallas_call x1, Pallas kernels: 79 us -> 73 us  [run_experts(): pl.pallas_call(functools.partial(expert_kernel, n, hp), out_shape=(shape(...]
where the time goes in v6:
time: 199 us
  Pallas kernels  196 us (98%)
    pallas_call x1, Pallas kernels, run_experts(): pl.pallas_call(functools.partial(expert_kernel, n, hp), out_shape=(shape(...  73 us
    pallas_call x1, Pallas kernels, run_back(): pl.pallas_call(functools.partial(back_kernel, n, hp), out_shape=(shape((r...  68.4 us
    pallas_call x1, Pallas kernels, run_front(): pl.pallas_call(functools.partial(front_kernel, n, hp, per_half), out_shap...  46.5 us
    pallas_call x1, Pallas kernels, run_results(): pl.pallas_call(results_kernel, out_shape=(*[shape(a.shape, a.dtype) for a...  8.38 us

profile of v6, /device:TPU:0, one launch (start us, length us, event | category | flops | bytes accessed | tf_op | source)
XLA Modules:
  0.0 199.1 jit_solution(4136986111152388587)
XLA Ops:
  0.6 0.7 stack.9
  1.3 0.7 stack.10
  2.0 0.6 maximum_convert_fusion.gains_ref
  2.6 46.5 %front.1 = (s32[8,1248]{1,0:T(8,128)}, s32[1248,8]{1,0:T(8,128)}, f32[8,128]{1,0:T(8,128)}, bf16[1248,768]{1,0:T(8,128)(2,1)}, bf16[1248,768]{1,0:T(8,128)(2,1)}...) custom-call(s32[8]{0:T(128)} %capacity_ref.1, ...), custom_call_target="tpu_custom_call" | custom-call | tf_op jit(solution)/shard_map/front/pallas_call | solution.py:553
  49.1 73.0 %experts.1 = (bf16[8,352,384]{2,1,0:T(8,128)(2,1)}, f32[8,2816]{1,0:T(8,128)}, f32[8,128]{1,0:T(8,128)}, bf16[4,176,384]{2,1,0:T(8,128)(2,1)}, f32[4,176,384]{2,...) custom-call(s32[8,1248]{1,0:T(8,128)} %get-tuple-element.54.place_ref, ...), custom_call_target="tpu_custom_call" | custom-call | tf_op jit(solution)/shard_map/experts/pallas_call | solution.py:984
  122.1 68.4 %back.1 = (bf16[1182,768]{1,0:T(8,128)(2,1)}, bf16[1182,768]{1,0:T(8,128)(2,1)}, f32[96,576]{1,0:T(8,128)}, f32[96,201]{1,0:T(8,128)}, f32[1,768]{1,0:T(1,128)}) custom-call(bf16[2816,384]{1,0:T(8,128)(2,1)} %bitcast.20, f32[8,2816]{1,0:T(8,128)} %get-tuple-element.59.gate_sum_ref, s32[1248,8]{1,0:T(8,128)} %get-tuple-element.60.index_ref, ...), custom_call_target="tpu_custom_call" | custom-call | tf_op jit(solution)/shard_map/back/pallas_call | solution.py:1537
  190.5 8.4 %results.1 = (bf16[1182,768]{1,0:T(8,128)(2,1)}, bf16[1182,768]{1,0:T(8,128)(2,1)}, f32[768,768]{1,0:T(8,128)}, f32[768,768]{1,0:T(8,128)}, f32[96]{0:T(128)}, /...) custom-call(f32[3]{0:T(128)} %threshold_ref.1, ...), custom_call_target="tpu_custom_call" | custom-call | tf_op jit(solution)/shard_map/results/pallas_call | solution.py:1654

commit v7 on v6

--- a/solution.py
+++ b/solution.py
@@ -1378,7 +1378,7 @@
         total.take(j, grad_part(2 * j + half))
         answer_turn((j + 1) % near)
 
-        @pl.when(j == 1)
+        @pl.when(j == 0)
         def _():
             small_grads()
 
@@ -1702,7 +1702,7 @@
     slot_count = 23 * TOK_DEV // (10 * n) + 1
     per_half = -(-slot_count // 2)
     hp = -(-per_half // 16) * 16
-    gains = jnp.stack([gain_attn, gain_moe]).astype(FULL)
+    gains = jnp.concatenate([gain_attn, gain_moe]).astype(FULL).reshape(2, -1)
     across = (w_query.T, w_key.T, w_value.T)
     (
         place,

time: 199 us -> 198 us (level)
  no operation moved by 1% of the time
where the time goes in v7:
time: 198 us; the launch traced here: 197 us
  Pallas kernels  195 us (98%)
    pallas_call x1, Pallas kernels, run_experts(): pl.pallas_call(functools.partial(expert_kernel, n, hp), out_shape=(shape(...  73 us
    pallas_call x1, Pallas kernels, run_back(): pl.pallas_call(functools.partial(back_kernel, n, hp), out_shape=(shape((r...  67.3 us
    pallas_call x1, Pallas kernels, run_front(): pl.pallas_call(functools.partial(front_kernel, n, hp, per_half), out_shap...  46.5 us
    pallas_call x1, Pallas kernels, run_results(): pl.pallas_call(results_kernel, out_shape=(*[shape(a.shape, a.dtype) for a...  8.38 us

profile of v7, /device:TPU:0, one launch (start us, length us, event | category | flops | bytes accessed | tf_op | source)
XLA Modules:
  0.0 197.3 jit_solution(10973098451756705471)
XLA Ops:
  0.6 0.7 maximum_convert_fusion
  1.4 0.6 reshape.36.gains_ref
  2.0 46.5 %front.1 = (s32[8,1248]{1,0:T(8,128)}, s32[1248,8]{1,0:T(8,128)}, f32[8,128]{1,0:T(8,128)}, bf16[1248,768]{1,0:T(8,128)(2,1)}, bf16[1248,768]{1,0:T(8,128)(2,1)}...) custom-call(s32[8]{0:T(128)} %capacity_ref.1, ...), custom_call_target="tpu_custom_call" | custom-call | tf_op jit(solution)/shard_map/front/pallas_call | solution.py:553
  48.5 73.0 %experts.1 = (bf16[8,352,384]{2,1,0:T(8,128)(2,1)}, f32[8,2816]{1,0:T(8,128)}, f32[8,128]{1,0:T(8,128)}, bf16[4,176,384]{2,1,0:T(8,128)(2,1)}, f32[4,176,384]{2,...) custom-call(s32[8,1248]{1,0:T(8,128)} %get-tuple-element.54.place_ref, ...), custom_call_target="tpu_custom_call" | custom-call | tf_op jit(solution)/shard_map/experts/pallas_call | solution.py:984
  121.5 67.3 %back.1 = (bf16[1182,768]{1,0:T(8,128)(2,1)}, bf16[1182,768]{1,0:T(8,128)(2,1)}, f32[96,576]{1,0:T(8,128)}, f32[96,201]{1,0:T(8,128)}, f32[1,768]{1,0:T(1,128)}) custom-call(bf16[2816,384]{1,0:T(8,128)(2,1)} %bitcast.20, f32[8,2816]{1,0:T(8,128)} %get-tuple-element.59.gate_sum_ref, s32[1248,8]{1,0:T(8,128)} %get-tuple-element.60.index_ref, ...), custom_call_target="tpu_custom_call" | custom-call | tf_op jit(solution)/shard_map/back/pallas_call | solution.py:1537
  188.8 8.4 %results.1 = (bf16[1182,768]{1,0:T(8,128)(2,1)}, bf16[1182,768]{1,0:T(8,128)(2,1)}, f32[768,768]{1,0:T(8,128)}, f32[768,768]{1,0:T(8,128)}, f32[96]{0:T(128)}, /...) custom-call(f32[3]{0:T(128)} %threshold_ref.1, ...), custom_call_target="tpu_custom_call" | custom-call | tf_op jit(solution)/shard_map/results/pallas_call | solution.py:1654

commit v8 on v7

--- a/solution.py
+++ b/solution.py
@@ -1059,7 +1059,6 @@
 def back_kernel(
     n,
     hp,
-    back_ref,
     gate_sum_ref,
     index_ref,
     gains_ref,
@@ -1068,10 +1067,11 @@
     answer_ready,
     *refs,
 ):
-    later, outs, scratch = refs[:13], refs[13:18], refs[18:]
+    later, outs, scratch = refs[:14], refs[14:19], refs[19:]
     block_out_ref, tokens_out_ref, weights_ref, small_ref, gain_ref = outs
-    held, scratch = scratch[:13], scratch[13:]
+    held, scratch = scratch[:14], scratch[14:]
     (
+        back_ref,
         residual_ref,
         upstream_ref,
         answer_out,
@@ -1247,8 +1247,9 @@
 
         moe_copy(j).start()
 
+    fetches[0].wait()
     loop(combine, 0, 3)
-    for fetch in fetches[:3]:
+    for fetch in fetches[1:4]:
         fetch.wait()
     loop(lambda k: answer_side_copy((k + 1) % near).start(), 0, near)
 
@@ -1290,7 +1291,7 @@
     loop(moe_back, 0, 3)
     router_copy().start()
     gain_two_copy().start()
-    for fetch in fetches[3:]:
+    for fetch in fetches[4:]:
         fetch.wait()
 
     def image_back(image):
@@ -1521,9 +1522,9 @@
 
 
 def run_back(n, hp, row_count, first, later):
-    upstream = later[1]
+    upstream = later[2]
     rows, model = upstream.shape
-    heads_width = later[8].shape[1]
+    heads_width = later[9].shape[1]
     width = model // 2
     piece = model // n
     vmem = pl.BlockSpec(memory_space=VMEM)
@@ -1738,8 +1739,9 @@
         n,
         hp,
         row_count,
-        (back.reshape(n * 2 * hp, -1), gate_sums, index, gains, w_output, router, answer_ready),
+        (gate_sums, index, gains, w_output, router, answer_ready),
         (
+            back.reshape(n * 2 * hp, -1),
             residual,
             upstream,
             answer_out,

time: 198 us -> 197 us (level)
  no operation moved by 1% of the time
where the time goes in v8:
time: 197 us
  Pallas kernels  195 us (99%)
    pallas_call x1, Pallas kernels, run_experts(): pl.pallas_call(functools.partial(expert_kernel, n, hp), out_shape=(shape(...  73 us
    pallas_call x1, Pallas kernels, run_back(): pl.pallas_call(functools.partial(back_kernel, n, hp), out_shape=(shape((r...  66.6 us
    pallas_call x1, Pallas kernels, run_front(): pl.pallas_call(functools.partial(front_kernel, n, hp, per_half), out_shap...  46.5 us
    pallas_call x1, Pallas kernels, run_results(): pl.pallas_call(results_kernel, out_shape=(*[shape(a.shape, a.dtype) for a...  8.38 us

profile of v8, /device:TPU:0, one launch (start us, length us, event | category | flops | bytes accessed | tf_op | source)
XLA Modules:
  0.0 196.6 jit_solution(15008167405019374683)
XLA Ops:
  0.6 0.7 maximum_convert_fusion
  1.4 0.6 reshape.36.gains_ref
  2.0 46.5 %front.1 = (s32[8,1248]{1,0:T(8,128)}, s32[1248,8]{1,0:T(8,128)}, f32[8,128]{1,0:T(8,128)}, bf16[1248,768]{1,0:T(8,128)(2,1)}, bf16[1248,768]{1,0:T(8,128)(2,1)}...) custom-call(s32[8]{0:T(128)} %capacity_ref.1, ...), custom_call_target="tpu_custom_call" | custom-call | tf_op jit(solution)/shard_map/front/pallas_call | solution.py:553
  48.5 73.0 %experts.1 = (bf16[8,352,384]{2,1,0:T(8,128)(2,1)}, f32[8,2816]{1,0:T(8,128)}, f32[8,128]{1,0:T(8,128)}, bf16[4,176,384]{2,1,0:T(8,128)(2,1)}, f32[4,176,384]{2,...) custom-call(s32[8,1248]{1,0:T(8,128)} %get-tuple-element.54.place_ref, ...), custom_call_target="tpu_custom_call" | custom-call | tf_op jit(solution)/shard_map/experts/pallas_call | solution.py:984
  121.5 66.6 %back.1 = (bf16[1182,768]{1,0:T(8,128)(2,1)}, bf16[1182,768]{1,0:T(8,128)(2,1)}, f32[96,576]{1,0:T(8,128)}, f32[96,201]{1,0:T(8,128)}, f32[1,768]{1,0:T(1,128)}) custom-call(f32[8,2816]{1,0:T(8,128)} %get-tuple-element.58.gate_sum_ref, s32[1248,8]{1,0:T(8,128)} %get-tuple-element.59.index_ref, f32[2,768]{1,0:T(2,128)} %reshape.36.gains_ref, ...), custom_call_target="tpu_custom_call" | custom-call | tf_op jit(solution)/shard_map/back/pallas_call | solution.py:1538
  188.1 8.4 %results.1 = (bf16[1182,768]{1,0:T(8,128)(2,1)}, bf16[1182,768]{1,0:T(8,128)(2,1)}, f32[768,768]{1,0:T(8,128)}, f32[768,768]{1,0:T(8,128)}, f32[96]{0:T(128)}, /...) custom-call(f32[3]{0:T(128)} %threshold_ref.1, ...), custom_call_target="tpu_custom_call" | custom-call | tf_op jit(solution)/shard_map/results/pallas_call | solution.py:1655
